TPU v7x, 256 devices: a whole 4x4x8 slice. The times are simulated.
256 devices in a mesh: sector: 16 (over z, x_lo), row: 16 (over x_hi, y, core).
Axes of the slice: x: 4 (x_hi: 2, x_lo: 2; x = x_hi * 2 + x_lo), y: 4, z: 8, core: 2. Of those that a mesh axis runs over, the one named last changes fastest.
Arguments:
- cosine_load: float32 [16384, 128], P('row'), may hold values from -6 to 6
- sine_load: float32 [16384, 128], P('row'), may hold values from -6 to 6
- base_stiffness: float32 [16384], P('row'), may hold values from 1 to 3
- coupling_ratio: float32 [16384], P('row'), may hold values from 0.35 to 0.42
- mistuning: float32 [4, 16384], P(None, 'row'), may hold values from -0.1 to 0.1
- sector_class: int32 [16], P('sector'), may hold values from 0 to 3
- engine_order: int32 [1], replicated, may hold values from 1 to 7
- block_values: bfloat16 [16, 64, 16, 256, 256], P('sector', 'row'), may hold values from -0.03125 to 0.03125
- block_columns: int32 [64, 16], P('row'), may hold values from 0 to 63, all different within a row
Outputs:
- solution: float32 [16, 16384, 128], P('sector', 'row')
Inputs may be any that keep to these rules, and one draw needn't show every extreme that they name: `block_columns`: each block row lists 16 distinct block columns; every block column is listed by some block row.
All inputs are finite; a program needn't handle non-finite values.
Results may differ from a plain program's by a relative error of at most 0.0015.
Values may be sent and summed in bfloat16 or wider, within the bound.
No kernel may reach another device: no remote copies, remote signals or barrier semaphores. Data moves between devices by JAX's collectives and lax.ppermute only.
A program may use at most 64 MiB of HBM per device.

v0:
```python
import math

import jax
import jax.numpy as jnp
from jax import lax
from jax.experimental import pallas as pl
from jax.experimental.pallas import tpu as pltpu
from jax.sharding import PartitionSpec as P

ITERS = 4
LEVELS = 3
ROW_PARTS = (2, 4, 2)


def row_peers(shift_x, shift_y, shift_core):
    pairs = []
    for x in range(ROW_PARTS[0]):
        for y in range(ROW_PARTS[1]):
            for core in range(ROW_PARTS[2]):
                source = (
                    ((x + shift_x) % ROW_PARTS[0] * ROW_PARTS[1] + (y + shift_y) % ROW_PARTS[1])
                    * ROW_PARTS[2]
                    + (core + shift_core) % ROW_PARTS[2]
                )
                target = (x * ROW_PARTS[1] + y) * ROW_PARTS[2] + core
                pairs.append((source, target))
    return pairs


SHIFTS = ((0, 0), (1, 0), (0, 2), (0, 1), (0, 3), (1, 1), (1, 3), (1, 2))


def gather_pieces(own):
    def fetch(block, *shift):
        return lax.ppermute(block, "row", row_peers(*shift))

    across = fetch(own, 1, 0, 0)
    opposite, above, below = fetch(own, 0, 2, 0), fetch(own, 0, 1, 0), fetch(own, 0, 3, 0)
    relayed = [fetch(across, 0, 1, 0), fetch(across, 0, 3, 0), fetch(opposite, 1, 0, 0)]
    same_core = [own, across, *lax.optimization_barrier([opposite, above, below, *relayed])]
    same_core = jnp.concatenate(same_core, axis=0)
    return [same_core, fetch(same_core, 0, 0, 1)]


def relative_columns(block_columns, blocks_per_device):
    row_id = lax.axis_index("row")
    owner = block_columns // blocks_per_device
    xs, ys, cores = ROW_PARTS
    core = (owner - row_id) % cores
    shift_y = (owner // cores - row_id // cores) % ys
    shift_x = (owner // (cores * ys) - row_id // (cores * ys)) % xs
    piece = sum(
        jnp.where((shift_x == x) & (shift_y == y), index, 0) for index, (x, y) in enumerate(SHIFTS)
    )
    return (core * len(SHIFTS) + piece) * blocks_per_device + block_columns % blocks_per_device


def product_kernel(columns, values, *refs):
    *pieces, out, tiles, held, arrived, collected = refs
    rows, count, order, _ = values.shape

    def fetch(row):
        return pltpu.make_async_copy(values.at[row], held.at[row], arrived.at[row])

    places, place = [], 0
    for index, piece in enumerate(pieces):
        span = piece.shape[0]
        places.append(
            pltpu.make_async_copy(piece, tiles.at[pl.ds(place, span)], collected.at[index])
        )
        place += span
    fetch(0).start()
    for copy in places:
        copy.start()
    for row in range(1, rows):
        fetch(row).start()
    for copy in places:
        copy.wait()

    def one_row(row, carry):
        fetch(row).wait()
        total = None
        for k in range(count):
            term = jnp.dot(
                held[row, k],
                tiles[columns[row * count + k]],
                preferred_element_type=jnp.float32,
            )
            total = term if total is None else total + term
        out[pl.ds(pl.multiple_of(row * order, order), order), :] = total
        return carry

    lax.fori_loop(0, rows, one_row, 0)


def block_product(block_values, columns, pieces):
    rows, count, order, _ = block_values.shape
    load_cases = pieces[0].shape[1]
    pieces = [piece.reshape(-1, order, load_cases) for piece in pieces]
    tiles = sum(piece.shape[0] for piece in pieces)
    return pl.pallas_call(
        product_kernel,
        out_shape=jax.ShapeDtypeStruct((rows * order, load_cases), jnp.float32),
        in_specs=[pl.BlockSpec(memory_space=pltpu.SMEM)]
        + [pl.BlockSpec(memory_space=pl.ANY)] * (1 + len(pieces)),
        out_specs=pl.BlockSpec(memory_space=pltpu.VMEM),
        scratch_shapes=[
            pltpu.VMEM((tiles, order, load_cases), jnp.bfloat16),
            pltpu.VMEM((rows, count, order, order), jnp.bfloat16),
            pltpu.SemaphoreType.DMA((rows,)),
            pltpu.SemaphoreType.DMA((len(pieces),)),
        ],
        compiler_params=pltpu.CompilerParams(vmem_limit_bytes=48 * 1024 * 1024),
        cost_estimate=pl.CostEstimate(
            flops=2 * rows * count * order * order * load_cases,
            bytes_accessed=2 * rows * count * order * order,
            transcendentals=0,
        ),
    )(columns, block_values, *pieces)


def reduce_coefficients(sub_diag, main_diag, super_diag):
    factors = []
    for exponent in range(LEVELS):
        stride = 2**exponent
        lower_factor = -sub_diag / jnp.roll(main_diag, stride, 0)
        upper_factor = -super_diag / jnp.roll(main_diag, -stride, 0)
        factors.append((lower_factor, upper_factor))
        sub_diag, main_diag, super_diag = (
            lower_factor * jnp.roll(sub_diag, stride, 0),
            main_diag
            + lower_factor * jnp.roll(super_diag, stride, 0)
            + upper_factor * jnp.roll(sub_diag, -stride, 0),
            upper_factor * jnp.roll(super_diag, -stride, 0),
        )
    return factors, main_diag


def apply_reduction(factors, reduced, right_side):
    for exponent in range(LEVELS):
        stride = 2**exponent
        lower_factor, upper_factor = factors[exponent]
        right_side = (
            right_side
            + lower_factor * jnp.roll(right_side, stride, 0)
            + upper_factor * jnp.roll(right_side, -stride, 0)
        )
    return right_side / reduced


def shards(
    cosine_load,
    sine_load,
    base_stiffness,
    coupling_ratio,
    mistuning,
    sector_class,
    engine_order,
    block_values,
    block_columns,
):
    sectors = lax.axis_size("sector")
    sector_id = lax.axis_index("sector")
    local_rows, load_cases = cosine_load.shape
    slice_rows = local_rows // sectors
    order = block_values.shape[-1]

    def swap(cells):
        return lax.all_to_all(cells, "sector", 0, 0, tiled=True)

    def own_slice(cells, axis):
        return lax.dynamic_slice_in_dim(cells, sector_id * slice_rows, slice_rows, axis)

    all_classes = swap(jnp.broadcast_to(sector_class[:, None], (sectors, 1)))
    turns = (engine_order[0] * jnp.arange(sectors, dtype=jnp.int32)) % sectors
    angle = turns.astype(jnp.float32) * (2.0 * math.pi / sectors)
    cosine, sine = jnp.cos(angle)[:, None], jnp.sin(angle)[:, None]

    classes = mistuning.shape[0]
    picked = sum(
        jnp.where(all_classes == index, mistuning[index][None], 0.0) for index in range(classes)
    )
    diagonal = base_stiffness[None] * (1.0 + picked)
    coupling = coupling_ratio * base_stiffness
    cycle = jnp.broadcast_to(-coupling[None], diagonal.shape)
    factors, reduced = reduce_coefficients(cycle, diagonal, cycle)
    cosine_gain = apply_reduction(factors, reduced, jnp.broadcast_to(cosine, diagonal.shape))
    sine_gain = apply_reduction(factors, reduced, jnp.broadcast_to(sine, diagonal.shape))

    own_cosine = lax.dynamic_index_in_dim(cosine_gain, sector_id, 0, keepdims=False)
    own_sine = lax.dynamic_index_in_dim(sine_gain, sector_id, 0, keepdims=False)
    rounded = (own_cosine[:, None] * cosine_load + own_sine[:, None] * sine_load).astype(
        jnp.bfloat16
    )

    cosine_slice, sine_slice = own_slice(cosine_load, 0)[None], own_slice(sine_load, 0)[None]

    def spread(cells):
        return own_slice(cells, 1)[:, :, None]

    slice_factors = [(spread(lower), spread(upper)) for lower, upper in factors]
    slice_reduced, slice_diagonal = spread(reduced), spread(diagonal)
    slice_coupling = own_slice(coupling, 0)[None, :, None]
    forcing = cosine[:, :, None] * cosine_slice + sine[:, :, None] * sine_slice
    current = spread(cosine_gain) * cosine_slice + spread(sine_gain) * sine_slice

    columns = relative_columns(block_columns, block_values.shape[1]).reshape(-1)
    for iteration in range(1, ITERS):
        last = iteration == ITERS - 1
        product = block_product(block_values[0], columns, gather_pieces(rounded))
        if last:
            change = (product - earlier_product).astype(jnp.bfloat16)
            change = swap(change.reshape(sectors, slice_rows, load_cases))
            slice_product = slice_product + change.astype(jnp.float32)
        else:
            earlier_product = product
            slice_product = swap(product.reshape(sectors, slice_rows, load_cases))
        neighbours = jnp.roll(current, 1, 0) + jnp.roll(current, -1, 0)
        residual = forcing - (
            slice_diagonal * current - slice_coupling * neighbours + slice_product
        )
        sent = current.astype(jnp.bfloat16).astype(jnp.float32)
        current = current + apply_reduction(slice_factors, slice_reduced, residual)
        if not last:
            rounded = swap(current.astype(jnp.bfloat16)).reshape(local_rows, load_cases)
    difference = swap((current - sent).astype(jnp.bfloat16)).reshape(local_rows, load_cases)
    return (rounded.astype(jnp.float32) + difference.astype(jnp.float32))[None]


def solution(mesh):
    return jax.shard_map(
        shards,
        mesh=mesh,
        in_specs=(
            P("row", None),
            P("row", None),
            P("row"),
            P("row"),
            P(None, "row"),
            P("sector"),
            P(),
            P("sector", "row", None, None, None),
            P("row", None),
        ),
        out_specs=P("sector", "row", None),
        check_vma=False,
    )
```

profile of v0, /device:TPU:2, one launch (start us, length us, event | category | flops | bytes accessed | tf_op | source)
XLA Modules:
  0.0 236.9 jit_solution(6133951949303451152)
XLA Ops:
  1.3 9.9 %all-to-all-start = ((s32[16,1,1]{2,1,0:T(1,128)}), s32[16,1,1]{2,1,0:T(1,128)S(1)}, u32[]{:S(2)}, u32[]{:S(2)}) async-start(s32[16,1,1]{2,1,0:T(1,128)} %broadcast_in_dim.129), calls=%async_computation | async-start | bytes 16384 | tf_op jit(solution)/shard_map/all_to_all | solution.py:169
  25.3 3.2 %collective-permute-start.1 = (bf16[1024,128]{1,0:T(8,128)(2,1)S(1)}, bf16[1024,128]{1,0:T(8,128)(2,1)S(1)}, u32[]{:S(2)}, u32[]{:S(2)}) collective-permute-start(bf16[1024,128]{1,0:T(8,128)(2,1)S(1)} %get-tuple-element.50), channel_id=1, source_target_pairs={{4,0},{5,1},{6,2},{7,3},{0,4},{1,5},{2,6},{3,7},{12,8},{13,9},{14,... | collective-permute-start | bytes 786440 | tf_op jit(solution)/shard_map/ppermute | solution.py:35
  31.7 3.0 %collective-permute-start.4 = (bf16[1024,128]{1,0:T(8,128)(2,1)S(1)}, bf16[1024,128]{1,0:T(8,128)(2,1)S(1)}, u32[]{:S(2)}, u32[]{:S(2)}) collective-permute-start(bf16[1024,128]{1,0:T(8,128)(2,1)S(1)} %collective-permute-done), channel_id=1, source_target_pairs={{2,0},{3,1},{4,2},{5,3},{6,4},{7,5},{0,6},{1,7},{10,8},{11,9},{12,... | collective-permute-start | bytes 786440 | tf_op jit(solution)/shard_map/ppermute | solution.py:35
  37.4 4.5 %collective-permute-done.2 = bf16[1024,128]{1,0:T(8,128)(2,1)S(1)} collective-permute-done((bf16[1024,128]{1,0:T(8,128)(2,1)S(1)}, bf16[1024,128]{1,0:T(8,128)(2,1)S(1)}, u32[]{:S(2)}, u32[]{:S(2)}) %collective-permute-start.2) | collective-permute-done | bytes 262176 | tf_op jit(solution)/shard_map/ppermute | solution.py:35
  42.0 3.2 %collective-permute-done.4 = bf16[1024,128]{1,0:T(8,128)(2,1)S(1)} collective-permute-done((bf16[1024,128]{1,0:T(8,128)(2,1)S(1)}, bf16[1024,128]{1,0:T(8,128)(2,1)S(1)}, u32[]{:S(2)}, u32[]{:S(2)}) %collective-permute-start.4) | collective-permute-done | bytes 262176 | tf_op jit(solution)/shard_map/ppermute | solution.py:35
  51.5 7.7 %shard_map.91 = f32[1024,128]{1,0:T(8,128)} custom-call(s32[64]{0:T(128)S(1)} %reshape.218.columns, bf16[4,16,256,256]{3,2,1,0:T(8,128)(2,1)} %bitcast.44, bf16[32,256,128]{2,1,0:T(8,128)(2,1)S(1)} %bitcast.41, bf16[32,256,128]{2,1,0:T(8,128)(2,1)} %bitcast.19.refs_1_), custom_call_target="tpu_custom_call" | custom-call | flops 1073741824 | bytes 8388608 | tf_op jit(solution)/shard_map/pallas_call | solution.py:101
  59.3 8.1 %all-to-all-start.1 = ((f32[16,64,128]{2,1,0:T(8,128)}), f32[16,64,128]{2,1,0:T(8,128)S(1)}, u32[]{:S(2)}, u32[]{:S(2)}) async-start(f32[16,64,128]{2,1,0:T(8,128)} %bitcast.20), calls=%async_computation.1 | async-start | bytes 1048576 | tf_op jit(solution)/shard_map/all_to_all | solution.py:169
  68.1 16.3 %all-to-all-done.1 = f32[16,64,128]{2,1,0:T(8,128)S(1)} async-done(((f32[16,64,128]{2,1,0:T(8,128)}), f32[16,64,128]{2,1,0:T(8,128)S(1)}, u32[]{:S(2)}, u32[]{:S(2)}) %all-to-all-start.1) | async-done | bytes 524320 | tf_op jit(solution)/shard_map/all_to_all | solution.py:169
  87.2 14.4 %all_to_all.36 = bf16[16,64,128]{2,1,0:T(8,128)(2,1)S(1)} all-to-all(bf16[16,64,128]{2,1,0:T(8,128)(2,1)S(1)} %get-tuple-element.47), channel_id=1, replica_groups=mesh['sector'=16,'row'=16] {'sector'}, dimensions={0} | all-to-all | bytes 524288 | tf_op jit(solution)/shard_map/all_to_all | solution.py:169
  103.0 2.8 %collective-permute-start.9 = (bf16[1024,128]{1,0:T(8,128)(2,1)S(1)}, bf16[1024,128]{1,0:T(8,128)(2,1)S(1)}, u32[]{:S(2)}, u32[]{:S(2)}) collective-permute-start(bf16[1024,128]{1,0:T(8,128)(2,1)S(1)} %bitcast.53), channel_id=1, source_target_pairs={{4,0},{5,1},{6,2},{7,3},{0,4},{1,5},{2,6},{3,7},{12,8},{13,9},{14,... | collective-permute-start | bytes 786440 | tf_op jit(solution)/shard_map/ppermute | solution.py:35
  118.5 2.8 %collective-permute-done.12 = bf16[1024,128]{1,0:T(8,128)(2,1)S(1)} collective-permute-done((bf16[1024,128]{1,0:T(8,128)(2,1)S(1)}, bf16[1024,128]{1,0:T(8,128)(2,1)S(1)}, u32[]{:S(2)}, u32[]{:S(2)}) %collective-permute-start.12) | collective-permute-done | bytes 262176 | tf_op jit(solution)/shard_map/ppermute | solution.py:35
  122.1 4.1 %collective-permute-done.15 = bf16[8192,128]{1,0:T(8,128)(2,1)S(1)} collective-permute-done((bf16[8192,128]{1,0:T(8,128)(2,1)S(1)}, bf16[8192,128]{1,0:T(8,128)(2,1)S(1)}, u32[]{:S(2)}, u32[]{:S(2)}) %collective-permute-start.15) | collective-permute-done | bytes 2097184 | tf_op jit(solution)/shard_map/ppermute | solution.py:35
  126.2 5.8 %shard_map.92 = f32[1024,128]{1,0:T(8,128)} custom-call(s32[64]{0:T(128)S(1)} %reshape.218.columns, bf16[4,16,256,256]{3,2,1,0:T(8,128)(2,1)} %bitcast.45, bf16[32,256,128]{2,1,0:T(8,128)(2,1)S(1)} %bitcast.39, bf16[32,256,128]{2,1,0:T(8,128)(2,1)S(1)} %bitcast.43), custom_call_target="tpu_custom_call" | custom-call | flops 1073741824 | bytes 8388608 | tf_op jit(solution)/shard_map/pallas_call | solution.py:101
  132.0 5.6 %all-to-all-start.3 = ((f32[16,64,128]{2,1,0:T(8,128)}), f32[16,64,128]{2,1,0:T(8,128)S(1)}, u32[]{:S(2)}, u32[]{:S(2)}) async-start(f32[16,64,128]{2,1,0:T(8,128)} %bitcast.24), calls=%async_computation.3 | async-start | bytes 1048576 | tf_op jit(solution)/shard_map/all_to_all | solution.py:169
  137.7 17.1 %all-to-all-done.3 = f32[16,64,128]{2,1,0:T(8,128)S(1)} async-done(((f32[16,64,128]{2,1,0:T(8,128)}), f32[16,64,128]{2,1,0:T(8,128)S(1)}, u32[]{:S(2)}, u32[]{:S(2)}) %all-to-all-start.3) | async-done | bytes 524320 | tf_op jit(solution)/shard_map/all_to_all | solution.py:169
  156.9 14.3 %all_to_all.37 = bf16[16,64,128]{2,1,0:T(8,128)(2,1)S(1)} all-to-all(bf16[16,64,128]{2,1,0:T(8,128)(2,1)S(1)} %get-tuple-element.45), channel_id=1, replica_groups=mesh['sector'=16,'row'=16] {'sector'}, dimensions={0} | all-to-all | bytes 524288 | tf_op jit(solution)/shard_map/all_to_all | solution.py:169
  172.3 2.8 %collective-permute-start.17 = (bf16[1024,128]{1,0:T(8,128)(2,1)S(1)}, bf16[1024,128]{1,0:T(8,128)(2,1)S(1)}, u32[]{:S(2)}, u32[]{:S(2)}) collective-permute-start(bf16[1024,128]{1,0:T(8,128)(2,1)S(1)} %bitcast.48), channel_id=1, source_target_pairs={{4,0},{5,1},{6,2},{7,3},{0,4},{1,5},{2,6},{3,7},{12,8},{13,9},{14,... | collective-permute-start | bytes 786440 | tf_op jit(solution)/shard_map/ppermute | solution.py:35
  185.6 2.7 %collective-permute-done.18 = bf16[1024,128]{1,0:T(8,128)(2,1)S(1)} collective-permute-done((bf16[1024,128]{1,0:T(8,128)(2,1)S(1)}, bf16[1024,128]{1,0:T(8,128)(2,1)S(1)}, u32[]{:S(2)}, u32[]{:S(2)}) %collective-permute-start.18) | collective-permute-done | bytes 262176 | tf_op jit(solution)/shard_map/ppermute | solution.py:35
  188.3 2.8 %collective-permute-done.20 = bf16[1024,128]{1,0:T(8,128)(2,1)S(1)} collective-permute-done((bf16[1024,128]{1,0:T(8,128)(2,1)S(1)}, bf16[1024,128]{1,0:T(8,128)(2,1)S(1)}, u32[]{:S(2)}, u32[]{:S(2)}) %collective-permute-start.20) | collective-permute-done | bytes 262176 | tf_op jit(solution)/shard_map/ppermute | solution.py:35
  191.8 4.1 %collective-permute-done.23 = bf16[8192,128]{1,0:T(8,128)(2,1)S(1)} collective-permute-done((bf16[8192,128]{1,0:T(8,128)(2,1)S(1)}, bf16[8192,128]{1,0:T(8,128)(2,1)S(1)}, u32[]{:S(2)}, u32[]{:S(2)}) %collective-permute-start.23) | collective-permute-done | bytes 2097184 | tf_op jit(solution)/shard_map/ppermute | solution.py:35
  195.9 5.0 %shard_map.93 = f32[1024,128]{1,0:T(8,128)S(1)} custom-call(s32[64]{0:T(128)S(1)} %reshape.218.columns, bf16[4,16,256,256]{3,2,1,0:T(8,128)(2,1)} %bitcast.46, bf16[32,256,128]{2,1,0:T(8,128)(2,1)S(1)} %bitcast.40, bf16[32,256,128]{2,1,0:T(8,128)(2,1)S(1)} %bitcast.42), custom_call_target="tpu_custom_call" | custom-call | flops 1073741824 | bytes 8388608 | tf_op jit(solution)/shard_map/pallas_call | solution.py:101
  202.7 5.5 %all-to-all-start.5 = ((bf16[16,64,128]{2,1,0:T(8,128)(2,1)}), bf16[16,64,128]{2,1,0:T(8,128)(2,1)S(1)}, u32[]{:S(2)}, u32[]{:S(2)}) async-start(bf16[16,64,128]{2,1,0:T(8,128)(2,1)} %bitcast.28), calls=%async_computation.5 | async-start | bytes 524288 | tf_op jit(solution)/shard_map/all_to_all | solution.py:169
  208.4 11.0 %all-to-all-done.5 = bf16[16,64,128]{2,1,0:T(8,128)(2,1)S(1)} async-done(((bf16[16,64,128]{2,1,0:T(8,128)(2,1)}), bf16[16,64,128]{2,1,0:T(8,128)(2,1)S(1)}, u32[]{:S(2)}, u32[]{:S(2)}) %all-to-all-start.5) | async-done | bytes 262176 | tf_op jit(solution)/shard_map/all_to_all | solution.py:169
  221.2 14.8 %all_to_all.38 = bf16[16,64,128]{2,1,0:T(8,128)(2,1)S(1)} all-to-all(bf16[16,64,128]{2,1,0:T(8,128)(2,1)S(1)} %fusion.37), channel_id=1, replica_groups=mesh['sector'=16,'row'=16] {'sector'}, dimensions={0} | all-to-all | bytes 524288 | tf_op jit(solution)/shard_map/all_to_all | solution.py:169
  (203 shorter events, 63.0 us)
Async XLA Ops:
  1.3 17.0 %all-to-all-start = ((s32[16,1,1]{2,1,0:T(1,128)}), s32[16,1,1]{2,1,0:T(1,128)S(1)}, u32[]{:S(2)}, u32[]{:S(2)}) async-start(s32[16,1,1]{2,1,0:T(1,128)} %broadcast_in_dim.129), calls=%async_computation | async-start | bytes 16384 | tf_op jit(solution)/shard_map/all_to_all | solution.py:169
  23.0 8.6 %collective-permute-start = (bf16[1024,128]{1,0:T(8,128)(2,1)S(1)}, bf16[1024,128]{1,0:T(8,128)(2,1)S(1)}, u32[]{:S(2)}, u32[]{:S(2)}) collective-permute-start(bf16[1024,128]{1,0:T(8,128)(2,1)S(1)} %get-tuple-element.50), channel_id=1, source_target_pairs={{8,0},{9,1},{10,2},{11,3},{12,4},{13,5},{14,6},{15,7},{0,8},{1,9},... | collective-permute-start | bytes 786440 | tf_op jit(solution)/shard_map/ppermute | solution.py:35
  25.3 10.7 %collective-permute-start.1 = (bf16[1024,128]{1,0:T(8,128)(2,1)S(1)}, bf16[1024,128]{1,0:T(8,128)(2,1)S(1)}, u32[]{:S(2)}, u32[]{:S(2)}) collective-permute-start(bf16[1024,128]{1,0:T(8,128)(2,1)S(1)} %get-tuple-element.50), channel_id=1, source_target_pairs={{4,0},{5,1},{6,2},{7,3},{0,4},{1,5},{2,6},{3,7},{12,8},{13,9},{14,... | collective-permute-start | bytes 786440 | tf_op jit(solution)/shard_map/ppermute | solution.py:35
  28.4 13.5 %collective-permute-start.2 = (bf16[1024,128]{1,0:T(8,128)(2,1)S(1)}, bf16[1024,128]{1,0:T(8,128)(2,1)S(1)}, u32[]{:S(2)}, u32[]{:S(2)}) collective-permute-start(bf16[1024,128]{1,0:T(8,128)(2,1)S(1)} %get-tuple-element.50), channel_id=1, source_target_pairs={{2,0},{3,1},{4,2},{5,3},{6,4},{7,5},{0,6},{1,7},{10,8},{11,9},{12,... | collective-permute-start | bytes 786440 | tf_op jit(solution)/shard_map/ppermute | solution.py:35
  29.5 12.5 %collective-permute-start.3 = (bf16[1024,128]{1,0:T(8,128)(2,1)S(1)}, bf16[1024,128]{1,0:T(8,128)(2,1)S(1)}, u32[]{:S(2)}, u32[]{:S(2)}) collective-permute-start(bf16[1024,128]{1,0:T(8,128)(2,1)S(1)} %get-tuple-element.50), channel_id=1, source_target_pairs={{6,0},{7,1},{0,2},{1,3},{2,4},{3,5},{4,6},{5,7},{14,8},{15,9},{8,1... | collective-permute-start | bytes 786440 | tf_op jit(solution)/shard_map/ppermute | solution.py:35
  31.7 13.5 %collective-permute-start.4 = (bf16[1024,128]{1,0:T(8,128)(2,1)S(1)}, bf16[1024,128]{1,0:T(8,128)(2,1)S(1)}, u32[]{:S(2)}, u32[]{:S(2)}) collective-permute-start(bf16[1024,128]{1,0:T(8,128)(2,1)S(1)} %collective-permute-done), channel_id=1, source_target_pairs={{2,0},{3,1},{4,2},{5,3},{6,4},{7,5},{0,6},{1,7},{10,8},{11,9},{12,... | collective-permute-start | bytes 786440 | tf_op jit(solution)/shard_map/ppermute | solution.py:35
  34.7 10.5 %collective-permute-start.5 = (bf16[1024,128]{1,0:T(8,128)(2,1)S(1)}, bf16[1024,128]{1,0:T(8,128)(2,1)S(1)}, u32[]{:S(2)}, u32[]{:S(2)}) collective-permute-start(bf16[1024,128]{1,0:T(8,128)(2,1)S(1)} %collective-permute-done), channel_id=1, source_target_pairs={{6,0},{7,1},{0,2},{1,3},{2,4},{3,5},{4,6},{5,7},{14,8},{15,9},{8,1... | collective-permute-start | bytes 786440 | tf_op jit(solution)/shard_map/ppermute | solution.py:35
  36.0 9.2 %collective-permute-start.6 = (bf16[1024,128]{1,0:T(8,128)(2,1)S(1)}, bf16[1024,128]{1,0:T(8,128)(2,1)S(1)}, u32[]{:S(2)}, u32[]{:S(2)}) collective-permute-start(bf16[1024,128]{1,0:T(8,128)(2,1)S(1)} %collective-permute-done.1), channel_id=1, source_target_pairs={{8,0},{9,1},{10,2},{11,3},{12,4},{13,5},{14,6},{15,7},{0,8},{1,9},... | collective-permute-start | bytes 786440 | tf_op jit(solution)/shard_map/ppermute | solution.py:35
  59.3 25.2 %all-to-all-start.1 = ((f32[16,64,128]{2,1,0:T(8,128)}), f32[16,64,128]{2,1,0:T(8,128)S(1)}, u32[]{:S(2)}, u32[]{:S(2)}) async-start(f32[16,64,128]{2,1,0:T(8,128)} %bitcast.20), calls=%async_computation.1 | async-start | bytes 1048576 | tf_op jit(solution)/shard_map/all_to_all | solution.py:169
  101.6 7.9 %collective-permute-start.8 = (bf16[1024,128]{1,0:T(8,128)(2,1)S(1)}, bf16[1024,128]{1,0:T(8,128)(2,1)S(1)}, u32[]{:S(2)}, u32[]{:S(2)}) collective-permute-start(bf16[1024,128]{1,0:T(8,128)(2,1)S(1)} %bitcast.52), channel_id=1, source_target_pairs={{8,0},{9,1},{10,2},{11,3},{12,4},{13,5},{14,6},{15,7},{0,8},{1,9},... | collective-permute-start | bytes 786440 | tf_op jit(solution)/shard_map/ppermute | solution.py:35
  103.0 10.8 %collective-permute-start.9 = (bf16[1024,128]{1,0:T(8,128)(2,1)S(1)}, bf16[1024,128]{1,0:T(8,128)(2,1)S(1)}, u32[]{:S(2)}, u32[]{:S(2)}) collective-permute-start(bf16[1024,128]{1,0:T(8,128)(2,1)S(1)} %bitcast.53), channel_id=1, source_target_pairs={{4,0},{5,1},{6,2},{7,3},{0,4},{1,5},{2,6},{3,7},{12,8},{13,9},{14,... | collective-permute-start | bytes 786440 | tf_op jit(solution)/shard_map/ppermute | solution.py:35
  105.8 12.7 %collective-permute-start.10 = (bf16[1024,128]{1,0:T(8,128)(2,1)S(1)}, bf16[1024,128]{1,0:T(8,128)(2,1)S(1)}, u32[]{:S(2)}, u32[]{:S(2)}) collective-permute-start(bf16[1024,128]{1,0:T(8,128)(2,1)S(1)} %bitcast.54), channel_id=1, source_target_pairs={{2,0},{3,1},{4,2},{5,3},{6,4},{7,5},{0,6},{1,7},{10,8},{11,9},{12,... | collective-permute-start | bytes 786440 | tf_op jit(solution)/shard_map/ppermute | solution.py:35
  107.0 11.5 %collective-permute-start.11 = (bf16[1024,128]{1,0:T(8,128)(2,1)S(1)}, bf16[1024,128]{1,0:T(8,128)(2,1)S(1)}, u32[]{:S(2)}, u32[]{:S(2)}) collective-permute-start(bf16[1024,128]{1,0:T(8,128)(2,1)S(1)} %bitcast.55), channel_id=1, source_target_pairs={{6,0},{7,1},{0,2},{1,3},{2,4},{3,5},{4,6},{5,7},{14,8},{15,9},{8,1... | collective-permute-start | bytes 786440 | tf_op jit(solution)/shard_map/ppermute | solution.py:35
  109.5 11.8 %collective-permute-start.12 = (bf16[1024,128]{1,0:T(8,128)(2,1)S(1)}, bf16[1024,128]{1,0:T(8,128)(2,1)S(1)}, u32[]{:S(2)}, u32[]{:S(2)}) collective-permute-start(bf16[1024,128]{1,0:T(8,128)(2,1)S(1)} %collective-permute-done.8), channel_id=1, source_target_pairs={{2,0},{3,1},{4,2},{5,3},{6,4},{7,5},{0,6},{1,7},{10,8},{11,9},{12,... | collective-permute-start | bytes 786440 | tf_op jit(solution)/shard_map/ppermute | solution.py:35
  112.1 9.6 %collective-permute-start.13 = (bf16[1024,128]{1,0:T(8,128)(2,1)S(1)}, bf16[1024,128]{1,0:T(8,128)(2,1)S(1)}, u32[]{:S(2)}, u32[]{:S(2)}) collective-permute-start(bf16[1024,128]{1,0:T(8,128)(2,1)S(1)} %collective-permute-done.8), channel_id=1, source_target_pairs={{6,0},{7,1},{0,2},{1,3},{2,4},{3,5},{4,6},{5,7},{14,8},{15,9},{8,1... | collective-permute-start | bytes 786440 | tf_op jit(solution)/shard_map/ppermute | solution.py:35
  113.8 7.9 %collective-permute-start.14 = (bf16[1024,128]{1,0:T(8,128)(2,1)S(1)}, bf16[1024,128]{1,0:T(8,128)(2,1)S(1)}, u32[]{:S(2)}, u32[]{:S(2)}) collective-permute-start(bf16[1024,128]{1,0:T(8,128)(2,1)S(1)} %collective-permute-done.9), channel_id=1, source_target_pairs={{8,0},{9,1},{10,2},{11,3},{12,4},{13,5},{14,6},{15,7},{0,8},{1,9},... | collective-permute-start | bytes 786440 | tf_op jit(solution)/shard_map/ppermute | solution.py:35
  132.0 22.8 %all-to-all-start.3 = ((f32[16,64,128]{2,1,0:T(8,128)}), f32[16,64,128]{2,1,0:T(8,128)S(1)}, u32[]{:S(2)}, u32[]{:S(2)}) async-start(f32[16,64,128]{2,1,0:T(8,128)} %bitcast.24), calls=%async_computation.3 | async-start | bytes 1048576 | tf_op jit(solution)/shard_map/all_to_all | solution.py:169
  172.3 10.8 %collective-permute-start.17 = (bf16[1024,128]{1,0:T(8,128)(2,1)S(1)}, bf16[1024,128]{1,0:T(8,128)(2,1)S(1)}, u32[]{:S(2)}, u32[]{:S(2)}) collective-permute-start(bf16[1024,128]{1,0:T(8,128)(2,1)S(1)} %bitcast.48), channel_id=1, source_target_pairs={{4,0},{5,1},{6,2},{7,3},{0,4},{1,5},{2,6},{3,7},{12,8},{13,9},{14,... | collective-permute-start | bytes 786440 | tf_op jit(solution)/shard_map/ppermute | solution.py:35
  175.1 13.1 %collective-permute-start.18 = (bf16[1024,128]{1,0:T(8,128)(2,1)S(1)}, bf16[1024,128]{1,0:T(8,128)(2,1)S(1)}, u32[]{:S(2)}, u32[]{:S(2)}) collective-permute-start(bf16[1024,128]{1,0:T(8,128)(2,1)S(1)} %bitcast.49), channel_id=1, source_target_pairs={{2,0},{3,1},{4,2},{5,3},{6,4},{7,5},{0,6},{1,7},{10,8},{11,9},{12,... | collective-permute-start | bytes 786440 | tf_op jit(solution)/shard_map/ppermute | solution.py:35
  176.3 11.9 %collective-permute-start.19 = (bf16[1024,128]{1,0:T(8,128)(2,1)S(1)}, bf16[1024,128]{1,0:T(8,128)(2,1)S(1)}, u32[]{:S(2)}, u32[]{:S(2)}) collective-permute-start(bf16[1024,128]{1,0:T(8,128)(2,1)S(1)} %bitcast.50), channel_id=1, source_target_pairs={{6,0},{7,1},{0,2},{1,3},{2,4},{3,5},{4,6},{5,7},{14,8},{15,9},{8,1... | collective-permute-start | bytes 786440 | tf_op jit(solution)/shard_map/ppermute | solution.py:35
  179.1 12.0 %collective-permute-start.20 = (bf16[1024,128]{1,0:T(8,128)(2,1)S(1)}, bf16[1024,128]{1,0:T(8,128)(2,1)S(1)}, u32[]{:S(2)}, u32[]{:S(2)}) collective-permute-start(bf16[1024,128]{1,0:T(8,128)(2,1)S(1)} %collective-permute-done.16), channel_id=1, source_target_pairs={{2,0},{3,1},{4,2},{5,3},{6,4},{7,5},{0,6},{1,7},{10,8},{11,9},{12,... | collective-permute-start | bytes 786440 | tf_op jit(solution)/shard_map/ppermute | solution.py:35
  181.7 9.7 %collective-permute-start.21 = (bf16[1024,128]{1,0:T(8,128)(2,1)S(1)}, bf16[1024,128]{1,0:T(8,128)(2,1)S(1)}, u32[]{:S(2)}, u32[]{:S(2)}) collective-permute-start(bf16[1024,128]{1,0:T(8,128)(2,1)S(1)} %collective-permute-done.16), channel_id=1, source_target_pairs={{6,0},{7,1},{0,2},{1,3},{2,4},{3,5},{4,6},{5,7},{14,8},{15,9},{8,1... | collective-permute-start | bytes 786440 | tf_op jit(solution)/shard_map/ppermute | solution.py:35
  183.1 8.4 %collective-permute-start.22 = (bf16[1024,128]{1,0:T(8,128)(2,1)S(1)}, bf16[1024,128]{1,0:T(8,128)(2,1)S(1)}, u32[]{:S(2)}, u32[]{:S(2)}) collective-permute-start(bf16[1024,128]{1,0:T(8,128)(2,1)S(1)} %collective-permute-done.17), channel_id=1, source_target_pairs={{8,0},{9,1},{10,2},{11,3},{12,4},{13,5},{14,6},{15,7},{0,8},{1,9},... | collective-permute-start | bytes 786440 | tf_op jit(solution)/shard_map/ppermute | solution.py:35
  202.7 16.6 %all-to-all-start.5 = ((bf16[16,64,128]{2,1,0:T(8,128)(2,1)}), bf16[16,64,128]{2,1,0:T(8,128)(2,1)S(1)}, u32[]{:S(2)}, u32[]{:S(2)}) async-start(bf16[16,64,128]{2,1,0:T(8,128)(2,1)} %bitcast.28), calls=%async_computation.5 | async-start | bytes 524288 | tf_op jit(solution)/shard_map/all_to_all | solution.py:169
  (25 other events, 280.9 us)
where the time goes:
time: 238 us; the launch traced here: 237 us
  waiting for transfers between devices  81.5 us (34%)
  starting transfers between devices  63.3 us (27%)
  blocking collectives  43.5 us (18%)
  Pallas kernels  18.5 us (8%)
  local copies, waits for them, and re-layouts  15.3 us (6%)
  other arithmetic  12.6 us (5%)
    all_to_all x4, waiting for transfers between devices, swap(): return lax.all_to_all(cells, 'sector', 0, 0, tiled=True)  44.8 us
    all_to_all x3, blocking collectives, swap(): return lax.all_to_all(cells, 'sector', 0, 0, tiled=True)  43.5 us
    ppermute x24, waiting for transfers between devices, fetch(): return lax.ppermute(block, 'row', row_peers(*shift))  36.7 us
    ppermute x24, starting transfers between devices, fetch(): return lax.ppermute(block, 'row', row_peers(*shift))  34.1 us
    all_to_all x4, starting transfers between devices, swap(): return lax.all_to_all(cells, 'sector', 0, 0, tiled=True)  29.2 us
    pallas_call x3, Pallas kernels, block_product(): pl.pallas_call(product_kernel, out_shape=jax.ShapeDtypeStruct((rows * ord...  18.5 us
    dynamic_slice x12, local copies, waits for them, and re-layouts, own_slice(): lax.dynamic_slice_in_dim(cells, sector_id * slice_rows, slice_rows, axis)  6.05 us
  transfers between devices with their start and end apart: 28, of which 20 were waited for; matrix products, arithmetic and copies ran while one was open for 5% of the time, Pallas kernels for 0%

commit v1 on v0

--- a/solution.py
+++ b/solution.py
@@ -37,9 +37,12 @@
     across = fetch(own, 1, 0, 0)
     opposite, above, below = fetch(own, 0, 2, 0), fetch(own, 0, 1, 0), fetch(own, 0, 3, 0)
     relayed = [fetch(across, 0, 1, 0), fetch(across, 0, 3, 0), fetch(opposite, 1, 0, 0)]
-    same_core = [own, across, *lax.optimization_barrier([opposite, above, below, *relayed])]
-    same_core = jnp.concatenate(same_core, axis=0)
-    return [same_core, fetch(same_core, 0, 0, 1)]
+    direct = [own, across, opposite, above, below]
+    order = direct + relayed
+    swapped = [
+        fetch(jnp.concatenate(part, axis=0), 0, 0, 1) for part in (order[:4], order[4:])
+    ]
+    return jnp.concatenate(direct + relayed + swapped, axis=0)
 
 
 def relative_columns(block_columns, blocks_per_device):
@@ -55,60 +58,53 @@
     return (core * len(SHIFTS) + piece) * blocks_per_device + block_columns % blocks_per_device
 
 
-def product_kernel(columns, values, *refs):
-    *pieces, out, tiles, held, arrived, collected = refs
+def product_kernel(columns, values, gathered, *refs):
+    *earlier, out, held, arrived = refs
     rows, count, order, _ = values.shape
 
     def fetch(row):
         return pltpu.make_async_copy(values.at[row], held.at[row], arrived.at[row])
 
-    places, place = [], 0
-    for index, piece in enumerate(pieces):
-        span = piece.shape[0]
-        places.append(
-            pltpu.make_async_copy(piece, tiles.at[pl.ds(place, span)], collected.at[index])
-        )
-        place += span
-    fetch(0).start()
-    for copy in places:
-        copy.start()
-    for row in range(1, rows):
+    for row in range(rows):
         fetch(row).start()
-    for copy in places:
-        copy.wait()
 
     def one_row(row, carry):
         fetch(row).wait()
         total = None
         for k in range(count):
+            column = pl.multiple_of(columns[row * count + k] * order, order)
             term = jnp.dot(
-                held[row, k],
-                tiles[columns[row * count + k]],
-                preferred_element_type=jnp.float32,
+                held[row, k], gathered[pl.ds(column, order), :], preferred_element_type=jnp.float32
             )
             total = term if total is None else total + term
-        out[pl.ds(pl.multiple_of(row * order, order), order), :] = total
+        own_rows = pl.ds(pl.multiple_of(row * order, order), order)
+        for product in earlier:
+            total = total - product[own_rows, :]
+        out[own_rows, :] = total.astype(out.dtype)
         return carry
 
     lax.fori_loop(0, rows, one_row, 0)
 
 
-def block_product(block_values, columns, pieces):
+def block_product(block_values, columns, gathered, *earlier):
     rows, count, order, _ = block_values.shape
-    load_cases = pieces[0].shape[1]
-    pieces = [piece.reshape(-1, order, load_cases) for piece in pieces]
-    tiles = sum(piece.shape[0] for piece in pieces)
+    load_cases = gathered.shape[1]
+    vmem = pl.BlockSpec(memory_space=pltpu.VMEM)
     return pl.pallas_call(
         product_kernel,
-        out_shape=jax.ShapeDtypeStruct((rows * order, load_cases), jnp.float32),
-        in_specs=[pl.BlockSpec(memory_space=pltpu.SMEM)]
-        + [pl.BlockSpec(memory_space=pl.ANY)] * (1 + len(pieces)),
-        out_specs=pl.BlockSpec(memory_space=pltpu.VMEM),
+        out_shape=jax.ShapeDtypeStruct(
+            (rows * order, load_cases), jnp.bfloat16 if earlier else jnp.float32
+        ),
+        in_specs=[
+            pl.BlockSpec(memory_space=pltpu.SMEM),
+            pl.BlockSpec(memory_space=pl.ANY),
+            vmem,
+            *[vmem] * len(earlier),
+        ],
+        out_specs=vmem,
         scratch_shapes=[
-            pltpu.VMEM((tiles, order, load_cases), jnp.bfloat16),
             pltpu.VMEM((rows, count, order, order), jnp.bfloat16),
             pltpu.SemaphoreType.DMA((rows,)),
-            pltpu.SemaphoreType.DMA((len(pieces),)),
         ],
         compiler_params=pltpu.CompilerParams(vmem_limit_bytes=48 * 1024 * 1024),
         cost_estimate=pl.CostEstimate(
@@ -116,7 +112,7 @@
             bytes_accessed=2 * rows * count * order * order,
             transcendentals=0,
         ),
-    )(columns, block_values, *pieces)
+    )(columns, block_values, gathered, *earlier)
 
 
 def reduce_coefficients(sub_diag, main_diag, super_diag):
@@ -207,13 +203,13 @@
     columns = relative_columns(block_columns, block_values.shape[1]).reshape(-1)
     for iteration in range(1, ITERS):
         last = iteration == ITERS - 1
-        product = block_product(block_values[0], columns, gather_pieces(rounded))
+        gathered = gather_pieces(rounded)
         if last:
-            change = (product - earlier_product).astype(jnp.bfloat16)
+            change = block_product(block_values[0], columns, gathered, product)
             change = swap(change.reshape(sectors, slice_rows, load_cases))
             slice_product = slice_product + change.astype(jnp.float32)
         else:
-            earlier_product = product
+            product = block_product(block_values[0], columns, gathered)
             slice_product = swap(product.reshape(sectors, slice_rows, load_cases))
         neighbours = jnp.roll(current, 1, 0) + jnp.roll(current, -1, 0)
         residual = forcing - (

time: 238 us -> 229 us (0.962)
  local copies, waits for them, and re-layouts: 15.3 us -> 10.2 us
  waiting for transfers between devices: 81.5 us -> 79 us
    dynamic_slice x12, local copies, waits for them, and re-layouts: 6.05 us -> 1.59 us  [own_slice(): lax.dynamic_slice_in_dim(cells, sector_id * slice_rows, slice_rows, axis)]
    ppermute x24 -> x27, waiting for transfers between devices: 36.7 us -> 35.1 us  [fetch(): return lax.ppermute(block, 'row', row_peers(*shift))]
    ppermute x24 -> x27, starting transfers between devices: 34.1 us -> 33.9 us  [fetch(): return lax.ppermute(block, 'row', row_peers(*shift))]
  transfers between devices with their start and end apart: 28 -> 31, of which waited for: 20 -> 20; matrix products, arithmetic and copies ran while one was open for 5% -> 5% of each run, Pallas kernels for 0% -> 0%
where the time goes in v1:
time: 229 us; the launch traced here: 228 us
  waiting for transfers between devices  79 us (34%)
  starting transfers between devices  63 us (28%)
  blocking collectives  43.6 us (19%)
  Pallas kernels  17.8 us (8%)
  other arithmetic  11.9 us (5%)
  local copies, waits for them, and re-layouts  10.2 us (4%)
  between operations  2.31 us (1%)
    all_to_all x4, waiting for transfers between devices, swap(): return lax.all_to_all(cells, 'sector', 0, 0, tiled=True)  43.9 us
    all_to_all x3, blocking collectives, swap(): return lax.all_to_all(cells, 'sector', 0, 0, tiled=True)  43.6 us
    ppermute x27, waiting for transfers between devices, fetch(): return lax.ppermute(block, 'row', row_peers(*shift))  35.1 us
    ppermute x27, starting transfers between devices, fetch(): return lax.ppermute(block, 'row', row_peers(*shift))  33.9 us
    all_to_all x4, starting transfers between devices, swap(): return lax.all_to_all(cells, 'sector', 0, 0, tiled=True)  29.1 us
    pallas_call x3, Pallas kernels, block_product(): pl.pallas_call(product_kernel, out_shape=jax.ShapeDtypeStruct((rows * ord...  17.8 us
  transfers between devices with their start and end apart: 31, of which 20 were waited for; matrix products, arithmetic and copies ran while one was open for 5% of the time, Pallas kernels for 0%

profile of v1, /device:TPU:2, one launch (start us, length us, event | category | flops | bytes accessed | tf_op | source)
XLA Modules:
  0.0 228.0 jit_solution(16487947432257881521)
XLA Ops:
  1.3 9.9 %all-to-all-start = ((s32[16,1,1]{2,1,0:T(1,128)}), s32[16,1,1]{2,1,0:T(1,128)S(1)}, u32[]{:S(2)}, u32[]{:S(2)}) async-start(s32[16,1,1]{2,1,0:T(1,128)} %broadcast_in_dim.129), calls=%async_computation | async-start | bytes 16384 | tf_op jit(solution)/shard_map/all_to_all | solution.py:165
  25.6 3.2 %collective-permute-start.1 = (bf16[1024,128]{1,0:T(8,128)(2,1)S(1)}, bf16[1024,128]{1,0:T(8,128)(2,1)S(1)}, u32[]{:S(2)}, u32[]{:S(2)}) collective-permute-start(bf16[1024,128]{1,0:T(8,128)(2,1)S(1)} %get-tuple-element.14), channel_id=1, source_target_pairs={{4,0},{5,1},{6,2},{7,3},{0,4},{1,5},{2,6},{3,7},{12,8},{13,9},{14,... | collective-permute-start | bytes 786440 | tf_op jit(solution)/shard_map/ppermute | solution.py:35
  32.5 3.0 %collective-permute-start.4 = (bf16[1024,128]{1,0:T(8,128)(2,1)S(1)}, bf16[1024,128]{1,0:T(8,128)(2,1)S(1)}, u32[]{:S(2)}, u32[]{:S(2)}) collective-permute-start(bf16[1024,128]{1,0:T(8,128)(2,1)S(1)} %collective-permute-done), channel_id=1, source_target_pairs={{2,0},{3,1},{4,2},{5,3},{6,4},{7,5},{0,6},{1,7},{10,8},{11,9},{12,... | collective-permute-start | bytes 786440 | tf_op jit(solution)/shard_map/ppermute | solution.py:35
  37.8 4.6 %collective-permute-done.2 = bf16[1024,128]{1,0:T(8,128)(2,1)S(1)} collective-permute-done((bf16[1024,128]{1,0:T(8,128)(2,1)S(1)}, bf16[1024,128]{1,0:T(8,128)(2,1)S(1)}, u32[]{:S(2)}, u32[]{:S(2)}) %collective-permute-start.2) | collective-permute-done | bytes 262176 | tf_op jit(solution)/shard_map/ppermute | solution.py:35
  42.7 3.3 %collective-permute-done.4 = bf16[1024,128]{1,0:T(8,128)(2,1)S(1)} collective-permute-done((bf16[1024,128]{1,0:T(8,128)(2,1)S(1)}, bf16[1024,128]{1,0:T(8,128)(2,1)S(1)}, u32[]{:S(2)}, u32[]{:S(2)}) %collective-permute-start.4) | collective-permute-done | bytes 262176 | tf_op jit(solution)/shard_map/ppermute | solution.py:35
  48.9 5.8 %shard_map.91 = f32[1024,128]{1,0:T(8,128)} custom-call(s32[64]{0:T(128)S(1)} %reshape.200.columns, bf16[4,16,256,256]{3,2,1,0:T(8,128)(2,1)} %bitcast.33, bf16[16384,128]{1,0:T(8,128)(2,1)S(1)} %constant_dynamic-update-slice_fusion.gathered), custom_call_target="tpu_custom_call" | custom-call | flops 1073741824 | bytes 8388608 | tf_op jit(solution)/shard_map/pallas_call | solution.py:93
  54.8 8.1 %all-to-all-start.1 = ((f32[16,64,128]{2,1,0:T(8,128)}), f32[16,64,128]{2,1,0:T(8,128)S(1)}, u32[]{:S(2)}, u32[]{:S(2)}) async-start(f32[16,64,128]{2,1,0:T(8,128)} %bitcast.18), calls=%async_computation.1 | async-start | bytes 1048576 | tf_op jit(solution)/shard_map/all_to_all | solution.py:165
  63.6 16.0 %all-to-all-done.1 = f32[16,64,128]{2,1,0:T(8,128)S(1)} async-done(((f32[16,64,128]{2,1,0:T(8,128)}), f32[16,64,128]{2,1,0:T(8,128)S(1)}, u32[]{:S(2)}, u32[]{:S(2)}) %all-to-all-start.1) | async-done | bytes 524320 | tf_op jit(solution)/shard_map/all_to_all | solution.py:165
  82.1 14.4 %all_to_all.36 = bf16[16,64,128]{2,1,0:T(8,128)(2,1)S(1)} all-to-all(bf16[16,64,128]{2,1,0:T(8,128)(2,1)S(1)} %get-tuple-element.11), channel_id=1, replica_groups=mesh['sector'=16,'row'=16] {'sector'}, dimensions={0} | all-to-all | bytes 524288 | tf_op jit(solution)/shard_map/all_to_all | solution.py:165
  97.9 2.8 %collective-permute-start.10 = (bf16[1024,128]{1,0:T(8,128)(2,1)S(1)}, bf16[1024,128]{1,0:T(8,128)(2,1)S(1)}, u32[]{:S(2)}, u32[]{:S(2)}) collective-permute-start(bf16[1024,128]{1,0:T(8,128)(2,1)S(1)} %bitcast.43), channel_id=1, source_target_pairs={{4,0},{5,1},{6,2},{7,3},{0,4},{1,5},{2,6},{3,7},{12,8},{13,9},{14,... | collective-permute-start | bytes 786440 | tf_op jit(solution)/shard_map/ppermute | solution.py:35
  104.4 2.6 %collective-permute-start.13 = (bf16[1024,128]{1,0:T(8,128)(2,1)S(1)}, bf16[1024,128]{1,0:T(8,128)(2,1)S(1)}, u32[]{:S(2)}, u32[]{:S(2)}) collective-permute-start(bf16[1024,128]{1,0:T(8,128)(2,1)S(1)} %collective-permute-done.9), channel_id=1, source_target_pairs={{2,0},{3,1},{4,2},{5,3},{6,4},{7,5},{0,6},{1,7},{10,8},{11,9},{12,... | collective-permute-start | bytes 786440 | tf_op jit(solution)/shard_map/ppermute | solution.py:35
  110.8 3.1 %collective-permute-done.11 = bf16[1024,128]{1,0:T(8,128)(2,1)S(1)} collective-permute-done((bf16[1024,128]{1,0:T(8,128)(2,1)S(1)}, bf16[1024,128]{1,0:T(8,128)(2,1)S(1)}, u32[]{:S(2)}, u32[]{:S(2)}) %collective-permute-start.11) | collective-permute-done | bytes 262176 | tf_op jit(solution)/shard_map/ppermute | solution.py:35
  114.1 2.5 %collective-permute-done.13 = bf16[1024,128]{1,0:T(8,128)(2,1)S(1)} collective-permute-done((bf16[1024,128]{1,0:T(8,128)(2,1)S(1)}, bf16[1024,128]{1,0:T(8,128)(2,1)S(1)}, u32[]{:S(2)}, u32[]{:S(2)}) %collective-permute-start.13) | collective-permute-done | bytes 262176 | tf_op jit(solution)/shard_map/ppermute | solution.py:35
  120.0 5.8 %shard_map.92.refs_0_ = f32[1024,128]{1,0:T(8,128)} custom-call(s32[64]{0:T(128)S(1)} %reshape.200.columns, bf16[4,16,256,256]{3,2,1,0:T(8,128)(2,1)} %bitcast.34, bf16[16384,128]{1,0:T(8,128)(2,1)S(1)} %constant_dynamic-update-slice_fusion.10.gathered), custom_call_target="tpu_custom_call" | custom-call | flops 1073741824 | bytes 8388608 | tf_op jit(solution)/shard_map/pallas_call | solution.py:93
  125.8 5.6 %all-to-all-start.3 = ((f32[16,64,128]{2,1,0:T(8,128)}), f32[16,64,128]{2,1,0:T(8,128)S(1)}, u32[]{:S(2)}, u32[]{:S(2)}) async-start(f32[16,64,128]{2,1,0:T(8,128)} %bitcast.20), calls=%async_computation.3 | async-start | bytes 1048576 | tf_op jit(solution)/shard_map/all_to_all | solution.py:165
  131.4 16.9 %all-to-all-done.3 = f32[16,64,128]{2,1,0:T(8,128)S(1)} async-done(((f32[16,64,128]{2,1,0:T(8,128)}), f32[16,64,128]{2,1,0:T(8,128)S(1)}, u32[]{:S(2)}, u32[]{:S(2)}) %all-to-all-start.3) | async-done | bytes 524320 | tf_op jit(solution)/shard_map/all_to_all | solution.py:165
  150.3 14.4 %all_to_all.37 = bf16[16,64,128]{2,1,0:T(8,128)(2,1)S(1)} all-to-all(bf16[16,64,128]{2,1,0:T(8,128)(2,1)S(1)} %get-tuple-element.9), channel_id=1, replica_groups=mesh['sector'=16,'row'=16] {'sector'}, dimensions={0} | all-to-all | bytes 524288 | tf_op jit(solution)/shard_map/all_to_all | solution.py:165
  165.7 2.6 %collective-permute-start.19 = (bf16[1024,128]{1,0:T(8,128)(2,1)S(1)}, bf16[1024,128]{1,0:T(8,128)(2,1)S(1)}, u32[]{:S(2)}, u32[]{:S(2)}) collective-permute-start(bf16[1024,128]{1,0:T(8,128)(2,1)S(1)} %bitcast.37), channel_id=1, source_target_pairs={{4,0},{5,1},{6,2},{7,3},{0,4},{1,5},{2,6},{3,7},{12,8},{13,9},{14,... | collective-permute-start | bytes 786440 | tf_op jit(solution)/shard_map/ppermute | solution.py:35
  176.4 2.6 %collective-permute-start.24 = (bf16[1024,128]{1,0:T(8,128)(2,1)S(1)}, bf16[1024,128]{1,0:T(8,128)(2,1)S(1)}, u32[]{:S(2)}, u32[]{:S(2)}) collective-permute-start(bf16[1024,128]{1,0:T(8,128)(2,1)S(1)} %collective-permute-done.19), channel_id=1, source_target_pairs={{8,0},{9,1},{10,2},{11,3},{12,4},{13,5},{14,6},{15,7},{0,8},{1,9},... | collective-permute-start | bytes 786440 | tf_op jit(solution)/shard_map/ppermute | solution.py:35
  181.7 2.5 %collective-permute-done.22 = bf16[1024,128]{1,0:T(8,128)(2,1)S(1)} collective-permute-done((bf16[1024,128]{1,0:T(8,128)(2,1)S(1)}, bf16[1024,128]{1,0:T(8,128)(2,1)S(1)}, u32[]{:S(2)}, u32[]{:S(2)}) %collective-permute-start.22) | collective-permute-done | bytes 262176 | tf_op jit(solution)/shard_map/ppermute | solution.py:35
  187.6 6.2 %shard_map.93 = bf16[1024,128]{1,0:T(8,128)(2,1)} custom-call(s32[64]{0:T(128)S(1)} %reshape.200.columns, bf16[4,16,256,256]{3,2,1,0:T(8,128)(2,1)} %bitcast.35, bf16[16384,128]{1,0:T(8,128)(2,1)S(1)} %constant_dynamic-update-slice_fusion.20.gathered, f32[1024,128]{1,0:T(8,128)} %shard_map.92.refs_0_), custom_call_target="tpu_custom_call" | custom-call | flops 1073741824 | bytes 8388608 | tf_op jit(solution)/shard_map/pallas_call | solution.py:93
  193.8 5.5 %all-to-all-start.5 = ((bf16[16,64,128]{2,1,0:T(8,128)(2,1)}), bf16[16,64,128]{2,1,0:T(8,128)(2,1)S(1)}, u32[]{:S(2)}, u32[]{:S(2)}) async-start(bf16[16,64,128]{2,1,0:T(8,128)(2,1)} %bitcast.22), calls=%async_computation.5 | async-start | bytes 524288 | tf_op jit(solution)/shard_map/all_to_all | solution.py:165
  199.5 11.0 %all-to-all-done.5 = bf16[16,64,128]{2,1,0:T(8,128)(2,1)S(1)} async-done(((bf16[16,64,128]{2,1,0:T(8,128)(2,1)}), bf16[16,64,128]{2,1,0:T(8,128)(2,1)S(1)}, u32[]{:S(2)}, u32[]{:S(2)}) %all-to-all-start.5) | async-done | bytes 262176 | tf_op jit(solution)/shard_map/all_to_all | solution.py:165
  212.3 14.8 %all_to_all.38 = bf16[16,64,128]{2,1,0:T(8,128)(2,1)S(1)} all-to-all(bf16[16,64,128]{2,1,0:T(8,128)(2,1)S(1)} %fusion.37), channel_id=1, replica_groups=mesh['sector'=16,'row'=16] {'sector'}, dimensions={0} | all-to-all | bytes 524288 | tf_op jit(solution)/shard_map/all_to_all | solution.py:165
  (182 shorter events, 58.2 us)
Async XLA Ops:
  1.3 18.0 %all-to-all-start = ((s32[16,1,1]{2,1,0:T(1,128)}), s32[16,1,1]{2,1,0:T(1,128)S(1)}, u32[]{:S(2)}, u32[]{:S(2)}) async-start(s32[16,1,1]{2,1,0:T(1,128)} %broadcast_in_dim.129), calls=%async_computation | async-start | bytes 16384 | tf_op jit(solution)/shard_map/all_to_all | solution.py:165
  23.4 9.1 %collective-permute-start = (bf16[1024,128]{1,0:T(8,128)(2,1)S(1)}, bf16[1024,128]{1,0:T(8,128)(2,1)S(1)}, u32[]{:S(2)}, u32[]{:S(2)}) collective-permute-start(bf16[1024,128]{1,0:T(8,128)(2,1)S(1)} %get-tuple-element.14), channel_id=1, source_target_pairs={{8,0},{9,1},{10,2},{11,3},{12,4},{13,5},{14,6},{15,7},{0,8},{1,9},... | collective-permute-start | bytes 786440 | tf_op jit(solution)/shard_map/ppermute | solution.py:35
  25.6 10.8 %collective-permute-start.1 = (bf16[1024,128]{1,0:T(8,128)(2,1)S(1)}, bf16[1024,128]{1,0:T(8,128)(2,1)S(1)}, u32[]{:S(2)}, u32[]{:S(2)}) collective-permute-start(bf16[1024,128]{1,0:T(8,128)(2,1)S(1)} %get-tuple-element.14), channel_id=1, source_target_pairs={{4,0},{5,1},{6,2},{7,3},{0,4},{1,5},{2,6},{3,7},{12,8},{13,9},{14,... | collective-permute-start | bytes 786440 | tf_op jit(solution)/shard_map/ppermute | solution.py:35
  28.8 13.6 %collective-permute-start.2 = (bf16[1024,128]{1,0:T(8,128)(2,1)S(1)}, bf16[1024,128]{1,0:T(8,128)(2,1)S(1)}, u32[]{:S(2)}, u32[]{:S(2)}) collective-permute-start(bf16[1024,128]{1,0:T(8,128)(2,1)S(1)} %get-tuple-element.14), channel_id=1, source_target_pairs={{2,0},{3,1},{4,2},{5,3},{6,4},{7,5},{0,6},{1,7},{10,8},{11,9},{12,... | collective-permute-start | bytes 786440 | tf_op jit(solution)/shard_map/ppermute | solution.py:35
  29.9 12.8 %collective-permute-start.3 = (bf16[1024,128]{1,0:T(8,128)(2,1)S(1)}, bf16[1024,128]{1,0:T(8,128)(2,1)S(1)}, u32[]{:S(2)}, u32[]{:S(2)}) collective-permute-start(bf16[1024,128]{1,0:T(8,128)(2,1)S(1)} %get-tuple-element.14), channel_id=1, source_target_pairs={{6,0},{7,1},{0,2},{1,3},{2,4},{3,5},{4,6},{5,7},{14,8},{15,9},{8,1... | collective-permute-start | bytes 786440 | tf_op jit(solution)/shard_map/ppermute | solution.py:35
  32.5 13.5 %collective-permute-start.4 = (bf16[1024,128]{1,0:T(8,128)(2,1)S(1)}, bf16[1024,128]{1,0:T(8,128)(2,1)S(1)}, u32[]{:S(2)}, u32[]{:S(2)}) collective-permute-start(bf16[1024,128]{1,0:T(8,128)(2,1)S(1)} %collective-permute-done), channel_id=1, source_target_pairs={{2,0},{3,1},{4,2},{5,3},{6,4},{7,5},{0,6},{1,7},{10,8},{11,9},{12,... | collective-permute-start | bytes 786440 | tf_op jit(solution)/shard_map/ppermute | solution.py:35
  35.5 10.5 %collective-permute-start.5 = (bf16[1024,128]{1,0:T(8,128)(2,1)S(1)}, bf16[1024,128]{1,0:T(8,128)(2,1)S(1)}, u32[]{:S(2)}, u32[]{:S(2)}) collective-permute-start(bf16[1024,128]{1,0:T(8,128)(2,1)S(1)} %collective-permute-done), channel_id=1, source_target_pairs={{6,0},{7,1},{0,2},{1,3},{2,4},{3,5},{4,6},{5,7},{14,8},{15,9},{8,1... | collective-permute-start | bytes 786440 | tf_op jit(solution)/shard_map/ppermute | solution.py:35
  36.4 9.6 %collective-permute-start.6 = (bf16[1024,128]{1,0:T(8,128)(2,1)S(1)}, bf16[1024,128]{1,0:T(8,128)(2,1)S(1)}, u32[]{:S(2)}, u32[]{:S(2)}) collective-permute-start(bf16[1024,128]{1,0:T(8,128)(2,1)S(1)} %collective-permute-done.1), channel_id=1, source_target_pairs={{8,0},{9,1},{10,2},{11,3},{12,4},{13,5},{14,6},{15,7},{0,8},{1,9},... | collective-permute-start | bytes 786440 | tf_op jit(solution)/shard_map/ppermute | solution.py:35
  54.8 24.8 %all-to-all-start.1 = ((f32[16,64,128]{2,1,0:T(8,128)}), f32[16,64,128]{2,1,0:T(8,128)S(1)}, u32[]{:S(2)}, u32[]{:S(2)}) async-start(f32[16,64,128]{2,1,0:T(8,128)} %bitcast.18), calls=%async_computation.1 | async-start | bytes 1048576 | tf_op jit(solution)/shard_map/all_to_all | solution.py:165
  97.9 10.7 %collective-permute-start.10 = (bf16[1024,128]{1,0:T(8,128)(2,1)S(1)}, bf16[1024,128]{1,0:T(8,128)(2,1)S(1)}, u32[]{:S(2)}, u32[]{:S(2)}) collective-permute-start(bf16[1024,128]{1,0:T(8,128)(2,1)S(1)} %bitcast.43), channel_id=1, source_target_pairs={{4,0},{5,1},{6,2},{7,3},{0,4},{1,5},{2,6},{3,7},{12,8},{13,9},{14,... | collective-permute-start | bytes 786440 | tf_op jit(solution)/shard_map/ppermute | solution.py:35
  100.7 13.2 %collective-permute-start.11 = (bf16[1024,128]{1,0:T(8,128)(2,1)S(1)}, bf16[1024,128]{1,0:T(8,128)(2,1)S(1)}, u32[]{:S(2)}, u32[]{:S(2)}) collective-permute-start(bf16[1024,128]{1,0:T(8,128)(2,1)S(1)} %bitcast.44), channel_id=1, source_target_pairs={{2,0},{3,1},{4,2},{5,3},{6,4},{7,5},{0,6},{1,7},{10,8},{11,9},{12,... | collective-permute-start | bytes 786440 | tf_op jit(solution)/shard_map/ppermute | solution.py:35
  101.9 12.2 %collective-permute-start.12 = (bf16[1024,128]{1,0:T(8,128)(2,1)S(1)}, bf16[1024,128]{1,0:T(8,128)(2,1)S(1)}, u32[]{:S(2)}, u32[]{:S(2)}) collective-permute-start(bf16[1024,128]{1,0:T(8,128)(2,1)S(1)} %bitcast.45), channel_id=1, source_target_pairs={{6,0},{7,1},{0,2},{1,3},{2,4},{3,5},{4,6},{5,7},{14,8},{15,9},{8,1... | collective-permute-start | bytes 786440 | tf_op jit(solution)/shard_map/ppermute | solution.py:35
  104.4 12.3 %collective-permute-start.13 = (bf16[1024,128]{1,0:T(8,128)(2,1)S(1)}, bf16[1024,128]{1,0:T(8,128)(2,1)S(1)}, u32[]{:S(2)}, u32[]{:S(2)}) collective-permute-start(bf16[1024,128]{1,0:T(8,128)(2,1)S(1)} %collective-permute-done.9), channel_id=1, source_target_pairs={{2,0},{3,1},{4,2},{5,3},{6,4},{7,5},{0,6},{1,7},{10,8},{11,9},{12,... | collective-permute-start | bytes 786440 | tf_op jit(solution)/shard_map/ppermute | solution.py:35
  107.0 10.0 %collective-permute-start.14 = (bf16[1024,128]{1,0:T(8,128)(2,1)S(1)}, bf16[1024,128]{1,0:T(8,128)(2,1)S(1)}, u32[]{:S(2)}, u32[]{:S(2)}) collective-permute-start(bf16[1024,128]{1,0:T(8,128)(2,1)S(1)} %collective-permute-done.9), channel_id=1, source_target_pairs={{6,0},{7,1},{0,2},{1,3},{2,4},{3,5},{4,6},{5,7},{14,8},{15,9},{8,1... | collective-permute-start | bytes 786440 | tf_op jit(solution)/shard_map/ppermute | solution.py:35
  108.6 8.4 %collective-permute-start.15 = (bf16[1024,128]{1,0:T(8,128)(2,1)S(1)}, bf16[1024,128]{1,0:T(8,128)(2,1)S(1)}, u32[]{:S(2)}, u32[]{:S(2)}) collective-permute-start(bf16[1024,128]{1,0:T(8,128)(2,1)S(1)} %collective-permute-done.10), channel_id=1, source_target_pairs={{8,0},{9,1},{10,2},{11,3},{12,4},{13,5},{14,6},{15,7},{0,8},{1,9},... | collective-permute-start | bytes 786440 | tf_op jit(solution)/shard_map/ppermute | solution.py:35
  125.8 22.6 %all-to-all-start.3 = ((f32[16,64,128]{2,1,0:T(8,128)}), f32[16,64,128]{2,1,0:T(8,128)S(1)}, u32[]{:S(2)}, u32[]{:S(2)}) async-start(f32[16,64,128]{2,1,0:T(8,128)} %bitcast.20), calls=%async_computation.3 | async-start | bytes 1048576 | tf_op jit(solution)/shard_map/all_to_all | solution.py:165
  164.7 7.9 %collective-permute-start.18 = (bf16[1024,128]{1,0:T(8,128)(2,1)S(1)}, bf16[1024,128]{1,0:T(8,128)(2,1)S(1)}, u32[]{:S(2)}, u32[]{:S(2)}) collective-permute-start(bf16[1024,128]{1,0:T(8,128)(2,1)S(1)} %bitcast.36), channel_id=1, source_target_pairs={{8,0},{9,1},{10,2},{11,3},{12,4},{13,5},{14,6},{15,7},{0,8},{1,9},... | collective-permute-start | bytes 786440 | tf_op jit(solution)/shard_map/ppermute | solution.py:35
  165.7 10.7 %collective-permute-start.19 = (bf16[1024,128]{1,0:T(8,128)(2,1)S(1)}, bf16[1024,128]{1,0:T(8,128)(2,1)S(1)}, u32[]{:S(2)}, u32[]{:S(2)}) collective-permute-start(bf16[1024,128]{1,0:T(8,128)(2,1)S(1)} %bitcast.37), channel_id=1, source_target_pairs={{4,0},{5,1},{6,2},{7,3},{0,4},{1,5},{2,6},{3,7},{12,8},{13,9},{14,... | collective-permute-start | bytes 786440 | tf_op jit(solution)/shard_map/ppermute | solution.py:35
  168.3 13.1 %collective-permute-start.20 = (bf16[1024,128]{1,0:T(8,128)(2,1)S(1)}, bf16[1024,128]{1,0:T(8,128)(2,1)S(1)}, u32[]{:S(2)}, u32[]{:S(2)}) collective-permute-start(bf16[1024,128]{1,0:T(8,128)(2,1)S(1)} %bitcast.38), channel_id=1, source_target_pairs={{2,0},{3,1},{4,2},{5,3},{6,4},{7,5},{0,6},{1,7},{10,8},{11,9},{12,... | collective-permute-start | bytes 786440 | tf_op jit(solution)/shard_map/ppermute | solution.py:35
  169.5 12.2 %collective-permute-start.21 = (bf16[1024,128]{1,0:T(8,128)(2,1)S(1)}, bf16[1024,128]{1,0:T(8,128)(2,1)S(1)}, u32[]{:S(2)}, u32[]{:S(2)}) collective-permute-start(bf16[1024,128]{1,0:T(8,128)(2,1)S(1)} %bitcast.39), channel_id=1, source_target_pairs={{6,0},{7,1},{0,2},{1,3},{2,4},{3,5},{4,6},{5,7},{14,8},{15,9},{8,1... | collective-permute-start | bytes 786440 | tf_op jit(solution)/shard_map/ppermute | solution.py:35
  172.6 11.6 %collective-permute-start.22 = (bf16[1024,128]{1,0:T(8,128)(2,1)S(1)}, bf16[1024,128]{1,0:T(8,128)(2,1)S(1)}, u32[]{:S(2)}, u32[]{:S(2)}) collective-permute-start(bf16[1024,128]{1,0:T(8,128)(2,1)S(1)} %collective-permute-done.18), channel_id=1, source_target_pairs={{2,0},{3,1},{4,2},{5,3},{6,4},{7,5},{0,6},{1,7},{10,8},{11,9},{12,... | collective-permute-start | bytes 786440 | tf_op jit(solution)/shard_map/ppermute | solution.py:35
  174.9 9.7 %collective-permute-start.23 = (bf16[1024,128]{1,0:T(8,128)(2,1)S(1)}, bf16[1024,128]{1,0:T(8,128)(2,1)S(1)}, u32[]{:S(2)}, u32[]{:S(2)}) collective-permute-start(bf16[1024,128]{1,0:T(8,128)(2,1)S(1)} %collective-permute-done.18), channel_id=1, source_target_pairs={{6,0},{7,1},{0,2},{1,3},{2,4},{3,5},{4,6},{5,7},{14,8},{15,9},{8,1... | collective-permute-start | bytes 786440 | tf_op jit(solution)/shard_map/ppermute | solution.py:35
  176.4 8.2 %collective-permute-start.24 = (bf16[1024,128]{1,0:T(8,128)(2,1)S(1)}, bf16[1024,128]{1,0:T(8,128)(2,1)S(1)}, u32[]{:S(2)}, u32[]{:S(2)}) collective-permute-start(bf16[1024,128]{1,0:T(8,128)(2,1)S(1)} %collective-permute-done.19), channel_id=1, source_target_pairs={{8,0},{9,1},{10,2},{11,3},{12,4},{13,5},{14,6},{15,7},{0,8},{1,9},... | collective-permute-start | bytes 786440 | tf_op jit(solution)/shard_map/ppermute | solution.py:35
  193.8 16.6 %all-to-all-start.5 = ((bf16[16,64,128]{2,1,0:T(8,128)(2,1)}), bf16[16,64,128]{2,1,0:T(8,128)(2,1)S(1)}, u32[]{:S(2)}, u32[]{:S(2)}) async-start(bf16[16,64,128]{2,1,0:T(8,128)(2,1)} %bitcast.22), calls=%async_computation.5 | async-start | bytes 524288 | tf_op jit(solution)/shard_map/all_to_all | solution.py:165
  (9 other events, 73.2 us)

commit v2 on v1

v2 whole, which is shorter than its diff:
```python
import functools
import math

import jax
import jax.numpy as jnp
from jax import lax
from jax.experimental import pallas as pl
from jax.experimental.pallas import tpu as pltpu
from jax.sharding import PartitionSpec as P

ITERS = 4
LEVELS = 3
ROW_PARTS = (2, 4, 2)


def row_peers(shift_x, shift_y, shift_core):
    pairs = []
    for x in range(ROW_PARTS[0]):
        for y in range(ROW_PARTS[1]):
            for core in range(ROW_PARTS[2]):
                source = (
                    ((x + shift_x) % ROW_PARTS[0] * ROW_PARTS[1] + (y + shift_y) % ROW_PARTS[1])
                    * ROW_PARTS[2]
                    + (core + shift_core) % ROW_PARTS[2]
                )
                target = (x * ROW_PARTS[1] + y) * ROW_PARTS[2] + core
                pairs.append((source, target))
    return pairs


SHIFTS = ((0, 0), (1, 0), (0, 2), (0, 1), (0, 3), (1, 1), (1, 3), (1, 2))


def gather_pieces(own):
    def fetch(block, *shift):
        return lax.ppermute(block, "row", row_peers(*shift))

    across = fetch(own, 1, 0, 0)
    opposite, above, below = fetch(own, 0, 2, 0), fetch(own, 0, 1, 0), fetch(own, 0, 3, 0)
    relayed = [fetch(across, 0, 1, 0), fetch(across, 0, 3, 0), fetch(opposite, 1, 0, 0)]
    direct = [own, across, opposite, above, below]
    order = direct + relayed
    swapped = [
        fetch(jnp.concatenate(part, axis=0), 0, 0, 1) for part in (order[:4], order[4:])
    ]
    return jnp.concatenate(direct + relayed + swapped, axis=0)


def relative_columns(block_columns, blocks_per_device):
    row_id = lax.axis_index("row")
    owner = block_columns // blocks_per_device
    xs, ys, cores = ROW_PARTS
    core = (owner - row_id) % cores
    shift_y = (owner // cores - row_id // cores) % ys
    shift_x = (owner // (cores * ys) - row_id // (cores * ys)) % xs
    piece = sum(
        jnp.where((shift_x == x) & (shift_y == y), index, 0) for index, (x, y) in enumerate(SHIFTS)
    )
    return (core * len(SHIFTS) + piece) * blocks_per_device + block_columns % blocks_per_device


def product_kernel(columns, values, gathered, *refs):
    *earlier, out = refs
    rows, count, order, _ = values.shape

    def one_row(row, carry):
        total = None
        for k in range(count):
            column = pl.multiple_of(columns[row * count + k] * order, order)
            term = jnp.dot(
                values[row, k], gathered[pl.ds(column, order), :], preferred_element_type=jnp.float32
            )
            total = term if total is None else total + term
        own_rows = pl.ds(pl.multiple_of(row * order, order), order)
        for product in earlier:
            total = total - product[own_rows, :]
        out[own_rows, :] = total.astype(out.dtype)
        return carry

    lax.fori_loop(0, rows, one_row, 0)


def block_product(block_values, columns, gathered, *earlier):
    rows, count, order, _ = block_values.shape
    load_cases = gathered.shape[1]
    vmem = pl.BlockSpec(memory_space=pltpu.VMEM)
    return pl.pallas_call(
        product_kernel,
        out_shape=jax.ShapeDtypeStruct(
            (rows * order, load_cases), jnp.bfloat16 if earlier else jnp.float32
        ),
        in_specs=[
            pl.BlockSpec(memory_space=pltpu.SMEM),
            vmem,
            vmem,
            *[vmem] * len(earlier),
        ],
        out_specs=vmem,
        compiler_params=pltpu.CompilerParams(vmem_limit_bytes=16 * 1024 * 1024),
        cost_estimate=pl.CostEstimate(
            flops=2 * rows * count * order * order * load_cases,
            bytes_accessed=2 * rows * count * order * order,
            transcendentals=0,
        ),
    )(columns, block_values, gathered, *earlier)


def shifted(cells, distance):
    return [cells[(sector - distance) % len(cells)] for sector in range(len(cells))]


def reduce_coefficients(sub_diag, main_diag, super_diag):
    factors = []
    for exponent in range(LEVELS):
        stride = 2**exponent
        lower = [-a / b for a, b in zip(sub_diag, shifted(main_diag, stride))]
        upper = [-a / b for a, b in zip(super_diag, shifted(main_diag, -stride))]
        factors.append((lower, upper))
        sub_diag, main_diag, super_diag = (
            [a * b for a, b in zip(lower, shifted(sub_diag, stride))],
            [
                main + a * b + c * d
                for main, a, b, c, d in zip(
                    main_diag,
                    lower,
                    shifted(super_diag, stride),
                    upper,
                    shifted(sub_diag, -stride),
                )
            ],
            [a * b for a, b in zip(upper, shifted(super_diag, -stride))],
        )
    return factors, main_diag


def apply_reduction(factors, reduced, right_side):
    for exponent in range(LEVELS):
        stride = 2**exponent
        lower, upper = factors[exponent]
        right_side = [
            own + a * below + b * above
            for own, a, below, b, above in zip(
                right_side,
                lower,
                shifted(right_side, stride),
                upper,
                shifted(right_side, -stride),
            )
        ]
    return [a / b for a, b in zip(right_side, reduced)]


GAINS = 2 * LEVELS
REDUCED, DIAGONAL, COUPLING, KINDS = GAINS + 2, GAINS + 3, GAINS + 4, GAINS + 5


def coefficient_kernel(
    classes, own, cosine, sine, mistuning, base, ratio, cosine_load, sine_load, rounded, table
):
    sectors = table.shape[1]
    stiffness = base[...]
    coupling = ratio[...] * stiffness
    diagonal = [stiffness * (1.0 + mistuning[classes[s]]) for s in range(sectors)]
    factors, reduced = reduce_coefficients([-coupling] * sectors, diagonal, [-coupling] * sectors)
    gains = [
        apply_reduction(
            factors, reduced, [jnp.full(stiffness.shape, wave[s], jnp.float32) for s in range(sectors)]
        )
        for wave in (cosine, sine)
    ]
    kinds = [part for pair in factors for part in pair]
    kinds += [*gains, reduced, diagonal, [coupling] * sectors]
    for kind, cells in enumerate(kinds):
        for s in range(sectors):
            table[kind, s] = cells[s]
    groups, lanes = stiffness.shape
    cosine_gain, sine_gain = table[GAINS, own[0]].T, table[GAINS + 1, own[0]].T
    for group in range(groups):
        rows = pl.ds(group * lanes, lanes)
        rounded[rows, :] = (
            cosine_gain[:, group : group + 1] * cosine_load[rows, :]
            + sine_gain[:, group : group + 1] * sine_load[rows, :]
        ).astype(rounded.dtype)


def sector_kernel(last, cosine, sine, table, cosine_load, sine_load, current, *refs):
    products, outs = (refs[:2], refs[2:]) if last else (refs[:1], refs[1:])
    sectors, rows, _ = current.shape
    step = 16

    def one_group(group, carry):
        at = pl.ds(pl.multiple_of(group * step, step), step)
        wave_c, wave_s = cosine_load[at, :], sine_load[at, :]
        before = [current[s, at, :] for s in range(sectors)]
        below, above = shifted(before, 1), shifted(before, -1)
        residual = []
        for s in range(sectors):
            forcing = cosine[s] * wave_c + sine[s] * wave_s
            product = sum(part[s, at, :].astype(jnp.float32) for part in products)
            applied = (
                table[DIAGONAL, s, at, :] * before[s]
                - table[COUPLING, s, at, :] * (below[s] + above[s])
                + product
            )
            residual.append(forcing - applied)
        factors = [
            tuple([table[2 * level + side, s, at, :] for s in range(sectors)] for side in range(2))
            for level in range(LEVELS)
        ]
        reduced = [table[REDUCED, s, at, :] for s in range(sectors)]
        correction = apply_reduction(factors, reduced, residual)
        for s in range(sectors):
            after = before[s] + correction[s]
            if last:
                sent = before[s].astype(jnp.bfloat16).astype(jnp.float32)
                outs[0][s, at, :] = (after - sent).astype(jnp.bfloat16)
            else:
                outs[0][s, at, :] = after.astype(jnp.bfloat16)
                outs[1][s, at, :] = after
        return carry

    lax.fori_loop(0, rows // step, one_group, 0)


def shards(
    cosine_load,
    sine_load,
    base_stiffness,
    coupling_ratio,
    mistuning,
    sector_class,
    engine_order,
    block_values,
    block_columns,
):
    sectors = lax.axis_size("sector")
    sector_id = lax.axis_index("sector")
    local_rows, load_cases = cosine_load.shape
    slice_rows = local_rows // sectors
    smem, vmem = (pl.BlockSpec(memory_space=space) for space in (pltpu.SMEM, pltpu.VMEM))

    def swap(cells):
        return lax.all_to_all(cells, "sector", 0, 0, tiled=True)

    def own_slice(cells, axis):
        return lax.dynamic_slice_in_dim(cells, sector_id * slice_rows, slice_rows, axis)

    all_classes = swap(jnp.broadcast_to(sector_class[:, None], (sectors, 1))).reshape(-1)
    turns = (engine_order[0] * jnp.arange(sectors, dtype=jnp.int32)) % sectors
    angle = turns.astype(jnp.float32) * (2.0 * math.pi / sectors)
    cosine, sine = jnp.cos(angle), jnp.sin(angle)

    lanes = 128
    groups = local_rows // lanes
    rounded, table = pl.pallas_call(
        coefficient_kernel,
        out_shape=(
            jax.ShapeDtypeStruct((local_rows, load_cases), jnp.bfloat16),
            jax.ShapeDtypeStruct((KINDS, sectors, groups, lanes), jnp.float32),
        ),
        in_specs=[smem] * 4 + [vmem] * 5,
        out_specs=(vmem, vmem),
        compiler_params=pltpu.CompilerParams(vmem_limit_bytes=16 * 1024 * 1024),
    )(
        all_classes,
        sector_id[None],
        cosine,
        sine,
        mistuning.reshape(-1, groups, lanes),
        base_stiffness.reshape(groups, lanes),
        coupling_ratio.reshape(groups, lanes),
        cosine_load,
        sine_load,
    )

    cosine_slice, sine_slice = own_slice(cosine_load, 0), own_slice(sine_load, 0)
    table = own_slice(table.reshape(KINDS * sectors, local_rows), 1)
    table = jnp.broadcast_to(
        table.reshape(KINDS, sectors, slice_rows, 1), (KINDS, sectors, slice_rows, load_cases)
    )
    current = table[GAINS] * cosine_slice + table[GAINS + 1] * sine_slice

    columns = relative_columns(block_columns, block_values.shape[1]).reshape(-1)
    slice_shape = (sectors, slice_rows, load_cases)
    products = []
    for iteration in range(1, ITERS):
        last = iteration == ITERS - 1
        gathered = gather_pieces(rounded)
        if last:
            change = block_product(block_values[0], columns, gathered, product)
            products.append(swap(change.reshape(slice_shape)))
        else:
            product = block_product(block_values[0], columns, gathered)
            products = [swap(product.reshape(slice_shape))]
        outs = [jax.ShapeDtypeStruct(slice_shape, jnp.bfloat16)]
        if not last:
            outs.append(jax.ShapeDtypeStruct(slice_shape, jnp.float32))
        outs = pl.pallas_call(
            functools.partial(sector_kernel, last),
            out_shape=outs,
            in_specs=[smem] * 2 + [vmem] * (4 + len(products)),
            out_specs=[vmem] * len(outs),
            compiler_params=pltpu.CompilerParams(vmem_limit_bytes=16 * 1024 * 1024),
        )(cosine, sine, table, cosine_slice, sine_slice, current, *products)
        received = swap(outs[0]).reshape(local_rows, load_cases)
        if last:
            return (rounded.astype(jnp.float32) + received.astype(jnp.float32))[None]
        rounded, current = received, outs[1]


def solution(mesh):
    return jax.shard_map(
        shards,
        mesh=mesh,
        in_specs=(
            P("row", None),
            P("row", None),
            P("row"),
            P("row"),
            P(None, "row"),
            P("sector"),
            P(),
            P("sector", "row", None, None, None),
            P("row", None),
        ),
        out_specs=P("sector", "row", None),
        check_vma=False,
    )
```

time: 229 us -> 217 us (0.948)
  blocking collectives: 43.6 us -> 81.3 us
  waiting for transfers between devices: 79 us -> 56.3 us
  starting transfers between devices: 63 us -> 48.6 us
  other arithmetic: 11.9 us -> 2.75 us
    all_to_all x3 -> x5, blocking collectives: 43.6 us -> 81.3 us  [swap(): return lax.all_to_all(cells, 'sector', 0, 0, tiled=True)]
    all_to_all x4 -> x2, waiting for transfers between devices: 43.9 us -> 21.4 us  [swap(): return lax.all_to_all(cells, 'sector', 0, 0, tiled=True)]
    all_to_all x4 -> x2, starting transfers between devices: 29.1 us -> 15.4 us  [swap(): return lax.all_to_all(cells, 'sector', 0, 0, tiled=True)]
    pallas_call x3, Pallas kernels: 17.8 us -> 11 us  [block_product(): pl.pallas_call(product_kernel, out_shape=jax.ShapeDtypeStruct((rows * ord...]
    pallas_call x0 -> x4, Pallas kernels: none -> 4.56 us  [the longest x3 3.34 us: shards(): pl.pallas_call(functools.partial(sector_kernel, last), out_shape=outs, in...]
    unnamed x30 -> x43, local copies, waits for them, and re-layouts: 1.23 us -> 5.56 us
    slice x51 -> x1, local copies, waits for them, and re-layouts: 3.65 us -> 0.09 us  [shards(): current = table[GAINS] * cosine_slice + table[GAINS + 1] * sine_slice]
    add x12 -> x2, other arithmetic: 4.28 us -> 1.19 us  [the longest x1 0.86 us: shards(): return (rounded.astype(jnp.float32) + received.astype(jnp.float32))[None]]
  transfers between devices with their start and end apart: 31 -> 29, of which waited for: 20 -> 20; matrix products, arithmetic and copies ran while one was open for 5% -> 2% of each run, Pallas kernels for 0% -> 0%
where the time goes in v2:
time: 217 us; the launch traced here: 216 us
  blocking collectives  81.3 us (37%)
  waiting for transfers between devices  56.3 us (26%)
  starting transfers between devices  48.6 us (22%)
  Pallas kernels  15.6 us (7%)
  local copies, waits for them, and re-layouts  9.24 us (4%)
  other arithmetic  2.75 us (1%)
    all_to_all x5, blocking collectives, swap(): return lax.all_to_all(cells, 'sector', 0, 0, tiled=True)  81.3 us
    ppermute x27, waiting for transfers between devices, fetch(): return lax.ppermute(block, 'row', row_peers(*shift))  34.9 us
    ppermute x27, starting transfers between devices, fetch(): return lax.ppermute(block, 'row', row_peers(*shift))  33.2 us
    all_to_all x2, waiting for transfers between devices, swap(): return lax.all_to_all(cells, 'sector', 0, 0, tiled=True)  21.4 us
    all_to_all x2, starting transfers between devices, swap(): return lax.all_to_all(cells, 'sector', 0, 0, tiled=True)  15.4 us
    pallas_call x3, Pallas kernels, block_product(): pl.pallas_call(product_kernel, out_shape=jax.ShapeDtypeStruct((rows * ord...  11 us
    unnamed x43, local copies, waits for them, and re-layouts  5.56 us
  transfers between devices with their start and end apart: 29, of which 20 were waited for; matrix products, arithmetic and copies ran while one was open for 2% of the time, Pallas kernels for 0%

profile of v2, /device:TPU:2, one launch (start us, length us, event | category | flops | bytes accessed | tf_op | source)
XLA Modules:
  0.0 215.5 jit_solution(10068374384350927537)
XLA Ops:
  1.3 9.9 %all-to-all-start = ((s32[16,1,1]{2,1,0:T(1,128)}), s32[16,1,1]{2,1,0:T(1,128)S(1)}, u32[]{:S(2)}, u32[]{:S(2)}) async-start(s32[16,1,1]{2,1,0:T(1,128)} %broadcast_in_dim.48), calls=%async_computation | async-start | bytes 16384 | tf_op jit(solution)/shard_map/all_to_all | solution.py:243
  12.6 5.6 %all-to-all-done = s32[16,1,1]{2,1,0:T(1,128)S(1)} async-done(((s32[16,1,1]{2,1,0:T(1,128)}), s32[16,1,1]{2,1,0:T(1,128)S(1)}, u32[]{:S(2)}, u32[]{:S(2)}) %all-to-all-start) | async-done | bytes 96 | tf_op jit(solution)/shard_map/all_to_all | solution.py:243
  25.5 3.2 %collective-permute-start.1 = (bf16[1024,128]{1,0:T(8,128)(2,1)S(1)}, bf16[1024,128]{1,0:T(8,128)(2,1)S(1)}, u32[]{:S(2)}, u32[]{:S(2)}) collective-permute-start(bf16[1024,128]{1,0:T(8,128)(2,1)S(1)} %get-tuple-element.12), channel_id=1, source_target_pairs={{4,0},{5,1},{6,2},{7,3},{0,4},{1,5},{2,6},{3,7},{12,8},{13,9},{14,... | collective-permute-start | bytes 786440 | tf_op jit(solution)/shard_map/ppermute | solution.py:36
  31.6 2.9 %collective-permute-start.4 = (bf16[1024,128]{1,0:T(8,128)(2,1)S(1)}, bf16[1024,128]{1,0:T(8,128)(2,1)S(1)}, u32[]{:S(2)}, u32[]{:S(2)}) collective-permute-start(bf16[1024,128]{1,0:T(8,128)(2,1)S(1)} %collective-permute-done), channel_id=1, source_target_pairs={{2,0},{3,1},{4,2},{5,3},{6,4},{7,5},{0,6},{1,7},{10,8},{11,9},{12,... | collective-permute-start | bytes 786440 | tf_op jit(solution)/shard_map/ppermute | solution.py:36
  37.5 4.7 %collective-permute-done.2 = bf16[1024,128]{1,0:T(8,128)(2,1)S(1)} collective-permute-done((bf16[1024,128]{1,0:T(8,128)(2,1)S(1)}, bf16[1024,128]{1,0:T(8,128)(2,1)S(1)}, u32[]{:S(2)}, u32[]{:S(2)}) %collective-permute-start.2) | collective-permute-done | bytes 262176 | tf_op jit(solution)/shard_map/ppermute | solution.py:36
  48.3 4.2 %shard_map.92 = f32[1024,128]{1,0:T(8,128)} custom-call(s32[64]{0:T(128)S(1)} %reshape.81.columns, bf16[4,16,256,256]{3,2,1,0:T(8,128)(2,1)S(1)} %bitcast.24, bf16[16384,128]{1,0:T(8,128)(2,1)S(1)} %constant_dynamic-update-slice_fusion.gathered), custom_call_target="tpu_custom_call" | custom-call | flops 1073741824 | bytes 8388608 | tf_op jit(solution)/shard_map/pallas_call | solution.py:87
  52.5 5.4 %all-to-all-start.1 = ((f32[16,64,128]{2,1,0:T(8,128)}), f32[16,64,128]{2,1,0:T(8,128)S(1)}, u32[]{:S(2)}, u32[]{:S(2)}) async-start(f32[16,64,128]{2,1,0:T(8,128)} %bitcast.7), calls=%async_computation.1 | async-start | bytes 1048576 | tf_op jit(solution)/shard_map/all_to_all | solution.py:243
  59.3 15.8 %all-to-all-done.1.refs_0_ = f32[16,64,128]{2,1,0:T(8,128)S(1)} async-done(((f32[16,64,128]{2,1,0:T(8,128)}), f32[16,64,128]{2,1,0:T(8,128)S(1)}, u32[]{:S(2)}, u32[]{:S(2)}) %all-to-all-start.1) | async-done | bytes 524320 | tf_op jit(solution)/shard_map/all_to_all | solution.py:243
  77.8 14.4 %all_to_all.36 = bf16[16,64,128]{2,1,0:T(8,128)(2,1)S(1)} all-to-all(bf16[16,64,128]{2,1,0:T(8,128)(2,1)S(1)} %get-tuple-element.14), channel_id=1, replica_groups=mesh['sector'=16,'row'=16] {'sector'}, dimensions={0} | all-to-all | bytes 524288 | tf_op jit(solution)/shard_map/all_to_all | solution.py:243
  92.5 2.5 %collective-permute-start.10 = (bf16[1024,128]{1,0:T(8,128)(2,1)S(1)}, bf16[1024,128]{1,0:T(8,128)(2,1)S(1)}, u32[]{:S(2)}, u32[]{:S(2)}) collective-permute-start(bf16[1024,128]{1,0:T(8,128)(2,1)S(1)} %bitcast.42), channel_id=1, source_target_pairs={{4,0},{5,1},{6,2},{7,3},{0,4},{1,5},{2,6},{3,7},{12,8},{13,9},{14,... | collective-permute-start | bytes 786440 | tf_op jit(solution)/shard_map/ppermute | solution.py:36
  97.1 3.1 %collective-permute-done.9 = bf16[1024,128]{1,0:T(8,128)(2,1)S(1)} collective-permute-done((bf16[1024,128]{1,0:T(8,128)(2,1)S(1)}, bf16[1024,128]{1,0:T(8,128)(2,1)S(1)}, u32[]{:S(2)}, u32[]{:S(2)}) %collective-permute-start.9) | collective-permute-done | bytes 262176 | tf_op jit(solution)/shard_map/ppermute | solution.py:36
  103.2 3.3 %collective-permute-start.15 = (bf16[1024,128]{1,0:T(8,128)(2,1)S(1)}, bf16[1024,128]{1,0:T(8,128)(2,1)S(1)}, u32[]{:S(2)}, u32[]{:S(2)}) collective-permute-start(bf16[1024,128]{1,0:T(8,128)(2,1)S(1)} %collective-permute-done.10), channel_id=1, source_target_pairs={{8,0},{9,1},{10,2},{11,3},{12,4},{13,5},{14,6},{15,7},{0,8},{1,9},... | collective-permute-start | bytes 786440 | tf_op jit(solution)/shard_map/ppermute | solution.py:36
  108.0 2.5 %collective-permute-done.13 = bf16[1024,128]{1,0:T(8,128)(2,1)S(1)} collective-permute-done((bf16[1024,128]{1,0:T(8,128)(2,1)S(1)}, bf16[1024,128]{1,0:T(8,128)(2,1)S(1)}, u32[]{:S(2)}, u32[]{:S(2)}) %collective-permute-start.13) | collective-permute-done | bytes 262176 | tf_op jit(solution)/shard_map/ppermute | solution.py:36
  114.1 3.4 %shard_map.94.refs_0_ = f32[1024,128]{1,0:T(8,128)S(1)} custom-call(s32[64]{0:T(128)S(1)} %reshape.81.columns, bf16[4,16,256,256]{3,2,1,0:T(8,128)(2,1)S(1)} %bitcast.27, bf16[16384,128]{1,0:T(8,128)(2,1)S(1)} %constant_dynamic-update-slice_fusion.10.gathered), custom_call_target="tpu_custom_call" | custom-call | flops 1073741824 | bytes 8388608 | tf_op jit(solution)/shard_map/pallas_call | solution.py:87
  117.5 21.8 %all_to_all.37.refs_0_ = f32[16,64,128]{2,1,0:T(8,128)S(1)} all-to-all(f32[16,64,128]{2,1,0:T(8,128)S(1)} %bitcast.29), channel_id=1, replica_groups=mesh['sector'=16,'row'=16] {'sector'}, dimensions={0} | all-to-all | bytes 1048576 | tf_op jit(solution)/shard_map/all_to_all | solution.py:243
  140.4 14.4 %all_to_all.38 = bf16[16,64,128]{2,1,0:T(8,128)(2,1)S(1)} all-to-all(bf16[16,64,128]{2,1,0:T(8,128)(2,1)S(1)} %get-tuple-element.15), channel_id=1, replica_groups=mesh['sector'=16,'row'=16] {'sector'}, dimensions={0} | all-to-all | bytes 524288 | tf_op jit(solution)/shard_map/all_to_all | solution.py:243
  154.8 2.9 %collective-permute-start.18 = (bf16[1024,128]{1,0:T(8,128)(2,1)S(1)}, bf16[1024,128]{1,0:T(8,128)(2,1)S(1)}, u32[]{:S(2)}, u32[]{:S(2)}) collective-permute-start(bf16[1024,128]{1,0:T(8,128)(2,1)S(1)} %bitcast.35), channel_id=1, source_target_pairs={{8,0},{9,1},{10,2},{11,3},{12,4},{13,5},{14,6},{15,7},{0,8},{1,9},... | collective-permute-start | bytes 786440 | tf_op jit(solution)/shard_map/ppermute | solution.py:36
  157.7 2.5 %collective-permute-start.19 = (bf16[1024,128]{1,0:T(8,128)(2,1)S(1)}, bf16[1024,128]{1,0:T(8,128)(2,1)S(1)}, u32[]{:S(2)}, u32[]{:S(2)}) collective-permute-start(bf16[1024,128]{1,0:T(8,128)(2,1)S(1)} %bitcast.36), channel_id=1, source_target_pairs={{4,0},{5,1},{6,2},{7,3},{0,4},{1,5},{2,6},{3,7},{12,8},{13,9},{14,... | collective-permute-start | bytes 786440 | tf_op jit(solution)/shard_map/ppermute | solution.py:36
  165.1 3.3 %collective-permute-done.19 = bf16[1024,128]{1,0:T(8,128)(2,1)S(1)} collective-permute-done((bf16[1024,128]{1,0:T(8,128)(2,1)S(1)}, bf16[1024,128]{1,0:T(8,128)(2,1)S(1)}, u32[]{:S(2)}, u32[]{:S(2)}) %collective-permute-start.19) | collective-permute-done | bytes 262176 | tf_op jit(solution)/shard_map/ppermute | solution.py:36
  169.1 4.3 %collective-permute-done.20 = bf16[1024,128]{1,0:T(8,128)(2,1)S(1)} collective-permute-done((bf16[1024,128]{1,0:T(8,128)(2,1)S(1)}, bf16[1024,128]{1,0:T(8,128)(2,1)S(1)}, u32[]{:S(2)}, u32[]{:S(2)}) %collective-permute-start.20) | collective-permute-done | bytes 262176 | tf_op jit(solution)/shard_map/ppermute | solution.py:36
  173.6 2.5 %collective-permute-done.22 = bf16[1024,128]{1,0:T(8,128)(2,1)S(1)} collective-permute-done((bf16[1024,128]{1,0:T(8,128)(2,1)S(1)}, bf16[1024,128]{1,0:T(8,128)(2,1)S(1)}, u32[]{:S(2)}, u32[]{:S(2)}) %collective-permute-start.22) | collective-permute-done | bytes 262176 | tf_op jit(solution)/shard_map/ppermute | solution.py:36
  179.5 3.4 %shard_map.96 = bf16[1024,128]{1,0:T(8,128)(2,1)S(1)} custom-call(s32[64]{0:T(128)S(1)} %reshape.81.columns, bf16[4,16,256,256]{3,2,1,0:T(8,128)(2,1)S(1)} %bitcast.28, bf16[16384,128]{1,0:T(8,128)(2,1)S(1)} %constant_dynamic-update-slice_fusion.20.gathered, f32[1024,128]{1,0:T(8,128)S(1)} %shard_map.94.refs_0_), custom_call_target="tpu_custom_call" | custom-call | flops 1073741824 | bytes 8388608 | tf_op jit(solution)/shard_map/pallas_call | solution.py:87
  182.9 16.2 %all_to_all.39.refs_1_ = bf16[16,64,128]{2,1,0:T(8,128)(2,1)S(1)} all-to-all(bf16[16,64,128]{2,1,0:T(8,128)(2,1)S(1)} %bitcast.30), channel_id=1, replica_groups=mesh['sector'=16,'row'=16] {'sector'}, dimensions={0} | all-to-all | bytes 524288 | tf_op jit(solution)/shard_map/all_to_all | solution.py:243
  200.3 14.4 %all_to_all.40 = bf16[16,64,128]{2,1,0:T(8,128)(2,1)S(1)} all-to-all(bf16[16,64,128]{2,1,0:T(8,128)(2,1)S(1)} %shard_map.97), channel_id=1, replica_groups=mesh['sector'=16,'row'=16] {'sector'}, dimensions={0} | all-to-all | bytes 524288 | tf_op jit(solution)/shard_map/all_to_all | solution.py:243
  (110 shorter events, 46.9 us)
Async XLA Ops:
  1.3 17.0 %all-to-all-start = ((s32[16,1,1]{2,1,0:T(1,128)}), s32[16,1,1]{2,1,0:T(1,128)S(1)}, u32[]{:S(2)}, u32[]{:S(2)}) async-start(s32[16,1,1]{2,1,0:T(1,128)} %broadcast_in_dim.48), calls=%async_computation | async-start | bytes 16384 | tf_op jit(solution)/shard_map/all_to_all | solution.py:243
  23.3 8.3 %collective-permute-start = (bf16[1024,128]{1,0:T(8,128)(2,1)S(1)}, bf16[1024,128]{1,0:T(8,128)(2,1)S(1)}, u32[]{:S(2)}, u32[]{:S(2)}) collective-permute-start(bf16[1024,128]{1,0:T(8,128)(2,1)S(1)} %get-tuple-element.12), channel_id=1, source_target_pairs={{8,0},{9,1},{10,2},{11,3},{12,4},{13,5},{14,6},{15,7},{0,8},{1,9},... | collective-permute-start | bytes 786440 | tf_op jit(solution)/shard_map/ppermute | solution.py:36
  25.5 10.6 %collective-permute-start.1 = (bf16[1024,128]{1,0:T(8,128)(2,1)S(1)}, bf16[1024,128]{1,0:T(8,128)(2,1)S(1)}, u32[]{:S(2)}, u32[]{:S(2)}) collective-permute-start(bf16[1024,128]{1,0:T(8,128)(2,1)S(1)} %get-tuple-element.12), channel_id=1, source_target_pairs={{4,0},{5,1},{6,2},{7,3},{0,4},{1,5},{2,6},{3,7},{12,8},{13,9},{14,... | collective-permute-start | bytes 786440 | tf_op jit(solution)/shard_map/ppermute | solution.py:36
  28.7 13.5 %collective-permute-start.2 = (bf16[1024,128]{1,0:T(8,128)(2,1)S(1)}, bf16[1024,128]{1,0:T(8,128)(2,1)S(1)}, u32[]{:S(2)}, u32[]{:S(2)}) collective-permute-start(bf16[1024,128]{1,0:T(8,128)(2,1)S(1)} %get-tuple-element.12), channel_id=1, source_target_pairs={{2,0},{3,1},{4,2},{5,3},{6,4},{7,5},{0,6},{1,7},{10,8},{11,9},{12,... | collective-permute-start | bytes 786440 | tf_op jit(solution)/shard_map/ppermute | solution.py:36
  30.6 11.9 %collective-permute-start.3 = (bf16[1024,128]{1,0:T(8,128)(2,1)S(1)}, bf16[1024,128]{1,0:T(8,128)(2,1)S(1)}, u32[]{:S(2)}, u32[]{:S(2)}) collective-permute-start(bf16[1024,128]{1,0:T(8,128)(2,1)S(1)} %get-tuple-element.12), channel_id=1, source_target_pairs={{6,0},{7,1},{0,2},{1,3},{2,4},{3,5},{4,6},{5,7},{14,8},{15,9},{8,1... | collective-permute-start | bytes 786440 | tf_op jit(solution)/shard_map/ppermute | solution.py:36
  31.6 13.4 %collective-permute-start.4 = (bf16[1024,128]{1,0:T(8,128)(2,1)S(1)}, bf16[1024,128]{1,0:T(8,128)(2,1)S(1)}, u32[]{:S(2)}, u32[]{:S(2)}) collective-permute-start(bf16[1024,128]{1,0:T(8,128)(2,1)S(1)} %collective-permute-done), channel_id=1, source_target_pairs={{2,0},{3,1},{4,2},{5,3},{6,4},{7,5},{0,6},{1,7},{10,8},{11,9},{12,... | collective-permute-start | bytes 786440 | tf_op jit(solution)/shard_map/ppermute | solution.py:36
  34.6 10.7 %collective-permute-start.5 = (bf16[1024,128]{1,0:T(8,128)(2,1)S(1)}, bf16[1024,128]{1,0:T(8,128)(2,1)S(1)}, u32[]{:S(2)}, u32[]{:S(2)}) collective-permute-start(bf16[1024,128]{1,0:T(8,128)(2,1)S(1)} %collective-permute-done), channel_id=1, source_target_pairs={{6,0},{7,1},{0,2},{1,3},{2,4},{3,5},{4,6},{5,7},{14,8},{15,9},{8,1... | collective-permute-start | bytes 786440 | tf_op jit(solution)/shard_map/ppermute | solution.py:36
  36.1 9.2 %collective-permute-start.6 = (bf16[1024,128]{1,0:T(8,128)(2,1)S(1)}, bf16[1024,128]{1,0:T(8,128)(2,1)S(1)}, u32[]{:S(2)}, u32[]{:S(2)}) collective-permute-start(bf16[1024,128]{1,0:T(8,128)(2,1)S(1)} %collective-permute-done.1), channel_id=1, source_target_pairs={{8,0},{9,1},{10,2},{11,3},{12,4},{13,5},{14,6},{15,7},{0,8},{1,9},... | collective-permute-start | bytes 786440 | tf_op jit(solution)/shard_map/ppermute | solution.py:36
  52.5 22.6 %all-to-all-start.1 = ((f32[16,64,128]{2,1,0:T(8,128)}), f32[16,64,128]{2,1,0:T(8,128)S(1)}, u32[]{:S(2)}, u32[]{:S(2)}) async-start(f32[16,64,128]{2,1,0:T(8,128)} %bitcast.7), calls=%async_computation.1 | async-start | bytes 1048576 | tf_op jit(solution)/shard_map/all_to_all | solution.py:243
  92.3 7.9 %collective-permute-start.9 = (bf16[1024,128]{1,0:T(8,128)(2,1)S(1)}, bf16[1024,128]{1,0:T(8,128)(2,1)S(1)}, u32[]{:S(2)}, u32[]{:S(2)}) collective-permute-start(bf16[1024,128]{1,0:T(8,128)(2,1)S(1)} %bitcast.41), channel_id=1, source_target_pairs={{8,0},{9,1},{10,2},{11,3},{12,4},{13,5},{14,6},{15,7},{0,8},{1,9},... | collective-permute-start | bytes 786440 | tf_op jit(solution)/shard_map/ppermute | solution.py:36
  92.5 10.7 %collective-permute-start.10 = (bf16[1024,128]{1,0:T(8,128)(2,1)S(1)}, bf16[1024,128]{1,0:T(8,128)(2,1)S(1)}, u32[]{:S(2)}, u32[]{:S(2)}) collective-permute-start(bf16[1024,128]{1,0:T(8,128)(2,1)S(1)} %bitcast.42), channel_id=1, source_target_pairs={{4,0},{5,1},{6,2},{7,3},{0,4},{1,5},{2,6},{3,7},{12,8},{13,9},{14,... | collective-permute-start | bytes 786440 | tf_op jit(solution)/shard_map/ppermute | solution.py:36
  95.0 12.7 %collective-permute-start.11 = (bf16[1024,128]{1,0:T(8,128)(2,1)S(1)}, bf16[1024,128]{1,0:T(8,128)(2,1)S(1)}, u32[]{:S(2)}, u32[]{:S(2)}) collective-permute-start(bf16[1024,128]{1,0:T(8,128)(2,1)S(1)} %bitcast.43), channel_id=1, source_target_pairs={{2,0},{3,1},{4,2},{5,3},{6,4},{7,5},{0,6},{1,7},{10,8},{11,9},{12,... | collective-permute-start | bytes 786440 | tf_op jit(solution)/shard_map/ppermute | solution.py:36
  96.2 11.8 %collective-permute-start.12 = (bf16[1024,128]{1,0:T(8,128)(2,1)S(1)}, bf16[1024,128]{1,0:T(8,128)(2,1)S(1)}, u32[]{:S(2)}, u32[]{:S(2)}) collective-permute-start(bf16[1024,128]{1,0:T(8,128)(2,1)S(1)} %bitcast.44), channel_id=1, source_target_pairs={{6,0},{7,1},{0,2},{1,3},{2,4},{3,5},{4,6},{5,7},{14,8},{15,9},{8,1... | collective-permute-start | bytes 786440 | tf_op jit(solution)/shard_map/ppermute | solution.py:36
  100.2 10.4 %collective-permute-start.13 = (bf16[1024,128]{1,0:T(8,128)(2,1)S(1)}, bf16[1024,128]{1,0:T(8,128)(2,1)S(1)}, u32[]{:S(2)}, u32[]{:S(2)}) collective-permute-start(bf16[1024,128]{1,0:T(8,128)(2,1)S(1)} %collective-permute-done.9), channel_id=1, source_target_pairs={{2,0},{3,1},{4,2},{5,3},{6,4},{7,5},{0,6},{1,7},{10,8},{11,9},{12,... | collective-permute-start | bytes 786440 | tf_op jit(solution)/shard_map/ppermute | solution.py:36
  102.5 8.4 %collective-permute-start.14 = (bf16[1024,128]{1,0:T(8,128)(2,1)S(1)}, bf16[1024,128]{1,0:T(8,128)(2,1)S(1)}, u32[]{:S(2)}, u32[]{:S(2)}) collective-permute-start(bf16[1024,128]{1,0:T(8,128)(2,1)S(1)} %collective-permute-done.9), channel_id=1, source_target_pairs={{6,0},{7,1},{0,2},{1,3},{2,4},{3,5},{4,6},{5,7},{14,8},{15,9},{8,1... | collective-permute-start | bytes 786440 | tf_op jit(solution)/shard_map/ppermute | solution.py:36
  103.2 7.9 %collective-permute-start.15 = (bf16[1024,128]{1,0:T(8,128)(2,1)S(1)}, bf16[1024,128]{1,0:T(8,128)(2,1)S(1)}, u32[]{:S(2)}, u32[]{:S(2)}) collective-permute-start(bf16[1024,128]{1,0:T(8,128)(2,1)S(1)} %collective-permute-done.10), channel_id=1, source_target_pairs={{8,0},{9,1},{10,2},{11,3},{12,4},{13,5},{14,6},{15,7},{0,8},{1,9},... | collective-permute-start | bytes 786440 | tf_op jit(solution)/shard_map/ppermute | solution.py:36
  107.8 3.7 %collective-permute-start.16 = (bf16[4096,128]{1,0:T(8,128)(2,1)S(1)}, bf16[4096,128]{1,0:T(8,128)(2,1)S(1)}, u32[]{:S(2)}, u32[]{:S(2)}) collective-permute-start(bf16[4096,128]{1,0:T(8,128)(2,1)S(1)} %pad_maximum_fusion.2), channel_id=1, source_target_pairs={{1,0},{0,1},{3,2},{2,3},{5,4},{4,5},{7,6},{6,7},{9,8},{8,9},{11,10... | collective-permute-start | bytes 3145736 | tf_op jit(solution)/shard_map/ppermute | solution.py:36
  154.8 7.9 %collective-permute-start.18 = (bf16[1024,128]{1,0:T(8,128)(2,1)S(1)}, bf16[1024,128]{1,0:T(8,128)(2,1)S(1)}, u32[]{:S(2)}, u32[]{:S(2)}) collective-permute-start(bf16[1024,128]{1,0:T(8,128)(2,1)S(1)} %bitcast.35), channel_id=1, source_target_pairs={{8,0},{9,1},{10,2},{11,3},{12,4},{13,5},{14,6},{15,7},{0,8},{1,9},... | collective-permute-start | bytes 786440 | tf_op jit(solution)/shard_map/ppermute | solution.py:36
  157.7 10.7 %collective-permute-start.19 = (bf16[1024,128]{1,0:T(8,128)(2,1)S(1)}, bf16[1024,128]{1,0:T(8,128)(2,1)S(1)}, u32[]{:S(2)}, u32[]{:S(2)}) collective-permute-start(bf16[1024,128]{1,0:T(8,128)(2,1)S(1)} %bitcast.36), channel_id=1, source_target_pairs={{4,0},{5,1},{6,2},{7,3},{0,4},{1,5},{2,6},{3,7},{12,8},{13,9},{14,... | collective-permute-start | bytes 786440 | tf_op jit(solution)/shard_map/ppermute | solution.py:36
  160.2 13.1 %collective-permute-start.20 = (bf16[1024,128]{1,0:T(8,128)(2,1)S(1)}, bf16[1024,128]{1,0:T(8,128)(2,1)S(1)}, u32[]{:S(2)}, u32[]{:S(2)}) collective-permute-start(bf16[1024,128]{1,0:T(8,128)(2,1)S(1)} %bitcast.37), channel_id=1, source_target_pairs={{2,0},{3,1},{4,2},{5,3},{6,4},{7,5},{0,6},{1,7},{10,8},{11,9},{12,... | collective-permute-start | bytes 786440 | tf_op jit(solution)/shard_map/ppermute | solution.py:36
  161.4 12.2 %collective-permute-start.21 = (bf16[1024,128]{1,0:T(8,128)(2,1)S(1)}, bf16[1024,128]{1,0:T(8,128)(2,1)S(1)}, u32[]{:S(2)}, u32[]{:S(2)}) collective-permute-start(bf16[1024,128]{1,0:T(8,128)(2,1)S(1)} %bitcast.38), channel_id=1, source_target_pairs={{6,0},{7,1},{0,2},{1,3},{2,4},{3,5},{4,6},{5,7},{14,8},{15,9},{8,1... | collective-permute-start | bytes 786440 | tf_op jit(solution)/shard_map/ppermute | solution.py:36
  162.7 13.4 %collective-permute-start.22 = (bf16[1024,128]{1,0:T(8,128)(2,1)S(1)}, bf16[1024,128]{1,0:T(8,128)(2,1)S(1)}, u32[]{:S(2)}, u32[]{:S(2)}) collective-permute-start(bf16[1024,128]{1,0:T(8,128)(2,1)S(1)} %collective-permute-done.18), channel_id=1, source_target_pairs={{2,0},{3,1},{4,2},{5,3},{6,4},{7,5},{0,6},{1,7},{10,8},{11,9},{12,... | collective-permute-start | bytes 786440 | tf_op jit(solution)/shard_map/ppermute | solution.py:36
  165.1 11.4 %collective-permute-start.23 = (bf16[1024,128]{1,0:T(8,128)(2,1)S(1)}, bf16[1024,128]{1,0:T(8,128)(2,1)S(1)}, u32[]{:S(2)}, u32[]{:S(2)}) collective-permute-start(bf16[1024,128]{1,0:T(8,128)(2,1)S(1)} %collective-permute-done.18), channel_id=1, source_target_pairs={{6,0},{7,1},{0,2},{1,3},{2,4},{3,5},{4,6},{5,7},{14,8},{15,9},{8,1... | collective-permute-start | bytes 786440 | tf_op jit(solution)/shard_map/ppermute | solution.py:36
  168.4 8.1 %collective-permute-start.24 = (bf16[1024,128]{1,0:T(8,128)(2,1)S(1)}, bf16[1024,128]{1,0:T(8,128)(2,1)S(1)}, u32[]{:S(2)}, u32[]{:S(2)}) collective-permute-start(bf16[1024,128]{1,0:T(8,128)(2,1)S(1)} %collective-permute-done.19), channel_id=1, source_target_pairs={{8,0},{9,1},{10,2},{11,3},{12,4},{13,5},{14,6},{15,7},{0,8},{1,9},... | collective-permute-start | bytes 786440 | tf_op jit(solution)/shard_map/ppermute | solution.py:36
  (12 other events, 78.8 us)

commit v3 on v2

--- a/solution.py
+++ b/solution.py
@@ -31,7 +31,7 @@
 SHIFTS = ((0, 0), (1, 0), (0, 2), (0, 1), (0, 3), (1, 1), (1, 3), (1, 2))
 
 
-def gather_pieces(own):
+def gather_pieces(own, riders=()):
     def fetch(block, *shift):
         return lax.ppermute(block, "row", row_peers(*shift))
 
@@ -40,10 +40,10 @@
     relayed = [fetch(across, 0, 1, 0), fetch(across, 0, 3, 0), fetch(opposite, 1, 0, 0)]
     direct = [own, across, opposite, above, below]
     order = direct + relayed
-    swapped = [
-        fetch(jnp.concatenate(part, axis=0), 0, 0, 1) for part in (order[:4], order[4:])
-    ]
-    return jnp.concatenate(direct + relayed + swapped, axis=0)
+    early, late = (jnp.concatenate(part, axis=0) for part in (order[:4], order[4:]))
+    early, riders = lax.optimization_barrier((early, riders))
+    swapped = [fetch(part, 0, 0, 1) for part in (early, late)]
+    return jnp.concatenate(order + swapped, axis=0), riders
 
 
 def relative_columns(block_columns, blocks_per_device):
@@ -155,16 +155,21 @@
 
 
 def coefficient_kernel(
-    classes, own, cosine, sine, mistuning, base, ratio, cosine_load, sine_load, rounded, table
+    classes, own, cosine, sine, diagonals, couplings, loads, more_loads, rounded, table, held, arrived
 ):
+    copies = [
+        pltpu.make_async_copy(source, held.at[side], arrived.at[side])
+        for side, source in enumerate((loads, more_loads))
+    ]
+    for copy in copies:
+        copy.start()
     sectors = table.shape[1]
-    stiffness = base[...]
-    coupling = ratio[...] * stiffness
-    diagonal = [stiffness * (1.0 + mistuning[classes[s]]) for s in range(sectors)]
+    coupling = couplings[...]
+    diagonal = [diagonals[classes[s]] for s in range(sectors)]
     factors, reduced = reduce_coefficients([-coupling] * sectors, diagonal, [-coupling] * sectors)
     gains = [
         apply_reduction(
-            factors, reduced, [jnp.full(stiffness.shape, wave[s], jnp.float32) for s in range(sectors)]
+            factors, reduced, [jnp.full(coupling.shape, wave[s], jnp.float32) for s in range(sectors)]
         )
         for wave in (cosine, sine)
     ]
@@ -173,13 +178,15 @@
     for kind, cells in enumerate(kinds):
         for s in range(sectors):
             table[kind, s] = cells[s]
-    groups, lanes = stiffness.shape
+    groups, lanes = coupling.shape
     cosine_gain, sine_gain = table[GAINS, own[0]].T, table[GAINS + 1, own[0]].T
+    for copy in copies:
+        copy.wait()
     for group in range(groups):
         rows = pl.ds(group * lanes, lanes)
         rounded[rows, :] = (
-            cosine_gain[:, group : group + 1] * cosine_load[rows, :]
-            + sine_gain[:, group : group + 1] * sine_load[rows, :]
+            cosine_gain[:, group : group + 1] * held[0, rows, :]
+            + sine_gain[:, group : group + 1] * held[1, rows, :]
         ).astype(rounded.dtype)
 
 
@@ -252,23 +259,29 @@
 
     lanes = 128
     groups = local_rows // lanes
+    base = base_stiffness.reshape(groups, lanes)
+    coupling = coupling_ratio.reshape(groups, lanes) * base
+    diagonals = base * (1.0 + mistuning.reshape(-1, groups, lanes))
     rounded, table = pl.pallas_call(
         coefficient_kernel,
         out_shape=(
             jax.ShapeDtypeStruct((local_rows, load_cases), jnp.bfloat16),
             jax.ShapeDtypeStruct((KINDS, sectors, groups, lanes), jnp.float32),
         ),
-        in_specs=[smem] * 4 + [vmem] * 5,
+        in_specs=[smem] * 4 + [vmem] * 2 + [pl.BlockSpec(memory_space=pl.ANY)] * 2,
         out_specs=(vmem, vmem),
-        compiler_params=pltpu.CompilerParams(vmem_limit_bytes=16 * 1024 * 1024),
+        scratch_shapes=[
+            pltpu.VMEM((2, local_rows, load_cases), jnp.float32),
+            pltpu.SemaphoreType.DMA((2,)),
+        ],
+        compiler_params=pltpu.CompilerParams(vmem_limit_bytes=58 * 1024 * 1024),
     )(
         all_classes,
         sector_id[None],
         cosine,
         sine,
-        mistuning.reshape(-1, groups, lanes),
-        base_stiffness.reshape(groups, lanes),
-        coupling_ratio.reshape(groups, lanes),
+        diagonals,
+        coupling,
         cosine_load,
         sine_load,
     )
@@ -285,7 +298,7 @@
     products = []
     for iteration in range(1, ITERS):
         last = iteration == ITERS - 1
-        gathered = gather_pieces(rounded)
+        gathered, (table, current) = gather_pieces(rounded, (table, current))
         if last:
             change = block_product(block_values[0], columns, gathered, product)
             products.append(swap(change.reshape(slice_shape)))

time: 217 us -> 216 us (level)
  blocking collectives: 81.3 us -> 106 us
  waiting for transfers between devices: 56.3 us -> 34.1 us
  starting transfers between devices: 48.6 us -> 41.1 us
  other arithmetic: 2.75 us -> 8.16 us
    all_to_all x5 -> x6, blocking collectives: 81.3 us -> 106 us  [swap(): return lax.all_to_all(cells, 'sector', 0, 0, tiled=True)]
    all_to_all x2 -> x1, waiting for transfers between devices: 21.4 us -> 0.9 us  [swap(): return lax.all_to_all(cells, 'sector', 0, 0, tiled=True)]
    all_to_all x2 -> x1, starting transfers between devices: 15.4 us -> 9.94 us  [swap(): return lax.all_to_all(cells, 'sector', 0, 0, tiled=True)]
    mul x0 -> x2, other arithmetic: none -> 2.58 us  [the longest x1 1.29 us: shards(): diagonals = base * (1.0 + mistuning.reshape(-1, groups, lanes))]
    unnamed x43 -> x36, local copies, waits for them, and re-layouts: 5.56 us -> 3.48 us
  transfers between devices with their start and end apart: 29 -> 28, of which waited for: 20 -> 19; matrix products, arithmetic and copies ran while one was open for 2% -> 6% of each run, Pallas kernels for 0% -> 0%
where the time goes in v3:
time: 216 us; the launch traced here: 215 us
  blocking collectives  106 us (49%)
  starting transfers between devices  41.1 us (19%)
  waiting for transfers between devices  34.1 us (16%)
  Pallas kernels  16.7 us (8%)
  other arithmetic  8.16 us (4%)
  local copies, waits for them, and re-layouts  7.18 us (3%)
    all_to_all x6, blocking collectives, swap(): return lax.all_to_all(cells, 'sector', 0, 0, tiled=True)  106 us
    ppermute x27, waiting for transfers between devices, fetch(): return lax.ppermute(block, 'row', row_peers(*shift))  33.2 us
    ppermute x27, starting transfers between devices, fetch(): return lax.ppermute(block, 'row', row_peers(*shift))  31.2 us
    pallas_call x3, Pallas kernels, block_product(): pl.pallas_call(product_kernel, out_shape=jax.ShapeDtypeStruct((rows * ord...  10.3 us
    all_to_all x1, starting transfers between devices, swap(): return lax.all_to_all(cells, 'sector', 0, 0, tiled=True)  9.94 us
  transfers between devices with their start and end apart: 28, of which 19 were waited for; matrix products, arithmetic and copies ran while one was open for 6% of the time, Pallas kernels for 0%

profile of v3, /device:TPU:2, one launch (start us, length us, event | category | flops | bytes accessed | tf_op | source)
XLA Modules:
  0.0 214.6 jit_solution(7317701603919077490)
XLA Ops:
  1.3 9.9 %all-to-all-start = ((s32[16,1,1]{2,1,0:T(1,128)}), s32[16,1,1]{2,1,0:T(1,128)S(1)}, u32[]{:S(2)}, u32[]{:S(2)}) async-start(s32[16,1,1]{2,1,0:T(1,128)} %broadcast_in_dim.48), calls=%async_computation | async-start | bytes 16384 | tf_op jit(solution)/shard_map/all_to_all | solution.py:250
  19.2 3.1 %shard_map.91 = (bf16[1024,128]{1,0:T(8,128)(2,1)}, f32[11,16,8,128]{3,2,1,0:T(8,128)}) custom-call(s32[16]{0:T(128)} %reduce.classes, s32[1]{0:T(128)} %bitcast.2.own, f32[16]{0:T(128)} %get-tuple-element.38.cosine, f32[16]{0:T(128)} %get-tuple-element.37.sine, f32[4,8,128]{2,1,0:T(8,128)} %bitcast_multiply_fusion.diagonals, ...), custom_call_target="tpu_custom_call" | custom-call | tf_op jit(solution)/shard_map/pallas_call | solution.py:265
  22.3 3.1 %collective-permute-start.2 = (bf16[1024,128]{1,0:T(8,128)(2,1)}, bf16[1024,128]{1,0:T(8,128)(2,1)S(1)}, u32[]{:S(2)}, u32[]{:S(2)}) collective-permute-start(bf16[1024,128]{1,0:T(8,128)(2,1)} %get-tuple-element.20), channel_id=1, source_target_pairs={{2,0},{3,1},{4,2},{5,3},{6,4},{7,5},{0,6},{1,7},{10,8},{11,9},{12,... | collective-permute-start | bytes 786440 | tf_op jit(solution)/shard_map/ppermute | solution.py:36
  32.0 2.1 collective-permute-done
  36.2 2.3 %collective-permute-start.6 = (bf16[1024,128]{1,0:T(8,128)(2,1)S(1)}, bf16[1024,128]{1,0:T(8,128)(2,1)S(1)}, u32[]{:S(2)}, u32[]{:S(2)}) collective-permute-start(bf16[1024,128]{1,0:T(8,128)(2,1)S(1)} %collective-permute-done.1), channel_id=1, source_target_pairs={{8,0},{9,1},{10,2},{11,3},{12,4},{13,5},{14,6},{15,7},{0,8},{1,9},... | collective-permute-start | bytes 786440 | tf_op jit(solution)/shard_map/ppermute | solution.py:36
  41.4 3.3 %collective-permute-done.5 = bf16[1024,128]{1,0:T(8,128)(2,1)S(1)} collective-permute-done((bf16[1024,128]{1,0:T(8,128)(2,1)S(1)}, bf16[1024,128]{1,0:T(8,128)(2,1)S(1)}, u32[]{:S(2)}, u32[]{:S(2)}) %collective-permute-start.5) | collective-permute-done | bytes 262176 | tf_op jit(solution)/shard_map/ppermute | solution.py:36
  45.3 2.3 %collective-permute-done.8 = bf16[4096,128]{1,0:T(8,128)(2,1)S(1)} collective-permute-done((bf16[4096,128]{1,0:T(8,128)(2,1)S(1)}, bf16[4096,128]{1,0:T(8,128)(2,1)S(1)}, u32[]{:S(2)}, u32[]{:S(2)}) %collective-permute-start.8) | collective-permute-done | bytes 1048608 | tf_op jit(solution)/shard_map/ppermute | solution.py:36
  47.8 3.4 %shard_map.92 = f32[1024,128]{1,0:T(8,128)S(1)} custom-call(s32[64]{0:T(128)S(1)} %reshape.78.columns, bf16[4,16,256,256]{3,2,1,0:T(8,128)(2,1)S(1)} %bitcast.28, bf16[16384,128]{1,0:T(8,128)(2,1)S(1)} %constant_dynamic-update-slice_fusion.gathered), custom_call_target="tpu_custom_call" | custom-call | flops 1073741824 | bytes 8388608 | tf_op jit(solution)/shard_map/pallas_call | solution.py:87
  51.2 24.5 %all_to_all.36.refs_0_ = f32[16,64,128]{2,1,0:T(8,128)S(1)} all-to-all(f32[16,64,128]{2,1,0:T(8,128)S(1)} %bitcast.32), channel_id=1, replica_groups=mesh['sector'=16,'row'=16] {'sector'}, dimensions={0} | all-to-all | bytes 1048576 | tf_op jit(solution)/shard_map/all_to_all | solution.py:250
  76.8 14.4 %all_to_all.37 = bf16[16,64,128]{2,1,0:T(8,128)(2,1)S(1)} all-to-all(bf16[16,64,128]{2,1,0:T(8,128)(2,1)S(1)} %get-tuple-element.25), channel_id=1, replica_groups=mesh['sector'=16,'row'=16] {'sector'}, dimensions={0} | all-to-all | bytes 524288 | tf_op jit(solution)/shard_map/all_to_all | solution.py:250
  95.2 2.2 %collective-permute-start.11 = (bf16[1024,128]{1,0:T(8,128)(2,1)S(1)}, bf16[1024,128]{1,0:T(8,128)(2,1)S(1)}, u32[]{:S(2)}, u32[]{:S(2)}) collective-permute-start(bf16[1024,128]{1,0:T(8,128)(2,1)S(1)} %bitcast.42), channel_id=1, source_target_pairs={{2,0},{3,1},{4,2},{5,3},{6,4},{7,5},{0,6},{1,7},{10,8},{11,9},{12,... | collective-permute-start | bytes 786440 | tf_op jit(solution)/shard_map/ppermute | solution.py:36
  101.1 3.0 %collective-permute-done.10 = bf16[1024,128]{1,0:T(8,128)(2,1)S(1)} collective-permute-done((bf16[1024,128]{1,0:T(8,128)(2,1)S(1)}, bf16[1024,128]{1,0:T(8,128)(2,1)S(1)}, u32[]{:S(2)}, u32[]{:S(2)}) %collective-permute-start.10) | collective-permute-done | bytes 262176 | tf_op jit(solution)/shard_map/ppermute | solution.py:36
  105.5 2.5 %collective-permute-done.11 = bf16[1024,128]{1,0:T(8,128)(2,1)S(1)} collective-permute-done((bf16[1024,128]{1,0:T(8,128)(2,1)S(1)}, bf16[1024,128]{1,0:T(8,128)(2,1)S(1)}, u32[]{:S(2)}, u32[]{:S(2)}) %collective-permute-start.11) | collective-permute-done | bytes 262176 | tf_op jit(solution)/shard_map/ppermute | solution.py:36
  113.1 2.3 %collective-permute-done.17 = bf16[4096,128]{1,0:T(8,128)(2,1)S(1)} collective-permute-done((bf16[4096,128]{1,0:T(8,128)(2,1)S(1)}, bf16[4096,128]{1,0:T(8,128)(2,1)S(1)}, u32[]{:S(2)}, u32[]{:S(2)}) %collective-permute-start.17) | collective-permute-done | bytes 1048608 | tf_op jit(solution)/shard_map/ppermute | solution.py:36
  115.5 3.4 %shard_map.94.refs_0_ = f32[1024,128]{1,0:T(8,128)S(1)} custom-call(s32[64]{0:T(128)S(1)} %reshape.78.columns, bf16[4,16,256,256]{3,2,1,0:T(8,128)(2,1)S(1)} %bitcast.29, bf16[16384,128]{1,0:T(8,128)(2,1)S(1)} %constant_dynamic-update-slice_fusion.10.gathered), custom_call_target="tpu_custom_call" | custom-call | flops 1073741824 | bytes 8388608 | tf_op jit(solution)/shard_map/pallas_call | solution.py:87
  118.9 21.7 %all_to_all.38.refs_0_ = f32[16,64,128]{2,1,0:T(8,128)S(1)} all-to-all(f32[16,64,128]{2,1,0:T(8,128)S(1)} %bitcast.31), channel_id=1, replica_groups=mesh['sector'=16,'row'=16] {'sector'}, dimensions={0} | all-to-all | bytes 1048576 | tf_op jit(solution)/shard_map/all_to_all | solution.py:250
  141.7 14.4 %all_to_all.39 = bf16[16,64,128]{2,1,0:T(8,128)(2,1)S(1)} all-to-all(bf16[16,64,128]{2,1,0:T(8,128)(2,1)S(1)} %get-tuple-element.30), channel_id=1, replica_groups=mesh['sector'=16,'row'=16] {'sector'}, dimensions={0} | all-to-all | bytes 524288 | tf_op jit(solution)/shard_map/all_to_all | solution.py:250
  161.0 3.0 %collective-permute-done.18 = bf16[1024,128]{1,0:T(8,128)(2,1)S(1)} collective-permute-done((bf16[1024,128]{1,0:T(8,128)(2,1)S(1)}, bf16[1024,128]{1,0:T(8,128)(2,1)S(1)}, u32[]{:S(2)}, u32[]{:S(2)}) %collective-permute-start.18) | collective-permute-done | bytes 262176 | tf_op jit(solution)/shard_map/ppermute | solution.py:36
  167.5 2.8 %collective-permute-start.24 = (bf16[1024,128]{1,0:T(8,128)(2,1)S(1)}, bf16[1024,128]{1,0:T(8,128)(2,1)S(1)}, u32[]{:S(2)}, u32[]{:S(2)}) collective-permute-start(bf16[1024,128]{1,0:T(8,128)(2,1)S(1)} %collective-permute-done.19), channel_id=1, source_target_pairs={{8,0},{9,1},{10,2},{11,3},{12,4},{13,5},{14,6},{15,7},{0,8},{1,9},... | collective-permute-start | bytes 786440 | tf_op jit(solution)/shard_map/ppermute | solution.py:36
  171.8 2.5 %collective-permute-done.22 = bf16[1024,128]{1,0:T(8,128)(2,1)S(1)} collective-permute-done((bf16[1024,128]{1,0:T(8,128)(2,1)S(1)}, bf16[1024,128]{1,0:T(8,128)(2,1)S(1)}, u32[]{:S(2)}, u32[]{:S(2)}) %collective-permute-start.22) | collective-permute-done | bytes 262176 | tf_op jit(solution)/shard_map/ppermute | solution.py:36
  176.1 2.3 %collective-permute-done.26 = bf16[4096,128]{1,0:T(8,128)(2,1)S(1)} collective-permute-done((bf16[4096,128]{1,0:T(8,128)(2,1)S(1)}, bf16[4096,128]{1,0:T(8,128)(2,1)S(1)}, u32[]{:S(2)}, u32[]{:S(2)}) %collective-permute-start.26) | collective-permute-done | bytes 1048608 | tf_op jit(solution)/shard_map/ppermute | solution.py:36
  178.5 3.4 %shard_map.96 = bf16[1024,128]{1,0:T(8,128)(2,1)S(1)} custom-call(s32[64]{0:T(128)S(1)} %reshape.78.columns, bf16[4,16,256,256]{3,2,1,0:T(8,128)(2,1)S(1)} %bitcast.30, bf16[16384,128]{1,0:T(8,128)(2,1)S(1)} %constant_dynamic-update-slice_fusion.20.gathered, f32[1024,128]{1,0:T(8,128)S(1)} %shard_map.94.refs_0_), custom_call_target="tpu_custom_call" | custom-call | flops 1073741824 | bytes 8388608 | tf_op jit(solution)/shard_map/pallas_call | solution.py:87
  181.9 16.3 %all_to_all.40.refs_1_ = bf16[16,64,128]{2,1,0:T(8,128)(2,1)S(1)} all-to-all(bf16[16,64,128]{2,1,0:T(8,128)(2,1)S(1)} %bitcast.33), channel_id=1, replica_groups=mesh['sector'=16,'row'=16] {'sector'}, dimensions={0} | all-to-all | bytes 524288 | tf_op jit(solution)/shard_map/all_to_all | solution.py:250
  199.4 14.4 %all_to_all.41 = bf16[16,64,128]{2,1,0:T(8,128)(2,1)S(1)} all-to-all(bf16[16,64,128]{2,1,0:T(8,128)(2,1)S(1)} %shard_map.97), channel_id=1, replica_groups=mesh['sector'=16,'row'=16] {'sector'}, dimensions={0} | all-to-all | bytes 524288 | tf_op jit(solution)/shard_map/all_to_all | solution.py:250
  (105 shorter events, 50.3 us)
Async XLA Ops:
  1.3 17.0 %all-to-all-start = ((s32[16,1,1]{2,1,0:T(1,128)}), s32[16,1,1]{2,1,0:T(1,128)S(1)}, u32[]{:S(2)}, u32[]{:S(2)}) async-start(s32[16,1,1]{2,1,0:T(1,128)} %broadcast_in_dim.48), calls=%async_computation | async-start | bytes 16384 | tf_op jit(solution)/shard_map/all_to_all | solution.py:250
  22.3 16.2 %collective-permute-start.2 = (bf16[1024,128]{1,0:T(8,128)(2,1)}, bf16[1024,128]{1,0:T(8,128)(2,1)S(1)}, u32[]{:S(2)}, u32[]{:S(2)}) collective-permute-start(bf16[1024,128]{1,0:T(8,128)(2,1)} %get-tuple-element.20), channel_id=1, source_target_pairs={{2,0},{3,1},{4,2},{5,3},{6,4},{7,5},{0,6},{1,7},{10,8},{11,9},{12,... | collective-permute-start | bytes 786440 | tf_op jit(solution)/shard_map/ppermute | solution.py:36
  25.4 10.8 %collective-permute-start.1 = (bf16[1024,128]{1,0:T(8,128)(2,1)}, bf16[1024,128]{1,0:T(8,128)(2,1)S(1)}, u32[]{:S(2)}, u32[]{:S(2)}) collective-permute-start(bf16[1024,128]{1,0:T(8,128)(2,1)} %get-tuple-element.20), channel_id=1, source_target_pairs={{4,0},{5,1},{6,2},{7,3},{0,4},{1,5},{2,6},{3,7},{12,8},{13,9},{14,... | collective-permute-start | bytes 786440 | tf_op jit(solution)/shard_map/ppermute | solution.py:36
  26.0 8.1 %collective-permute-start = (bf16[1024,128]{1,0:T(8,128)(2,1)}, bf16[1024,128]{1,0:T(8,128)(2,1)S(1)}, u32[]{:S(2)}, u32[]{:S(2)}) collective-permute-start(bf16[1024,128]{1,0:T(8,128)(2,1)} %get-tuple-element.20), channel_id=1, source_target_pairs={{8,0},{9,1},{10,2},{11,3},{12,4},{13,5},{14,6},{15,7},{0,8},{1,9},... | collective-permute-start | bytes 786440 | tf_op jit(solution)/shard_map/ppermute | solution.py:36
  29.2 12.2 %collective-permute-start.3 = (bf16[1024,128]{1,0:T(8,128)(2,1)}, bf16[1024,128]{1,0:T(8,128)(2,1)S(1)}, u32[]{:S(2)}, u32[]{:S(2)}) collective-permute-start(bf16[1024,128]{1,0:T(8,128)(2,1)} %get-tuple-element.20), channel_id=1, source_target_pairs={{6,0},{7,1},{0,2},{1,3},{2,4},{3,5},{4,6},{5,7},{14,8},{15,9},{8,1... | collective-permute-start | bytes 786440 | tf_op jit(solution)/shard_map/ppermute | solution.py:36
  34.1 7.3 %collective-permute-start.4 = (bf16[1024,128]{1,0:T(8,128)(2,1)S(1)}, bf16[1024,128]{1,0:T(8,128)(2,1)S(1)}, u32[]{:S(2)}, u32[]{:S(2)}) collective-permute-start(bf16[1024,128]{1,0:T(8,128)(2,1)S(1)} %collective-permute-done), channel_id=1, source_target_pairs={{2,0},{3,1},{4,2},{5,3},{6,4},{7,5},{0,6},{1,7},{10,8},{11,9},{12,... | collective-permute-start | bytes 786440 | tf_op jit(solution)/shard_map/ppermute | solution.py:36
  35.2 9.6 %collective-permute-start.5 = (bf16[1024,128]{1,0:T(8,128)(2,1)S(1)}, bf16[1024,128]{1,0:T(8,128)(2,1)S(1)}, u32[]{:S(2)}, u32[]{:S(2)}) collective-permute-start(bf16[1024,128]{1,0:T(8,128)(2,1)S(1)} %collective-permute-done), channel_id=1, source_target_pairs={{6,0},{7,1},{0,2},{1,3},{2,4},{3,5},{4,6},{5,7},{14,8},{15,9},{8,1... | collective-permute-start | bytes 786440 | tf_op jit(solution)/shard_map/ppermute | solution.py:36
  36.2 8.5 %collective-permute-start.6 = (bf16[1024,128]{1,0:T(8,128)(2,1)S(1)}, bf16[1024,128]{1,0:T(8,128)(2,1)S(1)}, u32[]{:S(2)}, u32[]{:S(2)}) collective-permute-start(bf16[1024,128]{1,0:T(8,128)(2,1)S(1)} %collective-permute-done.1), channel_id=1, source_target_pairs={{8,0},{9,1},{10,2},{11,3},{12,4},{13,5},{14,6},{15,7},{0,8},{1,9},... | collective-permute-start | bytes 786440 | tf_op jit(solution)/shard_map/ppermute | solution.py:36
  91.2 7.9 %collective-permute-start.9 = (bf16[1024,128]{1,0:T(8,128)(2,1)S(1)}, bf16[1024,128]{1,0:T(8,128)(2,1)S(1)}, u32[]{:S(2)}, u32[]{:S(2)}) collective-permute-start(bf16[1024,128]{1,0:T(8,128)(2,1)S(1)} %bitcast.40), channel_id=1, source_target_pairs={{8,0},{9,1},{10,2},{11,3},{12,4},{13,5},{14,6},{15,7},{0,8},{1,9},... | collective-permute-start | bytes 786440 | tf_op jit(solution)/shard_map/ppermute | solution.py:36
  93.3 10.7 %collective-permute-start.10 = (bf16[1024,128]{1,0:T(8,128)(2,1)S(1)}, bf16[1024,128]{1,0:T(8,128)(2,1)S(1)}, u32[]{:S(2)}, u32[]{:S(2)}) collective-permute-start(bf16[1024,128]{1,0:T(8,128)(2,1)S(1)} %bitcast.41), channel_id=1, source_target_pairs={{4,0},{5,1},{6,2},{7,3},{0,4},{1,5},{2,6},{3,7},{12,8},{13,9},{14,... | collective-permute-start | bytes 786440 | tf_op jit(solution)/shard_map/ppermute | solution.py:36
  95.2 12.7 %collective-permute-start.11 = (bf16[1024,128]{1,0:T(8,128)(2,1)S(1)}, bf16[1024,128]{1,0:T(8,128)(2,1)S(1)}, u32[]{:S(2)}, u32[]{:S(2)}) collective-permute-start(bf16[1024,128]{1,0:T(8,128)(2,1)S(1)} %bitcast.42), channel_id=1, source_target_pairs={{2,0},{3,1},{4,2},{5,3},{6,4},{7,5},{0,6},{1,7},{10,8},{11,9},{12,... | collective-permute-start | bytes 786440 | tf_op jit(solution)/shard_map/ppermute | solution.py:36
  97.5 11.4 %collective-permute-start.12 = (bf16[1024,128]{1,0:T(8,128)(2,1)S(1)}, bf16[1024,128]{1,0:T(8,128)(2,1)S(1)}, u32[]{:S(2)}, u32[]{:S(2)}) collective-permute-start(bf16[1024,128]{1,0:T(8,128)(2,1)S(1)} %bitcast.43), channel_id=1, source_target_pairs={{6,0},{7,1},{0,2},{1,3},{2,4},{3,5},{4,6},{5,7},{14,8},{15,9},{8,1... | collective-permute-start | bytes 786440 | tf_op jit(solution)/shard_map/ppermute | solution.py:36
  99.1 11.7 %collective-permute-start.13 = (bf16[1024,128]{1,0:T(8,128)(2,1)S(1)}, bf16[1024,128]{1,0:T(8,128)(2,1)S(1)}, u32[]{:S(2)}, u32[]{:S(2)}) collective-permute-start(bf16[1024,128]{1,0:T(8,128)(2,1)S(1)} %collective-permute-done.9), channel_id=1, source_target_pairs={{2,0},{3,1},{4,2},{5,3},{6,4},{7,5},{0,6},{1,7},{10,8},{11,9},{12,... | collective-permute-start | bytes 786440 | tf_op jit(solution)/shard_map/ppermute | solution.py:36
  100.8 11.7 %collective-permute-start.14 = (bf16[1024,128]{1,0:T(8,128)(2,1)S(1)}, bf16[1024,128]{1,0:T(8,128)(2,1)S(1)}, u32[]{:S(2)}, u32[]{:S(2)}) collective-permute-start(bf16[1024,128]{1,0:T(8,128)(2,1)S(1)} %collective-permute-done.9), channel_id=1, source_target_pairs={{6,0},{7,1},{0,2},{1,3},{2,4},{3,5},{4,6},{5,7},{14,8},{15,9},{8,1... | collective-permute-start | bytes 786440 | tf_op jit(solution)/shard_map/ppermute | solution.py:36
  104.1 8.5 %collective-permute-start.15 = (bf16[1024,128]{1,0:T(8,128)(2,1)S(1)}, bf16[1024,128]{1,0:T(8,128)(2,1)S(1)}, u32[]{:S(2)}, u32[]{:S(2)}) collective-permute-start(bf16[1024,128]{1,0:T(8,128)(2,1)S(1)} %collective-permute-done.10), channel_id=1, source_target_pairs={{8,0},{9,1},{10,2},{11,3},{12,4},{13,5},{14,6},{15,7},{0,8},{1,9},... | collective-permute-start | bytes 786440 | tf_op jit(solution)/shard_map/ppermute | solution.py:36
  108.0 4.9 %collective-permute-start.16 = (bf16[4096,128]{1,0:T(8,128)(2,1)S(1)}, bf16[4096,128]{1,0:T(8,128)(2,1)S(1)}, u32[]{:S(2)}, u32[]{:S(2)}) collective-permute-start(bf16[4096,128]{1,0:T(8,128)(2,1)S(1)} %pad_maximum_fusion.2), channel_id=1, source_target_pairs={{1,0},{0,1},{3,2},{2,3},{5,4},{4,5},{7,6},{6,7},{9,8},{8,9},{11,10... | collective-permute-start | bytes 3145736 | tf_op jit(solution)/shard_map/ppermute | solution.py:36
  156.1 7.9 %collective-permute-start.18 = (bf16[1024,128]{1,0:T(8,128)(2,1)S(1)}, bf16[1024,128]{1,0:T(8,128)(2,1)S(1)}, u32[]{:S(2)}, u32[]{:S(2)}) collective-permute-start(bf16[1024,128]{1,0:T(8,128)(2,1)S(1)} %bitcast.34), channel_id=1, source_target_pairs={{8,0},{9,1},{10,2},{11,3},{12,4},{13,5},{14,6},{15,7},{0,8},{1,9},... | collective-permute-start | bytes 786440 | tf_op jit(solution)/shard_map/ppermute | solution.py:36
  156.8 10.7 %collective-permute-start.19 = (bf16[1024,128]{1,0:T(8,128)(2,1)S(1)}, bf16[1024,128]{1,0:T(8,128)(2,1)S(1)}, u32[]{:S(2)}, u32[]{:S(2)}) collective-permute-start(bf16[1024,128]{1,0:T(8,128)(2,1)S(1)} %bitcast.35), channel_id=1, source_target_pairs={{4,0},{5,1},{6,2},{7,3},{0,4},{1,5},{2,6},{3,7},{12,8},{13,9},{14,... | collective-permute-start | bytes 786440 | tf_op jit(solution)/shard_map/ppermute | solution.py:36
  158.9 12.5 %collective-permute-start.20 = (bf16[1024,128]{1,0:T(8,128)(2,1)S(1)}, bf16[1024,128]{1,0:T(8,128)(2,1)S(1)}, u32[]{:S(2)}, u32[]{:S(2)}) collective-permute-start(bf16[1024,128]{1,0:T(8,128)(2,1)S(1)} %bitcast.36), channel_id=1, source_target_pairs={{2,0},{3,1},{4,2},{5,3},{6,4},{7,5},{0,6},{1,7},{10,8},{11,9},{12,... | collective-permute-start | bytes 786440 | tf_op jit(solution)/shard_map/ppermute | solution.py:36
  159.9 11.9 %collective-permute-start.21 = (bf16[1024,128]{1,0:T(8,128)(2,1)S(1)}, bf16[1024,128]{1,0:T(8,128)(2,1)S(1)}, u32[]{:S(2)}, u32[]{:S(2)}) collective-permute-start(bf16[1024,128]{1,0:T(8,128)(2,1)S(1)} %bitcast.37), channel_id=1, source_target_pairs={{6,0},{7,1},{0,2},{1,3},{2,4},{3,5},{4,6},{5,7},{14,8},{15,9},{8,1... | collective-permute-start | bytes 786440 | tf_op jit(solution)/shard_map/ppermute | solution.py:36
  163.9 10.3 %collective-permute-start.22 = (bf16[1024,128]{1,0:T(8,128)(2,1)S(1)}, bf16[1024,128]{1,0:T(8,128)(2,1)S(1)}, u32[]{:S(2)}, u32[]{:S(2)}) collective-permute-start(bf16[1024,128]{1,0:T(8,128)(2,1)S(1)} %collective-permute-done.18), channel_id=1, source_target_pairs={{2,0},{3,1},{4,2},{5,3},{6,4},{7,5},{0,6},{1,7},{10,8},{11,9},{12,... | collective-permute-start | bytes 786440 | tf_op jit(solution)/shard_map/ppermute | solution.py:36
  165.3 10.2 %collective-permute-start.23 = (bf16[1024,128]{1,0:T(8,128)(2,1)S(1)}, bf16[1024,128]{1,0:T(8,128)(2,1)S(1)}, u32[]{:S(2)}, u32[]{:S(2)}) collective-permute-start(bf16[1024,128]{1,0:T(8,128)(2,1)S(1)} %collective-permute-done.18), channel_id=1, source_target_pairs={{6,0},{7,1},{0,2},{1,3},{2,4},{3,5},{4,6},{5,7},{14,8},{15,9},{8,1... | collective-permute-start | bytes 786440 | tf_op jit(solution)/shard_map/ppermute | solution.py:36
  167.5 8.0 %collective-permute-start.24 = (bf16[1024,128]{1,0:T(8,128)(2,1)S(1)}, bf16[1024,128]{1,0:T(8,128)(2,1)S(1)}, u32[]{:S(2)}, u32[]{:S(2)}) collective-permute-start(bf16[1024,128]{1,0:T(8,128)(2,1)S(1)} %collective-permute-done.19), channel_id=1, source_target_pairs={{8,0},{9,1},{10,2},{11,3},{12,4},{13,5},{14,6},{15,7},{0,8},{1,9},... | collective-permute-start | bytes 786440 | tf_op jit(solution)/shard_map/ppermute | solution.py:36
  171.5 4.4 %collective-permute-start.25 = (bf16[4096,128]{1,0:T(8,128)(2,1)S(1)}, bf16[4096,128]{1,0:T(8,128)(2,1)S(1)}, u32[]{:S(2)}, u32[]{:S(2)}) collective-permute-start(bf16[4096,128]{1,0:T(8,128)(2,1)S(1)} %pad_maximum_fusion.4), channel_id=1, source_target_pairs={{1,0},{0,1},{3,2},{2,3},{5,4},{4,5},{7,6},{6,7},{9,8},{8,9},{11,10... | collective-permute-start | bytes 3145736 | tf_op jit(solution)/shard_map/ppermute | solution.py:36
  (8 other events, 82.7 us)

commit v4 on v3

--- a/solution.py
+++ b/solution.py
@@ -31,6 +31,11 @@
 SHIFTS = ((0, 0), (1, 0), (0, 2), (0, 1), (0, 3), (1, 1), (1, 3), (1, 2))
 
 
+def joined(blocks):
+    half = blocks[0].shape[0] // 2
+    return jnp.concatenate([blocks[0][:half], blocks[0][half:], *blocks[1:]], axis=0)
+
+
 def gather_pieces(own, riders=()):
     def fetch(block, *shift):
         return lax.ppermute(block, "row", row_peers(*shift))
@@ -40,7 +45,7 @@
     relayed = [fetch(across, 0, 1, 0), fetch(across, 0, 3, 0), fetch(opposite, 1, 0, 0)]
     direct = [own, across, opposite, above, below]
     order = direct + relayed
-    early, late = (jnp.concatenate(part, axis=0) for part in (order[:4], order[4:]))
+    early, late = (joined(part) for part in (order[:4], order[4:]))
     early, riders = lax.optimization_barrier((early, riders))
     swapped = [fetch(part, 0, 0, 1) for part in (early, late)]
     return jnp.concatenate(order + swapped, axis=0), riders
@@ -154,15 +159,33 @@
 REDUCED, DIAGONAL, COUPLING, KINDS = GAINS + 2, GAINS + 3, GAINS + 4, GAINS + 5
 
 
-def coefficient_kernel(
-    classes, own, cosine, sine, diagonals, couplings, loads, more_loads, rounded, table, held, arrived
-):
+def staging_kernel(cosine_load, sine_load, base, ratio, mistuning, loads, diagonals, couplings, *held):
+    *held, arrived = held
+    targets = (loads.at[0], loads.at[1], *held)
     copies = [
-        pltpu.make_async_copy(source, held.at[side], arrived.at[side])
-        for side, source in enumerate((loads, more_loads))
+        pltpu.make_async_copy(source, target, arrived.at[index])
+        for index, (source, target) in enumerate(
+            zip((cosine_load, sine_load, base, ratio, mistuning), targets)
+        )
     ]
-    for copy in copies:
+    for copy in copies[::-1]:
         copy.start()
+    for copy in copies[2:]:
+        copy.wait()
+    stiffness, spring, deviation = (part[...] for part in held)
+    groups, lanes = stiffness.shape
+    couplings[...] = spring * stiffness
+    for index in range(deviation.shape[0]):
+        rows = [
+            deviation[index : index + 1, group * lanes : (group + 1) * lanes]
+            for group in range(groups)
+        ]
+        diagonals[index] = stiffness * (1.0 + jnp.concatenate(rows, axis=0))
+    for copy in copies[:2]:
+        copy.wait()
+
+
+def coefficient_kernel(classes, own, cosine, sine, diagonals, couplings, loads, rounded, table):
     sectors = table.shape[1]
     coupling = couplings[...]
     diagonal = [diagonals[classes[s]] for s in range(sectors)]
@@ -180,13 +203,11 @@
             table[kind, s] = cells[s]
     groups, lanes = coupling.shape
     cosine_gain, sine_gain = table[GAINS, own[0]].T, table[GAINS + 1, own[0]].T
-    for copy in copies:
-        copy.wait()
     for group in range(groups):
         rows = pl.ds(group * lanes, lanes)
         rounded[rows, :] = (
-            cosine_gain[:, group : group + 1] * held[0, rows, :]
-            + sine_gain[:, group : group + 1] * held[1, rows, :]
+            cosine_gain[:, group : group + 1] * loads[0, rows, :]
+            + sine_gain[:, group : group + 1] * loads[1, rows, :]
         ).astype(rounded.dtype)
 
 
@@ -259,34 +280,47 @@
 
     lanes = 128
     groups = local_rows // lanes
-    base = base_stiffness.reshape(groups, lanes)
-    coupling = coupling_ratio.reshape(groups, lanes) * base
-    diagonals = base * (1.0 + mistuning.reshape(-1, groups, lanes))
+    loads, diagonals, couplings = pl.pallas_call(
+        staging_kernel,
+        out_shape=(
+            jax.ShapeDtypeStruct((2, local_rows, load_cases), jnp.float32),
+            jax.ShapeDtypeStruct((mistuning.shape[0], groups, lanes), jnp.float32),
+            jax.ShapeDtypeStruct((groups, lanes), jnp.float32),
+        ),
+        in_specs=[pl.BlockSpec(memory_space=pl.ANY)] * 5,
+        out_specs=(vmem,) * 3,
+        scratch_shapes=[
+            pltpu.VMEM((groups, lanes), jnp.float32),
+            pltpu.VMEM((groups, lanes), jnp.float32),
+            pltpu.VMEM(mistuning.shape, jnp.float32),
+            pltpu.SemaphoreType.DMA((5,)),
+        ],
+        compiler_params=pltpu.CompilerParams(vmem_limit_bytes=16 * 1024 * 1024),
+    )(
+        *[
+            pltpu.with_memory_space_constraint(part, pltpu.HBM)
+            for part in (
+                cosine_load,
+                sine_load,
+                base_stiffness.reshape(groups, lanes),
+                coupling_ratio.reshape(groups, lanes),
+                mistuning,
+            )
+        ]
+    )
     rounded, table = pl.pallas_call(
         coefficient_kernel,
         out_shape=(
             jax.ShapeDtypeStruct((local_rows, load_cases), jnp.bfloat16),
             jax.ShapeDtypeStruct((KINDS, sectors, groups, lanes), jnp.float32),
         ),
-        in_specs=[smem] * 4 + [vmem] * 2 + [pl.BlockSpec(memory_space=pl.ANY)] * 2,
+        in_specs=[smem] * 4 + [vmem] * 3,
         out_specs=(vmem, vmem),
-        scratch_shapes=[
-            pltpu.VMEM((2, local_rows, load_cases), jnp.float32),
-            pltpu.SemaphoreType.DMA((2,)),
-        ],
-        compiler_params=pltpu.CompilerParams(vmem_limit_bytes=58 * 1024 * 1024),
-    )(
-        all_classes,
-        sector_id[None],
-        cosine,
-        sine,
-        diagonals,
-        coupling,
-        cosine_load,
-        sine_load,
-    )
-
-    cosine_slice, sine_slice = own_slice(cosine_load, 0), own_slice(sine_load, 0)
+        compiler_params=pltpu.CompilerParams(vmem_limit_bytes=16 * 1024 * 1024),
+    )(all_classes, sector_id[None], cosine, sine, diagonals, couplings, loads)
+    rounded, loads, block_columns = lax.optimization_barrier((rounded, loads, block_columns))
+
+    cosine_slice, sine_slice = own_slice(loads[0], 0), own_slice(loads[1], 0)
     table = own_slice(table.reshape(KINDS * sectors, local_rows), 1)
     table = jnp.broadcast_to(
         table.reshape(KINDS, sectors, slice_rows, 1), (KINDS, sectors, slice_rows, load_cases)

time: 216 us -> 210 us (0.972)
  other arithmetic: 8.16 us -> 1.93 us
  waiting for transfers between devices: 34.1 us -> 39.2 us
  blocking collectives: 106 us -> 102 us
    all_to_all x1, waiting for transfers between devices: 0.9 us -> 5.03 us  [swap(): return lax.all_to_all(cells, 'sector', 0, 0, tiled=True)]
    all_to_all x6, blocking collectives: 106 us -> 102 us  [swap(): return lax.all_to_all(cells, 'sector', 0, 0, tiled=True)]
    mul x2 -> x0, other arithmetic: 2.58 us -> none  [the longest x1 1.29 us: shards(): diagonals = base * (1.0 + mistuning.reshape(-1, groups, lanes))]
  transfers between devices with their start and end apart: 28 -> 28, of which waited for: 19 -> 21; matrix products, arithmetic and copies ran while one was open for 6% -> 2% of each run, Pallas kernels for 0% -> 1%
where the time goes in v4:
time: 210 us; the launch traced here: 209 us
  blocking collectives  102 us (49%)
  starting transfers between devices  42 us (20%)
  waiting for transfers between devices  39.2 us (19%)
  Pallas kernels  16.1 us (8%)
  local copies, waits for them, and re-layouts  5.43 us (3%)
    all_to_all x6, blocking collectives, swap(): return lax.all_to_all(cells, 'sector', 0, 0, tiled=True)  102 us
    ppermute x27, waiting for transfers between devices, fetch(): return lax.ppermute(block, 'row', row_peers(*shift))  34.1 us
    ppermute x27, starting transfers between devices, fetch(): return lax.ppermute(block, 'row', row_peers(*shift))  32.1 us
    pallas_call x3, Pallas kernels, block_product(): pl.pallas_call(product_kernel, out_shape=jax.ShapeDtypeStruct((rows * ord...  10.2 us
    all_to_all x1, starting transfers between devices, swap(): return lax.all_to_all(cells, 'sector', 0, 0, tiled=True)  9.94 us
    all_to_all x1, waiting for transfers between devices, swap(): return lax.all_to_all(cells, 'sector', 0, 0, tiled=True)  5.03 us
  transfers between devices with their start and end apart: 28, of which 21 were waited for; matrix products, arithmetic and copies ran while one was open for 2% of the time, Pallas kernels for 1%

profile of v4, /device:TPU:2, one launch (start us, length us, event | category | flops | bytes accessed | tf_op | source)
XLA Modules:
  0.0 208.6 jit_solution(14384111247009269979)
XLA Ops:
  1.3 9.9 %all-to-all-start = ((s32[16,1,1]{2,1,0:T(1,128)}), s32[16,1,1]{2,1,0:T(1,128)S(1)}, u32[]{:S(2)}, u32[]{:S(2)}) async-start(s32[16,1,1]{2,1,0:T(1,128)} %broadcast_in_dim.48), calls=%async_computation | async-start | bytes 16384 | tf_op jit(solution)/shard_map/all_to_all | solution.py:271
  13.2 5.0 %all-to-all-done = s32[16,1,1]{2,1,0:T(1,128)S(1)} async-done(((s32[16,1,1]{2,1,0:T(1,128)}), s32[16,1,1]{2,1,0:T(1,128)S(1)}, u32[]{:S(2)}, u32[]{:S(2)}) %all-to-all-start) | async-done | bytes 96 | tf_op jit(solution)/shard_map/all_to_all | solution.py:271
  19.9 3.1 %collective-permute-start.2 = (bf16[1024,128]{1,0:T(8,128)(2,1)S(1)}, bf16[1024,128]{1,0:T(8,128)(2,1)S(1)}, u32[]{:S(2)}, u32[]{:S(2)}) collective-permute-start(bf16[1024,128]{1,0:T(8,128)(2,1)S(1)} %get-tuple-element.30), channel_id=1, source_target_pairs={{2,0},{3,1},{4,2},{5,3},{6,4},{7,5},{0,6},{1,7},{10,8},{11,9},{12,... | collective-permute-start | bytes 786440 | tf_op jit(solution)/shard_map/ppermute | solution.py:41
  28.3 3.1 %collective-permute-done = bf16[1024,128]{1,0:T(8,128)(2,1)S(1)} collective-permute-done((bf16[1024,128]{1,0:T(8,128)(2,1)S(1)}, bf16[1024,128]{1,0:T(8,128)(2,1)S(1)}, u32[]{:S(2)}, u32[]{:S(2)}) %collective-permute-start) | collective-permute-done | bytes 262176 | tf_op jit(solution)/shard_map/ppermute | solution.py:41
  38.3 3.7 %collective-permute-done.5 = bf16[1024,128]{1,0:T(8,128)(2,1)S(1)} collective-permute-done((bf16[1024,128]{1,0:T(8,128)(2,1)S(1)}, bf16[1024,128]{1,0:T(8,128)(2,1)S(1)}, u32[]{:S(2)}, u32[]{:S(2)}) %collective-permute-start.5) | collective-permute-done | bytes 262176 | tf_op jit(solution)/shard_map/ppermute | solution.py:41
  42.6 2.3 %collective-permute-done.8 = bf16[4096,128]{1,0:T(8,128)(2,1)S(1)} collective-permute-done((bf16[4096,128]{1,0:T(8,128)(2,1)S(1)}, bf16[4096,128]{1,0:T(8,128)(2,1)S(1)}, u32[]{:S(2)}, u32[]{:S(2)}) %collective-permute-start.8) | collective-permute-done | bytes 1048608 | tf_op jit(solution)/shard_map/ppermute | solution.py:41
  45.0 3.4 %shard_map.93 = f32[1024,128]{1,0:T(8,128)S(1)} custom-call(s32[64]{0:T(128)S(1)} %reshape.83.columns, bf16[4,16,256,256]{3,2,1,0:T(8,128)(2,1)S(1)} %bitcast.30, bf16[16384,128]{1,0:T(8,128)(2,1)S(1)} %constant_dynamic-update-slice_fusion.gathered), custom_call_target="tpu_custom_call" | custom-call | flops 1073741824 | bytes 8388608 | tf_op jit(solution)/shard_map/pallas_call | solution.py:92
  48.5 21.2 %all_to_all.36.refs_0_ = f32[16,64,128]{2,1,0:T(8,128)S(1)} all-to-all(f32[16,64,128]{2,1,0:T(8,128)S(1)} %bitcast.34), channel_id=1, replica_groups=mesh['sector'=16,'row'=16] {'sector'}, dimensions={0} | all-to-all | bytes 1048576 | tf_op jit(solution)/shard_map/all_to_all | solution.py:271
  70.7 14.3 %all_to_all.37 = bf16[16,64,128]{2,1,0:T(8,128)(2,1)S(1)} all-to-all(bf16[16,64,128]{2,1,0:T(8,128)(2,1)S(1)} %get-tuple-element.37), channel_id=1, replica_groups=mesh['sector'=16,'row'=16] {'sector'}, dimensions={0} | all-to-all | bytes 524288 | tf_op jit(solution)/shard_map/all_to_all | solution.py:271
  89.3 2.4 %collective-permute-start.11 = (bf16[1024,128]{1,0:T(8,128)(2,1)S(1)}, bf16[1024,128]{1,0:T(8,128)(2,1)S(1)}, u32[]{:S(2)}, u32[]{:S(2)}) collective-permute-start(bf16[1024,128]{1,0:T(8,128)(2,1)S(1)} %bitcast.44), channel_id=1, source_target_pairs={{2,0},{3,1},{4,2},{5,3},{6,4},{7,5},{0,6},{1,7},{10,8},{11,9},{12,... | collective-permute-start | bytes 786440 | tf_op jit(solution)/shard_map/ppermute | solution.py:41
  95.1 2.7 %collective-permute-done.10 = bf16[1024,128]{1,0:T(8,128)(2,1)S(1)} collective-permute-done((bf16[1024,128]{1,0:T(8,128)(2,1)S(1)}, bf16[1024,128]{1,0:T(8,128)(2,1)S(1)}, u32[]{:S(2)}, u32[]{:S(2)}) %collective-permute-start.10) | collective-permute-done | bytes 262176 | tf_op jit(solution)/shard_map/ppermute | solution.py:41
  99.4 2.3 %collective-permute-done.11 = bf16[1024,128]{1,0:T(8,128)(2,1)S(1)} collective-permute-done((bf16[1024,128]{1,0:T(8,128)(2,1)S(1)}, bf16[1024,128]{1,0:T(8,128)(2,1)S(1)}, u32[]{:S(2)}, u32[]{:S(2)}) %collective-permute-start.11) | collective-permute-done | bytes 262176 | tf_op jit(solution)/shard_map/ppermute | solution.py:41
  106.8 2.3 %collective-permute-done.17 = bf16[4096,128]{1,0:T(8,128)(2,1)S(1)} collective-permute-done((bf16[4096,128]{1,0:T(8,128)(2,1)S(1)}, bf16[4096,128]{1,0:T(8,128)(2,1)S(1)}, u32[]{:S(2)}, u32[]{:S(2)}) %collective-permute-start.17) | collective-permute-done | bytes 1048608 | tf_op jit(solution)/shard_map/ppermute | solution.py:41
  109.3 3.4 %shard_map.95.refs_0_ = f32[1024,128]{1,0:T(8,128)S(1)} custom-call(s32[64]{0:T(128)S(1)} %reshape.83.columns, bf16[4,16,256,256]{3,2,1,0:T(8,128)(2,1)S(1)} %bitcast.31, bf16[16384,128]{1,0:T(8,128)(2,1)S(1)} %constant_dynamic-update-slice_fusion.15.gathered), custom_call_target="tpu_custom_call" | custom-call | flops 1073741824 | bytes 8388608 | tf_op jit(solution)/shard_map/pallas_call | solution.py:92
  112.7 21.6 %all_to_all.38.refs_0_ = f32[16,64,128]{2,1,0:T(8,128)S(1)} all-to-all(f32[16,64,128]{2,1,0:T(8,128)S(1)} %bitcast.33), channel_id=1, replica_groups=mesh['sector'=16,'row'=16] {'sector'}, dimensions={0} | all-to-all | bytes 1048576 | tf_op jit(solution)/shard_map/all_to_all | solution.py:271
  135.3 14.4 %all_to_all.39 = bf16[16,64,128]{2,1,0:T(8,128)(2,1)S(1)} all-to-all(bf16[16,64,128]{2,1,0:T(8,128)(2,1)S(1)} %get-tuple-element.42), channel_id=1, replica_groups=mesh['sector'=16,'row'=16] {'sector'}, dimensions={0} | all-to-all | bytes 524288 | tf_op jit(solution)/shard_map/all_to_all | solution.py:271
  150.7 2.5 %collective-permute-start.19 = (bf16[1024,128]{1,0:T(8,128)(2,1)S(1)}, bf16[1024,128]{1,0:T(8,128)(2,1)S(1)}, u32[]{:S(2)}, u32[]{:S(2)}) collective-permute-start(bf16[1024,128]{1,0:T(8,128)(2,1)S(1)} %bitcast.38), channel_id=1, source_target_pairs={{4,0},{5,1},{6,2},{7,3},{0,4},{1,5},{2,6},{3,7},{12,8},{13,9},{14,... | collective-permute-start | bytes 786440 | tf_op jit(solution)/shard_map/ppermute | solution.py:41
  155.4 2.2 %collective-permute-done.18 = bf16[1024,128]{1,0:T(8,128)(2,1)S(1)} collective-permute-done((bf16[1024,128]{1,0:T(8,128)(2,1)S(1)}, bf16[1024,128]{1,0:T(8,128)(2,1)S(1)}, u32[]{:S(2)}, u32[]{:S(2)}) %collective-permute-start.18) | collective-permute-done | bytes 262176 | tf_op jit(solution)/shard_map/ppermute | solution.py:41
  161.5 2.5 %collective-permute-start.24 = (bf16[1024,128]{1,0:T(8,128)(2,1)S(1)}, bf16[1024,128]{1,0:T(8,128)(2,1)S(1)}, u32[]{:S(2)}, u32[]{:S(2)}) collective-permute-start(bf16[1024,128]{1,0:T(8,128)(2,1)S(1)} %collective-permute-done.19), channel_id=1, source_target_pairs={{8,0},{9,1},{10,2},{11,3},{12,4},{13,5},{14,6},{15,7},{0,8},{1,9},... | collective-permute-start | bytes 786440 | tf_op jit(solution)/shard_map/ppermute | solution.py:41
  166.0 2.3 %collective-permute-done.22 = bf16[1024,128]{1,0:T(8,128)(2,1)S(1)} collective-permute-done((bf16[1024,128]{1,0:T(8,128)(2,1)S(1)}, bf16[1024,128]{1,0:T(8,128)(2,1)S(1)}, u32[]{:S(2)}, u32[]{:S(2)}) %collective-permute-start.22) | collective-permute-done | bytes 262176 | tf_op jit(solution)/shard_map/ppermute | solution.py:41
  170.0 2.3 %collective-permute-done.26 = bf16[4096,128]{1,0:T(8,128)(2,1)S(1)} collective-permute-done((bf16[4096,128]{1,0:T(8,128)(2,1)S(1)}, bf16[4096,128]{1,0:T(8,128)(2,1)S(1)}, u32[]{:S(2)}, u32[]{:S(2)}) %collective-permute-start.26) | collective-permute-done | bytes 1048608 | tf_op jit(solution)/shard_map/ppermute | solution.py:41
  172.5 3.4 %shard_map.97 = bf16[1024,128]{1,0:T(8,128)(2,1)S(1)} custom-call(s32[64]{0:T(128)S(1)} %reshape.83.columns, bf16[4,16,256,256]{3,2,1,0:T(8,128)(2,1)S(1)} %bitcast.32, bf16[16384,128]{1,0:T(8,128)(2,1)S(1)} %constant_dynamic-update-slice_fusion.30.gathered, f32[1024,128]{1,0:T(8,128)S(1)} %shard_map.95.refs_0_), custom_call_target="tpu_custom_call" | custom-call | flops 1073741824 | bytes 8388608 | tf_op jit(solution)/shard_map/pallas_call | solution.py:92
  175.9 16.3 %all_to_all.40.refs_1_ = bf16[16,64,128]{2,1,0:T(8,128)(2,1)S(1)} all-to-all(bf16[16,64,128]{2,1,0:T(8,128)(2,1)S(1)} %bitcast.35), channel_id=1, replica_groups=mesh['sector'=16,'row'=16] {'sector'}, dimensions={0} | all-to-all | bytes 524288 | tf_op jit(solution)/shard_map/all_to_all | solution.py:271
  193.3 14.4 %all_to_all.41 = bf16[16,64,128]{2,1,0:T(8,128)(2,1)S(1)} all-to-all(bf16[16,64,128]{2,1,0:T(8,128)(2,1)S(1)} %shard_map.98), channel_id=1, replica_groups=mesh['sector'=16,'row'=16] {'sector'}, dimensions={0} | all-to-all | bytes 524288 | tf_op jit(solution)/shard_map/all_to_all | solution.py:271
  (109 shorter events, 45.7 us)
Async XLA Ops:
  1.3 17.0 %all-to-all-start = ((s32[16,1,1]{2,1,0:T(1,128)}), s32[16,1,1]{2,1,0:T(1,128)S(1)}, u32[]{:S(2)}, u32[]{:S(2)}) async-start(s32[16,1,1]{2,1,0:T(1,128)} %broadcast_in_dim.48), calls=%async_computation | async-start | bytes 16384 | tf_op jit(solution)/shard_map/all_to_all | solution.py:271
  19.9 16.0 %collective-permute-start.2 = (bf16[1024,128]{1,0:T(8,128)(2,1)S(1)}, bf16[1024,128]{1,0:T(8,128)(2,1)S(1)}, u32[]{:S(2)}, u32[]{:S(2)}) collective-permute-start(bf16[1024,128]{1,0:T(8,128)(2,1)S(1)} %get-tuple-element.30), channel_id=1, source_target_pairs={{2,0},{3,1},{4,2},{5,3},{6,4},{7,5},{0,6},{1,7},{10,8},{11,9},{12,... | collective-permute-start | bytes 786440 | tf_op jit(solution)/shard_map/ppermute | solution.py:41
  23.0 10.7 %collective-permute-start.1 = (bf16[1024,128]{1,0:T(8,128)(2,1)S(1)}, bf16[1024,128]{1,0:T(8,128)(2,1)S(1)}, u32[]{:S(2)}, u32[]{:S(2)}) collective-permute-start(bf16[1024,128]{1,0:T(8,128)(2,1)S(1)} %get-tuple-element.30), channel_id=1, source_target_pairs={{4,0},{5,1},{6,2},{7,3},{0,4},{1,5},{2,6},{3,7},{12,8},{13,9},{14,... | collective-permute-start | bytes 786440 | tf_op jit(solution)/shard_map/ppermute | solution.py:41
  23.6 7.9 %collective-permute-start = (bf16[1024,128]{1,0:T(8,128)(2,1)S(1)}, bf16[1024,128]{1,0:T(8,128)(2,1)S(1)}, u32[]{:S(2)}, u32[]{:S(2)}) collective-permute-start(bf16[1024,128]{1,0:T(8,128)(2,1)S(1)} %get-tuple-element.30), channel_id=1, source_target_pairs={{8,0},{9,1},{10,2},{11,3},{12,4},{13,5},{14,6},{15,7},{0,8},{1,9},... | collective-permute-start | bytes 786440 | tf_op jit(solution)/shard_map/ppermute | solution.py:41
  26.5 11.7 %collective-permute-start.3 = (bf16[1024,128]{1,0:T(8,128)(2,1)S(1)}, bf16[1024,128]{1,0:T(8,128)(2,1)S(1)}, u32[]{:S(2)}, u32[]{:S(2)}) collective-permute-start(bf16[1024,128]{1,0:T(8,128)(2,1)S(1)} %get-tuple-element.30), channel_id=1, source_target_pairs={{6,0},{7,1},{0,2},{1,3},{2,4},{3,5},{4,6},{5,7},{14,8},{15,9},{8,1... | collective-permute-start | bytes 786440 | tf_op jit(solution)/shard_map/ppermute | solution.py:41
  31.5 6.9 %collective-permute-start.4 = (bf16[1024,128]{1,0:T(8,128)(2,1)S(1)}, bf16[1024,128]{1,0:T(8,128)(2,1)S(1)}, u32[]{:S(2)}, u32[]{:S(2)}) collective-permute-start(bf16[1024,128]{1,0:T(8,128)(2,1)S(1)} %collective-permute-done), channel_id=1, source_target_pairs={{2,0},{3,1},{4,2},{5,3},{6,4},{7,5},{0,6},{1,7},{10,8},{11,9},{12,... | collective-permute-start | bytes 786440 | tf_op jit(solution)/shard_map/ppermute | solution.py:41
  32.5 9.5 %collective-permute-start.5 = (bf16[1024,128]{1,0:T(8,128)(2,1)S(1)}, bf16[1024,128]{1,0:T(8,128)(2,1)S(1)}, u32[]{:S(2)}, u32[]{:S(2)}) collective-permute-start(bf16[1024,128]{1,0:T(8,128)(2,1)S(1)} %collective-permute-done), channel_id=1, source_target_pairs={{6,0},{7,1},{0,2},{1,3},{2,4},{3,5},{4,6},{5,7},{14,8},{15,9},{8,1... | collective-permute-start | bytes 786440 | tf_op jit(solution)/shard_map/ppermute | solution.py:41
  33.6 8.4 %collective-permute-start.6 = (bf16[1024,128]{1,0:T(8,128)(2,1)S(1)}, bf16[1024,128]{1,0:T(8,128)(2,1)S(1)}, u32[]{:S(2)}, u32[]{:S(2)}) collective-permute-start(bf16[1024,128]{1,0:T(8,128)(2,1)S(1)} %collective-permute-done.1), channel_id=1, source_target_pairs={{8,0},{9,1},{10,2},{11,3},{12,4},{13,5},{14,6},{15,7},{0,8},{1,9},... | collective-permute-start | bytes 786440 | tf_op jit(solution)/shard_map/ppermute | solution.py:41
  37.6 4.9 %collective-permute-start.7 = (bf16[4096,128]{1,0:T(8,128)(2,1)S(1)}, bf16[4096,128]{1,0:T(8,128)(2,1)S(1)}, u32[]{:S(2)}, u32[]{:S(2)}) collective-permute-start(bf16[4096,128]{1,0:T(8,128)(2,1)S(1)} %pad_maximum_fusion), channel_id=1, source_target_pairs={{1,0},{0,1},{3,2},{2,3},{5,4},{4,5},{7,6},{6,7},{9,8},{8,9},{11,10... | collective-permute-start | bytes 3145736 | tf_op jit(solution)/shard_map/ppermute | solution.py:41
  85.0 7.9 %collective-permute-start.9 = (bf16[1024,128]{1,0:T(8,128)(2,1)S(1)}, bf16[1024,128]{1,0:T(8,128)(2,1)S(1)}, u32[]{:S(2)}, u32[]{:S(2)}) collective-permute-start(bf16[1024,128]{1,0:T(8,128)(2,1)S(1)} %bitcast.42), channel_id=1, source_target_pairs={{8,0},{9,1},{10,2},{11,3},{12,4},{13,5},{14,6},{15,7},{0,8},{1,9},... | collective-permute-start | bytes 786440 | tf_op jit(solution)/shard_map/ppermute | solution.py:41
  87.1 10.7 %collective-permute-start.10 = (bf16[1024,128]{1,0:T(8,128)(2,1)S(1)}, bf16[1024,128]{1,0:T(8,128)(2,1)S(1)}, u32[]{:S(2)}, u32[]{:S(2)}) collective-permute-start(bf16[1024,128]{1,0:T(8,128)(2,1)S(1)} %bitcast.43), channel_id=1, source_target_pairs={{4,0},{5,1},{6,2},{7,3},{0,4},{1,5},{2,6},{3,7},{12,8},{13,9},{14,... | collective-permute-start | bytes 786440 | tf_op jit(solution)/shard_map/ppermute | solution.py:41
  89.3 12.4 %collective-permute-start.11 = (bf16[1024,128]{1,0:T(8,128)(2,1)S(1)}, bf16[1024,128]{1,0:T(8,128)(2,1)S(1)}, u32[]{:S(2)}, u32[]{:S(2)}) collective-permute-start(bf16[1024,128]{1,0:T(8,128)(2,1)S(1)} %bitcast.44), channel_id=1, source_target_pairs={{2,0},{3,1},{4,2},{5,3},{6,4},{7,5},{0,6},{1,7},{10,8},{11,9},{12,... | collective-permute-start | bytes 786440 | tf_op jit(solution)/shard_map/ppermute | solution.py:41
  91.7 11.1 %collective-permute-start.12 = (bf16[1024,128]{1,0:T(8,128)(2,1)S(1)}, bf16[1024,128]{1,0:T(8,128)(2,1)S(1)}, u32[]{:S(2)}, u32[]{:S(2)}) collective-permute-start(bf16[1024,128]{1,0:T(8,128)(2,1)S(1)} %bitcast.45), channel_id=1, source_target_pairs={{6,0},{7,1},{0,2},{1,3},{2,4},{3,5},{4,6},{5,7},{14,8},{15,9},{8,1... | collective-permute-start | bytes 786440 | tf_op jit(solution)/shard_map/ppermute | solution.py:41
  92.9 11.6 %collective-permute-start.13 = (bf16[1024,128]{1,0:T(8,128)(2,1)S(1)}, bf16[1024,128]{1,0:T(8,128)(2,1)S(1)}, u32[]{:S(2)}, u32[]{:S(2)}) collective-permute-start(bf16[1024,128]{1,0:T(8,128)(2,1)S(1)} %collective-permute-done.9), channel_id=1, source_target_pairs={{2,0},{3,1},{4,2},{5,3},{6,4},{7,5},{0,6},{1,7},{10,8},{11,9},{12,... | collective-permute-start | bytes 786440 | tf_op jit(solution)/shard_map/ppermute | solution.py:41
  95.1 11.2 %collective-permute-start.14 = (bf16[1024,128]{1,0:T(8,128)(2,1)S(1)}, bf16[1024,128]{1,0:T(8,128)(2,1)S(1)}, u32[]{:S(2)}, u32[]{:S(2)}) collective-permute-start(bf16[1024,128]{1,0:T(8,128)(2,1)S(1)} %collective-permute-done.9), channel_id=1, source_target_pairs={{6,0},{7,1},{0,2},{1,3},{2,4},{3,5},{4,6},{5,7},{14,8},{15,9},{8,1... | collective-permute-start | bytes 786440 | tf_op jit(solution)/shard_map/ppermute | solution.py:41
  97.8 8.5 %collective-permute-start.15 = (bf16[1024,128]{1,0:T(8,128)(2,1)S(1)}, bf16[1024,128]{1,0:T(8,128)(2,1)S(1)}, u32[]{:S(2)}, u32[]{:S(2)}) collective-permute-start(bf16[1024,128]{1,0:T(8,128)(2,1)S(1)} %collective-permute-done.10), channel_id=1, source_target_pairs={{8,0},{9,1},{10,2},{11,3},{12,4},{13,5},{14,6},{15,7},{0,8},{1,9},... | collective-permute-start | bytes 786440 | tf_op jit(solution)/shard_map/ppermute | solution.py:41
  101.8 4.9 %collective-permute-start.16 = (bf16[4096,128]{1,0:T(8,128)(2,1)S(1)}, bf16[4096,128]{1,0:T(8,128)(2,1)S(1)}, u32[]{:S(2)}, u32[]{:S(2)}) collective-permute-start(bf16[4096,128]{1,0:T(8,128)(2,1)S(1)} %get-tuple-element.41), channel_id=1, source_target_pairs={{1,0},{0,1},{3,2},{2,3},{5,4},{4,5},{7,6},{6,7},{9,8},{8,9},{11,10... | collective-permute-start | bytes 3145736 | tf_op jit(solution)/shard_map/ppermute | solution.py:41
  149.7 7.9 %collective-permute-start.18 = (bf16[1024,128]{1,0:T(8,128)(2,1)S(1)}, bf16[1024,128]{1,0:T(8,128)(2,1)S(1)}, u32[]{:S(2)}, u32[]{:S(2)}) collective-permute-start(bf16[1024,128]{1,0:T(8,128)(2,1)S(1)} %bitcast.37), channel_id=1, source_target_pairs={{8,0},{9,1},{10,2},{11,3},{12,4},{13,5},{14,6},{15,7},{0,8},{1,9},... | collective-permute-start | bytes 786440 | tf_op jit(solution)/shard_map/ppermute | solution.py:41
  150.7 10.7 %collective-permute-start.19 = (bf16[1024,128]{1,0:T(8,128)(2,1)S(1)}, bf16[1024,128]{1,0:T(8,128)(2,1)S(1)}, u32[]{:S(2)}, u32[]{:S(2)}) collective-permute-start(bf16[1024,128]{1,0:T(8,128)(2,1)S(1)} %bitcast.38), channel_id=1, source_target_pairs={{4,0},{5,1},{6,2},{7,3},{0,4},{1,5},{2,6},{3,7},{12,8},{13,9},{14,... | collective-permute-start | bytes 786440 | tf_op jit(solution)/shard_map/ppermute | solution.py:41
  153.2 12.2 %collective-permute-start.20 = (bf16[1024,128]{1,0:T(8,128)(2,1)S(1)}, bf16[1024,128]{1,0:T(8,128)(2,1)S(1)}, u32[]{:S(2)}, u32[]{:S(2)}) collective-permute-start(bf16[1024,128]{1,0:T(8,128)(2,1)S(1)} %bitcast.39), channel_id=1, source_target_pairs={{2,0},{3,1},{4,2},{5,3},{6,4},{7,5},{0,6},{1,7},{10,8},{11,9},{12,... | collective-permute-start | bytes 786440 | tf_op jit(solution)/shard_map/ppermute | solution.py:41
  154.3 11.6 %collective-permute-start.21 = (bf16[1024,128]{1,0:T(8,128)(2,1)S(1)}, bf16[1024,128]{1,0:T(8,128)(2,1)S(1)}, u32[]{:S(2)}, u32[]{:S(2)}) collective-permute-start(bf16[1024,128]{1,0:T(8,128)(2,1)S(1)} %bitcast.40), channel_id=1, source_target_pairs={{6,0},{7,1},{0,2},{1,3},{2,4},{3,5},{4,6},{5,7},{14,8},{15,9},{8,1... | collective-permute-start | bytes 786440 | tf_op jit(solution)/shard_map/ppermute | solution.py:41
  157.6 10.7 %collective-permute-start.22 = (bf16[1024,128]{1,0:T(8,128)(2,1)S(1)}, bf16[1024,128]{1,0:T(8,128)(2,1)S(1)}, u32[]{:S(2)}, u32[]{:S(2)}) collective-permute-start(bf16[1024,128]{1,0:T(8,128)(2,1)S(1)} %collective-permute-done.18), channel_id=1, source_target_pairs={{2,0},{3,1},{4,2},{5,3},{6,4},{7,5},{0,6},{1,7},{10,8},{11,9},{12,... | collective-permute-start | bytes 786440 | tf_op jit(solution)/shard_map/ppermute | solution.py:41
  159.1 10.4 %collective-permute-start.23 = (bf16[1024,128]{1,0:T(8,128)(2,1)S(1)}, bf16[1024,128]{1,0:T(8,128)(2,1)S(1)}, u32[]{:S(2)}, u32[]{:S(2)}) collective-permute-start(bf16[1024,128]{1,0:T(8,128)(2,1)S(1)} %collective-permute-done.18), channel_id=1, source_target_pairs={{6,0},{7,1},{0,2},{1,3},{2,4},{3,5},{4,6},{5,7},{14,8},{15,9},{8,1... | collective-permute-start | bytes 786440 | tf_op jit(solution)/shard_map/ppermute | solution.py:41
  161.5 8.0 %collective-permute-start.24 = (bf16[1024,128]{1,0:T(8,128)(2,1)S(1)}, bf16[1024,128]{1,0:T(8,128)(2,1)S(1)}, u32[]{:S(2)}, u32[]{:S(2)}) collective-permute-start(bf16[1024,128]{1,0:T(8,128)(2,1)S(1)} %collective-permute-done.19), channel_id=1, source_target_pairs={{8,0},{9,1},{10,2},{11,3},{12,4},{13,5},{14,6},{15,7},{0,8},{1,9},... | collective-permute-start | bytes 786440 | tf_op jit(solution)/shard_map/ppermute | solution.py:41
  (8 other events, 66.4 us)

commit v5 on v4

--- a/solution.py
+++ b/solution.py
@@ -64,50 +64,86 @@
     return (core * len(SHIFTS) + piece) * blocks_per_device + block_columns % blocks_per_device
 
 
-def product_kernel(columns, values, gathered, *refs):
-    *earlier, out = refs
-    rows, count, order, _ = values.shape
-
-    def one_row(row, carry):
+SCALE_ROWS = 8
+TOP_EXPONENT = 13.0
+
+
+def product_kernel(message, keep, columns, values, gathered, *refs):
+    count, order, _ = values.shape[1:]
+    load_cases = gathered.shape[1]
+    earlier, outs = (refs[:0], refs) if message else (refs[:1], refs[1:])
+
+    def one_row(row, largest):
         total = None
         for k in range(count):
             column = pl.multiple_of(columns[row * count + k] * order, order)
             term = jnp.dot(
-                values[row, k], gathered[pl.ds(column, order), :], preferred_element_type=jnp.float32
+                values[row, k],
+                gathered[pl.ds(column, order), :],
+                preferred_element_type=jnp.float32,
             )
             total = term if total is None else total + term
         own_rows = pl.ds(pl.multiple_of(row * order, order), order)
-        for product in earlier:
-            total = total - product[own_rows, :]
-        out[own_rows, :] = total.astype(out.dtype)
-        return carry
-
-    lax.fori_loop(0, rows, one_row, 0)
-
-
-def block_product(block_values, columns, gathered, *earlier):
+        if keep:
+            outs[1][own_rows, :] = total
+        if message:
+            slice_rows = outs[0].shape[1] - SCALE_ROWS
+            parts = order // slice_rows
+            for part in range(parts):
+                outs[0][row * parts + part, :slice_rows, :] = total[
+                    part * slice_rows : (part + 1) * slice_rows, :
+                ]
+            return jnp.maximum(
+                largest, jnp.max(jnp.abs(total).reshape(-1, SCALE_ROWS, load_cases), axis=0)
+            )
+        outs[0][own_rows, :] = (total - earlier[0][own_rows, :]).astype(outs[0].dtype)
+        return largest
+
+    start = jnp.zeros((SCALE_ROWS, load_cases), jnp.float32)
+    largest = lax.fori_loop(0, values.shape[0], one_row, start)
+    if message:
+        top = jnp.full(start.shape, jnp.max(largest), jnp.float32)
+        exponent = TOP_EXPONENT - jnp.floor(jnp.log2(jnp.maximum(top, 1e-30)))
+        scale = jnp.exp2(exponent)[:1, :]
+
+        def scaled(part, carry):
+            slice_rows = outs[0].shape[1] - SCALE_ROWS
+            outs[0][part, :slice_rows, :] = outs[0][part, :slice_rows, :] * scale
+            outs[0][part, slice_rows:, :] = exponent
+            return carry
+
+        lax.fori_loop(0, outs[0].shape[0], scaled, 0)
+
+
+def block_product(block_values, columns, gathered, slices, earlier=None, keep=False):
     rows, count, order, _ = block_values.shape
     load_cases = gathered.shape[1]
+    message = earlier is None
     vmem = pl.BlockSpec(memory_space=pltpu.VMEM)
+    whole = (rows * order, load_cases)
+    if message:
+        outs = [
+            jax.ShapeDtypeStruct(
+                (slices, rows * order // slices + SCALE_ROWS, load_cases), jnp.float32
+            )
+        ]
+    else:
+        outs = [jax.ShapeDtypeStruct(whole, jnp.bfloat16)]
+    if keep:
+        outs.append(jax.ShapeDtypeStruct(whole, jnp.float32))
+    operands = [block_values, gathered] + ([] if message else [earlier])
     return pl.pallas_call(
-        product_kernel,
-        out_shape=jax.ShapeDtypeStruct(
-            (rows * order, load_cases), jnp.bfloat16 if earlier else jnp.float32
-        ),
-        in_specs=[
-            pl.BlockSpec(memory_space=pltpu.SMEM),
-            vmem,
-            vmem,
-            *[vmem] * len(earlier),
-        ],
-        out_specs=vmem,
+        functools.partial(product_kernel, message, keep),
+        out_shape=outs,
+        in_specs=[pl.BlockSpec(memory_space=pltpu.SMEM)] + [vmem] * len(operands),
+        out_specs=[vmem] * len(outs),
         compiler_params=pltpu.CompilerParams(vmem_limit_bytes=16 * 1024 * 1024),
         cost_estimate=pl.CostEstimate(
             flops=2 * rows * count * order * order * load_cases,
             bytes_accessed=2 * rows * count * order * order,
             transcendentals=0,
         ),
-    )(columns, block_values, gathered, *earlier)
+    )(columns, *operands)
 
 
 def shifted(cells, distance):
@@ -215,6 +251,7 @@
     products, outs = (refs[:2], refs[2:]) if last else (refs[:1], refs[1:])
     sectors, rows, _ = current.shape
     step = 16
+    unscale = [jnp.exp2(-products[0][s, rows : rows + 1, :]) for s in range(sectors)]
 
     def one_group(group, carry):
         at = pl.ds(pl.multiple_of(group * step, step), step)
@@ -224,7 +261,9 @@
         residual = []
         for s in range(sectors):
             forcing = cosine[s] * wave_c + sine[s] * wave_s
-            product = sum(part[s, at, :].astype(jnp.float32) for part in products)
+            product = products[0][s, at, :] * unscale[s]
+            if last:
+                product = product + products[1][s, at, :].astype(jnp.float32)
             applied = (
                 table[DIAGONAL, s, at, :] * before[s]
                 - table[COUPLING, s, at, :] * (below[s] + above[s])
@@ -334,11 +373,14 @@
         last = iteration == ITERS - 1
         gathered, (table, current) = gather_pieces(rounded, (table, current))
         if last:
-            change = block_product(block_values[0], columns, gathered, product)
+            (change,) = block_product(block_values[0], columns, gathered, sectors, kept)
             products.append(swap(change.reshape(slice_shape)))
         else:
-            product = block_product(block_values[0], columns, gathered)
-            products = [swap(product.reshape(slice_shape))]
+            scaled, *kept = block_product(
+                block_values[0], columns, gathered, sectors, keep=iteration == ITERS - 2
+            )
+            kept = kept[0] if kept else None
+            products = [swap(scaled.astype(jnp.float16)).astype(jnp.float32)]
         outs = [jax.ShapeDtypeStruct(slice_shape, jnp.bfloat16)]
         if not last:
             outs.append(jax.ShapeDtypeStruct(slice_shape, jnp.float32))

time: 210 us -> 200 us (0.952)
  blocking collectives: 102 us -> 92 us
    all_to_all x6, blocking collectives: 102 us -> 92 us  [swap(): return lax.all_to_all(cells, 'sector', 0, 0, tiled=True)]
  transfers between devices with their start and end apart: 28 -> 28, of which waited for: 21 -> 22; matrix products, arithmetic and copies ran while one was open for 2% -> 3% of each run, Pallas kernels for 1% -> 1%
where the time goes in v5:
time: 200 us; the launch traced here: 199 us
  blocking collectives  92 us (46%)
  starting transfers between devices  42 us (21%)
  waiting for transfers between devices  38.9 us (19%)
  Pallas kernels  16.7 us (8%)
  local copies, waits for them, and re-layouts  5.43 us (3%)
  other arithmetic  2.1 us (1%)
    all_to_all x6, blocking collectives, swap(): return lax.all_to_all(cells, 'sector', 0, 0, tiled=True)  92 us
    ppermute x27, waiting for transfers between devices, fetch(): return lax.ppermute(block, 'row', row_peers(*shift))  33.9 us
    ppermute x27, starting transfers between devices, fetch(): return lax.ppermute(block, 'row', row_peers(*shift))  32 us
    pallas_call x3, Pallas kernels, block_product(): pl.pallas_call(functools.partial(product_kernel, message, keep), out_shap...  10.8 us
    all_to_all x1, starting transfers between devices, swap(): return lax.all_to_all(cells, 'sector', 0, 0, tiled=True)  9.94 us
    all_to_all x1, waiting for transfers between devices, swap(): return lax.all_to_all(cells, 'sector', 0, 0, tiled=True)  5.03 us
  transfers between devices with their start and end apart: 28, of which 22 were waited for; matrix products, arithmetic and copies ran while one was open for 3% of the time, Pallas kernels for 1%

profile of v5, /device:TPU:2, one launch (start us, length us, event | category | flops | bytes accessed | tf_op | source)
XLA Modules:
  0.0 199.0 jit_solution(2738744607657451176)
XLA Ops:
  1.3 9.9 %all-to-all-start = ((s32[16,1,1]{2,1,0:T(1,128)}), s32[16,1,1]{2,1,0:T(1,128)S(1)}, u32[]{:S(2)}, u32[]{:S(2)}) async-start(s32[16,1,1]{2,1,0:T(1,128)} %broadcast_in_dim.48), calls=%async_computation | async-start | bytes 16384 | tf_op jit(solution)/shard_map/all_to_all | solution.py:310
  13.2 5.0 %all-to-all-done = s32[16,1,1]{2,1,0:T(1,128)S(1)} async-done(((s32[16,1,1]{2,1,0:T(1,128)}), s32[16,1,1]{2,1,0:T(1,128)S(1)}, u32[]{:S(2)}, u32[]{:S(2)}) %all-to-all-start) | async-done | bytes 96 | tf_op jit(solution)/shard_map/all_to_all | solution.py:310
  19.9 3.1 %collective-permute-start.2 = (bf16[1024,128]{1,0:T(8,128)(2,1)S(1)}, bf16[1024,128]{1,0:T(8,128)(2,1)S(1)}, u32[]{:S(2)}, u32[]{:S(2)}) collective-permute-start(bf16[1024,128]{1,0:T(8,128)(2,1)S(1)} %get-tuple-element.32), channel_id=1, source_target_pairs={{2,0},{3,1},{4,2},{5,3},{6,4},{7,5},{0,6},{1,7},{10,8},{11,9},{12,... | collective-permute-start | bytes 786440 | tf_op jit(solution)/shard_map/ppermute | solution.py:41
  28.3 3.1 %collective-permute-done = bf16[1024,128]{1,0:T(8,128)(2,1)S(1)} collective-permute-done((bf16[1024,128]{1,0:T(8,128)(2,1)S(1)}, bf16[1024,128]{1,0:T(8,128)(2,1)S(1)}, u32[]{:S(2)}, u32[]{:S(2)}) %collective-permute-start) | collective-permute-done | bytes 262176 | tf_op jit(solution)/shard_map/ppermute | solution.py:41
  38.3 3.7 %collective-permute-done.5 = bf16[1024,128]{1,0:T(8,128)(2,1)S(1)} collective-permute-done((bf16[1024,128]{1,0:T(8,128)(2,1)S(1)}, bf16[1024,128]{1,0:T(8,128)(2,1)S(1)}, u32[]{:S(2)}, u32[]{:S(2)}) %collective-permute-start.5) | collective-permute-done | bytes 262176 | tf_op jit(solution)/shard_map/ppermute | solution.py:41
  42.6 2.3 %collective-permute-done.8 = bf16[4096,128]{1,0:T(8,128)(2,1)S(1)} collective-permute-done((bf16[4096,128]{1,0:T(8,128)(2,1)S(1)}, bf16[4096,128]{1,0:T(8,128)(2,1)S(1)}, u32[]{:S(2)}, u32[]{:S(2)}) %collective-permute-start.8) | collective-permute-done | bytes 1048608 | tf_op jit(solution)/shard_map/ppermute | solution.py:41
  45.0 3.7 %shard_map.93 = f32[16,72,128]{2,1,0:T(8,128)S(1)} custom-call(s32[64]{0:T(128)S(1)} %reshape.77.columns, bf16[4,16,256,256]{3,2,1,0:T(8,128)(2,1)S(1)} %bitcast.28, bf16[16384,128]{1,0:T(8,128)(2,1)S(1)} %constant_dynamic-update-slice_fusion.gathered), custom_call_target="tpu_custom_call" | custom-call | flops 1073741824 | bytes 8388608 | tf_op jit(solution)/shard_map/pallas_call | solution.py:135
  48.8 16.4 %all_to_all.36 = f16[16,72,128]{2,1,0:T(8,128)(2,1)S(1)} all-to-all(f16[16,72,128]{2,1,0:T(8,128)(2,1)S(1)} %convert_element_type.38), channel_id=1, replica_groups=mesh['sector'=16,'row'=16] {'sector'}, dimensions={0} | all-to-all | bytes 589824 | tf_op jit(solution)/shard_map/all_to_all | solution.py:310
  66.3 14.2 %all_to_all.37 = bf16[16,64,128]{2,1,0:T(8,128)(2,1)S(1)} all-to-all(bf16[16,64,128]{2,1,0:T(8,128)(2,1)S(1)} %get-tuple-element.39), channel_id=1, replica_groups=mesh['sector'=16,'row'=16] {'sector'}, dimensions={0} | all-to-all | bytes 524288 | tf_op jit(solution)/shard_map/all_to_all | solution.py:310
  82.6 2.2 %collective-permute-start.10 = (bf16[1024,128]{1,0:T(8,128)(2,1)S(1)}, bf16[1024,128]{1,0:T(8,128)(2,1)S(1)}, u32[]{:S(2)}, u32[]{:S(2)}) collective-permute-start(bf16[1024,128]{1,0:T(8,128)(2,1)S(1)} %bitcast.39), channel_id=1, source_target_pairs={{4,0},{5,1},{6,2},{7,3},{0,4},{1,5},{2,6},{3,7},{12,8},{13,9},{14,... | collective-permute-start | bytes 786440 | tf_op jit(solution)/shard_map/ppermute | solution.py:41
  84.8 2.4 %collective-permute-start.11 = (bf16[1024,128]{1,0:T(8,128)(2,1)S(1)}, bf16[1024,128]{1,0:T(8,128)(2,1)S(1)}, u32[]{:S(2)}, u32[]{:S(2)}) collective-permute-start(bf16[1024,128]{1,0:T(8,128)(2,1)S(1)} %bitcast.40), channel_id=1, source_target_pairs={{2,0},{3,1},{4,2},{5,3},{6,4},{7,5},{0,6},{1,7},{10,8},{11,9},{12,... | collective-permute-start | bytes 786440 | tf_op jit(solution)/shard_map/ppermute | solution.py:41
  88.4 2.2 %collective-permute-start.13 = (bf16[1024,128]{1,0:T(8,128)(2,1)S(1)}, bf16[1024,128]{1,0:T(8,128)(2,1)S(1)}, u32[]{:S(2)}, u32[]{:S(2)}) collective-permute-start(bf16[1024,128]{1,0:T(8,128)(2,1)S(1)} %collective-permute-done.9), channel_id=1, source_target_pairs={{2,0},{3,1},{4,2},{5,3},{6,4},{7,5},{0,6},{1,7},{10,8},{11,9},{12,... | collective-permute-start | bytes 786440 | tf_op jit(solution)/shard_map/ppermute | solution.py:41
  90.6 2.7 %collective-permute-done.10 = bf16[1024,128]{1,0:T(8,128)(2,1)S(1)} collective-permute-done((bf16[1024,128]{1,0:T(8,128)(2,1)S(1)}, bf16[1024,128]{1,0:T(8,128)(2,1)S(1)}, u32[]{:S(2)}, u32[]{:S(2)}) %collective-permute-start.10) | collective-permute-done | bytes 262176 | tf_op jit(solution)/shard_map/ppermute | solution.py:41
  102.2 2.3 %collective-permute-done.17 = bf16[4096,128]{1,0:T(8,128)(2,1)S(1)} collective-permute-done((bf16[4096,128]{1,0:T(8,128)(2,1)S(1)}, bf16[4096,128]{1,0:T(8,128)(2,1)S(1)}, u32[]{:S(2)}, u32[]{:S(2)}) %collective-permute-start.17) | collective-permute-done | bytes 1048608 | tf_op jit(solution)/shard_map/ppermute | solution.py:41
  104.6 3.7 %shard_map.95 = (f32[16,72,128]{2,1,0:T(8,128)S(1)}, f32[1024,128]{1,0:T(8,128)S(1)}) custom-call(s32[64]{0:T(128)S(1)} %reshape.77.columns, bf16[4,16,256,256]{3,2,1,0:T(8,128)(2,1)S(1)} %bitcast.29, bf16[16384,128]{1,0:T(8,128)(2,1)S(1)} %constant_dynamic-update-slice_fusion.15.gathered), custom_call_target="tpu_custom_call" | custom-call | flops 1073741824 | bytes 8388608 | tf_op jit(solution)/shard_map/pallas_call | solution.py:135
  108.3 16.5 %all_to_all.38 = f16[16,72,128]{2,1,0:T(8,128)(2,1)S(1)} all-to-all(f16[16,72,128]{2,1,0:T(8,128)(2,1)S(1)} %convert_element_type.40), channel_id=1, replica_groups=mesh['sector'=16,'row'=16] {'sector'}, dimensions={0} | all-to-all | bytes 589824 | tf_op jit(solution)/shard_map/all_to_all | solution.py:310
  126.0 14.5 %all_to_all.39 = bf16[16,64,128]{2,1,0:T(8,128)(2,1)S(1)} all-to-all(bf16[16,64,128]{2,1,0:T(8,128)(2,1)S(1)} %get-tuple-element.45), channel_id=1, replica_groups=mesh['sector'=16,'row'=16] {'sector'}, dimensions={0} | all-to-all | bytes 524288 | tf_op jit(solution)/shard_map/all_to_all | solution.py:310
  141.4 2.4 %collective-permute-start.19 = (bf16[1024,128]{1,0:T(8,128)(2,1)S(1)}, bf16[1024,128]{1,0:T(8,128)(2,1)S(1)}, u32[]{:S(2)}, u32[]{:S(2)}) collective-permute-start(bf16[1024,128]{1,0:T(8,128)(2,1)S(1)} %bitcast.34), channel_id=1, source_target_pairs={{4,0},{5,1},{6,2},{7,3},{0,4},{1,5},{2,6},{3,7},{12,8},{13,9},{14,... | collective-permute-start | bytes 786440 | tf_op jit(solution)/shard_map/ppermute | solution.py:41
  146.0 2.3 %collective-permute-done.18 = bf16[1024,128]{1,0:T(8,128)(2,1)S(1)} collective-permute-done((bf16[1024,128]{1,0:T(8,128)(2,1)S(1)}, bf16[1024,128]{1,0:T(8,128)(2,1)S(1)}, u32[]{:S(2)}, u32[]{:S(2)}) %collective-permute-start.18) | collective-permute-done | bytes 262176 | tf_op jit(solution)/shard_map/ppermute | solution.py:41
  152.2 2.6 %collective-permute-start.24 = (bf16[1024,128]{1,0:T(8,128)(2,1)S(1)}, bf16[1024,128]{1,0:T(8,128)(2,1)S(1)}, u32[]{:S(2)}, u32[]{:S(2)}) collective-permute-start(bf16[1024,128]{1,0:T(8,128)(2,1)S(1)} %collective-permute-done.19), channel_id=1, source_target_pairs={{8,0},{9,1},{10,2},{11,3},{12,4},{13,5},{14,6},{15,7},{0,8},{1,9},... | collective-permute-start | bytes 786440 | tf_op jit(solution)/shard_map/ppermute | solution.py:41
  160.6 2.3 %collective-permute-done.26 = bf16[4096,128]{1,0:T(8,128)(2,1)S(1)} collective-permute-done((bf16[4096,128]{1,0:T(8,128)(2,1)S(1)}, bf16[4096,128]{1,0:T(8,128)(2,1)S(1)}, u32[]{:S(2)}, u32[]{:S(2)}) %collective-permute-start.26) | collective-permute-done | bytes 1048608 | tf_op jit(solution)/shard_map/ppermute | solution.py:41
  163.0 3.4 %shard_map.97 = bf16[1024,128]{1,0:T(8,128)(2,1)S(1)} custom-call(s32[64]{0:T(128)S(1)} %reshape.77.columns, bf16[4,16,256,256]{3,2,1,0:T(8,128)(2,1)S(1)} %bitcast.30, bf16[16384,128]{1,0:T(8,128)(2,1)S(1)} %constant_dynamic-update-slice_fusion.30.gathered, f32[1024,128]{1,0:T(8,128)S(1)} %get-tuple-element.50.refs_0_), custom_call_target="tpu_custom_call" | custom-call | flops 1073741824 | bytes 8388608 | tf_op jit(solution)/shard_map/pallas_call | solution.py:135
  166.4 16.1 %all_to_all.40.refs_1_ = bf16[16,64,128]{2,1,0:T(8,128)(2,1)S(1)} all-to-all(bf16[16,64,128]{2,1,0:T(8,128)(2,1)S(1)} %bitcast.31), channel_id=1, replica_groups=mesh['sector'=16,'row'=16] {'sector'}, dimensions={0} | all-to-all | bytes 524288 | tf_op jit(solution)/shard_map/all_to_all | solution.py:310
  183.8 14.4 %all_to_all.41 = bf16[16,64,128]{2,1,0:T(8,128)(2,1)S(1)} all-to-all(bf16[16,64,128]{2,1,0:T(8,128)(2,1)S(1)} %shard_map.98), channel_id=1, replica_groups=mesh['sector'=16,'row'=16] {'sector'}, dimensions={0} | all-to-all | bytes 524288 | tf_op jit(solution)/shard_map/all_to_all | solution.py:310
  (113 shorter events, 45.7 us)
Async XLA Ops:
  1.3 17.0 %all-to-all-start = ((s32[16,1,1]{2,1,0:T(1,128)}), s32[16,1,1]{2,1,0:T(1,128)S(1)}, u32[]{:S(2)}, u32[]{:S(2)}) async-start(s32[16,1,1]{2,1,0:T(1,128)} %broadcast_in_dim.48), calls=%async_computation | async-start | bytes 16384 | tf_op jit(solution)/shard_map/all_to_all | solution.py:310
  19.9 16.0 %collective-permute-start.2 = (bf16[1024,128]{1,0:T(8,128)(2,1)S(1)}, bf16[1024,128]{1,0:T(8,128)(2,1)S(1)}, u32[]{:S(2)}, u32[]{:S(2)}) collective-permute-start(bf16[1024,128]{1,0:T(8,128)(2,1)S(1)} %get-tuple-element.32), channel_id=1, source_target_pairs={{2,0},{3,1},{4,2},{5,3},{6,4},{7,5},{0,6},{1,7},{10,8},{11,9},{12,... | collective-permute-start | bytes 786440 | tf_op jit(solution)/shard_map/ppermute | solution.py:41
  23.0 10.7 %collective-permute-start.1 = (bf16[1024,128]{1,0:T(8,128)(2,1)S(1)}, bf16[1024,128]{1,0:T(8,128)(2,1)S(1)}, u32[]{:S(2)}, u32[]{:S(2)}) collective-permute-start(bf16[1024,128]{1,0:T(8,128)(2,1)S(1)} %get-tuple-element.32), channel_id=1, source_target_pairs={{4,0},{5,1},{6,2},{7,3},{0,4},{1,5},{2,6},{3,7},{12,8},{13,9},{14,... | collective-permute-start | bytes 786440 | tf_op jit(solution)/shard_map/ppermute | solution.py:41
  23.6 7.9 %collective-permute-start = (bf16[1024,128]{1,0:T(8,128)(2,1)S(1)}, bf16[1024,128]{1,0:T(8,128)(2,1)S(1)}, u32[]{:S(2)}, u32[]{:S(2)}) collective-permute-start(bf16[1024,128]{1,0:T(8,128)(2,1)S(1)} %get-tuple-element.32), channel_id=1, source_target_pairs={{8,0},{9,1},{10,2},{11,3},{12,4},{13,5},{14,6},{15,7},{0,8},{1,9},... | collective-permute-start | bytes 786440 | tf_op jit(solution)/shard_map/ppermute | solution.py:41
  26.5 11.7 %collective-permute-start.3 = (bf16[1024,128]{1,0:T(8,128)(2,1)S(1)}, bf16[1024,128]{1,0:T(8,128)(2,1)S(1)}, u32[]{:S(2)}, u32[]{:S(2)}) collective-permute-start(bf16[1024,128]{1,0:T(8,128)(2,1)S(1)} %get-tuple-element.32), channel_id=1, source_target_pairs={{6,0},{7,1},{0,2},{1,3},{2,4},{3,5},{4,6},{5,7},{14,8},{15,9},{8,1... | collective-permute-start | bytes 786440 | tf_op jit(solution)/shard_map/ppermute | solution.py:41
  31.5 6.9 %collective-permute-start.4 = (bf16[1024,128]{1,0:T(8,128)(2,1)S(1)}, bf16[1024,128]{1,0:T(8,128)(2,1)S(1)}, u32[]{:S(2)}, u32[]{:S(2)}) collective-permute-start(bf16[1024,128]{1,0:T(8,128)(2,1)S(1)} %collective-permute-done), channel_id=1, source_target_pairs={{2,0},{3,1},{4,2},{5,3},{6,4},{7,5},{0,6},{1,7},{10,8},{11,9},{12,... | collective-permute-start | bytes 786440 | tf_op jit(solution)/shard_map/ppermute | solution.py:41
  32.5 9.5 %collective-permute-start.5 = (bf16[1024,128]{1,0:T(8,128)(2,1)S(1)}, bf16[1024,128]{1,0:T(8,128)(2,1)S(1)}, u32[]{:S(2)}, u32[]{:S(2)}) collective-permute-start(bf16[1024,128]{1,0:T(8,128)(2,1)S(1)} %collective-permute-done), channel_id=1, source_target_pairs={{6,0},{7,1},{0,2},{1,3},{2,4},{3,5},{4,6},{5,7},{14,8},{15,9},{8,1... | collective-permute-start | bytes 786440 | tf_op jit(solution)/shard_map/ppermute | solution.py:41
  33.6 8.4 %collective-permute-start.6 = (bf16[1024,128]{1,0:T(8,128)(2,1)S(1)}, bf16[1024,128]{1,0:T(8,128)(2,1)S(1)}, u32[]{:S(2)}, u32[]{:S(2)}) collective-permute-start(bf16[1024,128]{1,0:T(8,128)(2,1)S(1)} %collective-permute-done.1), channel_id=1, source_target_pairs={{8,0},{9,1},{10,2},{11,3},{12,4},{13,5},{14,6},{15,7},{0,8},{1,9},... | collective-permute-start | bytes 786440 | tf_op jit(solution)/shard_map/ppermute | solution.py:41
  37.6 4.9 %collective-permute-start.7 = (bf16[4096,128]{1,0:T(8,128)(2,1)S(1)}, bf16[4096,128]{1,0:T(8,128)(2,1)S(1)}, u32[]{:S(2)}, u32[]{:S(2)}) collective-permute-start(bf16[4096,128]{1,0:T(8,128)(2,1)S(1)} %pad_maximum_fusion), channel_id=1, source_target_pairs={{1,0},{0,1},{3,2},{2,3},{5,4},{4,5},{7,6},{6,7},{9,8},{8,9},{11,10... | collective-permute-start | bytes 3145736 | tf_op jit(solution)/shard_map/ppermute | solution.py:41
  80.5 7.9 %collective-permute-start.9 = (bf16[1024,128]{1,0:T(8,128)(2,1)S(1)}, bf16[1024,128]{1,0:T(8,128)(2,1)S(1)}, u32[]{:S(2)}, u32[]{:S(2)}) collective-permute-start(bf16[1024,128]{1,0:T(8,128)(2,1)S(1)} %bitcast.38), channel_id=1, source_target_pairs={{8,0},{9,1},{10,2},{11,3},{12,4},{13,5},{14,6},{15,7},{0,8},{1,9},... | collective-permute-start | bytes 786440 | tf_op jit(solution)/shard_map/ppermute | solution.py:41
  82.6 10.8 %collective-permute-start.10 = (bf16[1024,128]{1,0:T(8,128)(2,1)S(1)}, bf16[1024,128]{1,0:T(8,128)(2,1)S(1)}, u32[]{:S(2)}, u32[]{:S(2)}) collective-permute-start(bf16[1024,128]{1,0:T(8,128)(2,1)S(1)} %bitcast.39), channel_id=1, source_target_pairs={{4,0},{5,1},{6,2},{7,3},{0,4},{1,5},{2,6},{3,7},{12,8},{13,9},{14,... | collective-permute-start | bytes 786440 | tf_op jit(solution)/shard_map/ppermute | solution.py:41
  84.8 12.2 %collective-permute-start.11 = (bf16[1024,128]{1,0:T(8,128)(2,1)S(1)}, bf16[1024,128]{1,0:T(8,128)(2,1)S(1)}, u32[]{:S(2)}, u32[]{:S(2)}) collective-permute-start(bf16[1024,128]{1,0:T(8,128)(2,1)S(1)} %bitcast.40), channel_id=1, source_target_pairs={{2,0},{3,1},{4,2},{5,3},{6,4},{7,5},{0,6},{1,7},{10,8},{11,9},{12,... | collective-permute-start | bytes 786440 | tf_op jit(solution)/shard_map/ppermute | solution.py:41
  87.2 11.1 %collective-permute-start.12 = (bf16[1024,128]{1,0:T(8,128)(2,1)S(1)}, bf16[1024,128]{1,0:T(8,128)(2,1)S(1)}, u32[]{:S(2)}, u32[]{:S(2)}) collective-permute-start(bf16[1024,128]{1,0:T(8,128)(2,1)S(1)} %bitcast.41), channel_id=1, source_target_pairs={{6,0},{7,1},{0,2},{1,3},{2,4},{3,5},{4,6},{5,7},{14,8},{15,9},{8,1... | collective-permute-start | bytes 786440 | tf_op jit(solution)/shard_map/ppermute | solution.py:41
  88.4 11.5 %collective-permute-start.13 = (bf16[1024,128]{1,0:T(8,128)(2,1)S(1)}, bf16[1024,128]{1,0:T(8,128)(2,1)S(1)}, u32[]{:S(2)}, u32[]{:S(2)}) collective-permute-start(bf16[1024,128]{1,0:T(8,128)(2,1)S(1)} %collective-permute-done.9), channel_id=1, source_target_pairs={{2,0},{3,1},{4,2},{5,3},{6,4},{7,5},{0,6},{1,7},{10,8},{11,9},{12,... | collective-permute-start | bytes 786440 | tf_op jit(solution)/shard_map/ppermute | solution.py:41
  90.6 11.0 %collective-permute-start.14 = (bf16[1024,128]{1,0:T(8,128)(2,1)S(1)}, bf16[1024,128]{1,0:T(8,128)(2,1)S(1)}, u32[]{:S(2)}, u32[]{:S(2)}) collective-permute-start(bf16[1024,128]{1,0:T(8,128)(2,1)S(1)} %collective-permute-done.9), channel_id=1, source_target_pairs={{6,0},{7,1},{0,2},{1,3},{2,4},{3,5},{4,6},{5,7},{14,8},{15,9},{8,1... | collective-permute-start | bytes 786440 | tf_op jit(solution)/shard_map/ppermute | solution.py:41
  93.3 8.3 %collective-permute-start.15 = (bf16[1024,128]{1,0:T(8,128)(2,1)S(1)}, bf16[1024,128]{1,0:T(8,128)(2,1)S(1)}, u32[]{:S(2)}, u32[]{:S(2)}) collective-permute-start(bf16[1024,128]{1,0:T(8,128)(2,1)S(1)} %collective-permute-done.10), channel_id=1, source_target_pairs={{8,0},{9,1},{10,2},{11,3},{12,4},{13,5},{14,6},{15,7},{0,8},{1,9},... | collective-permute-start | bytes 786440 | tf_op jit(solution)/shard_map/ppermute | solution.py:41
  97.1 4.9 %collective-permute-start.16 = (bf16[4096,128]{1,0:T(8,128)(2,1)S(1)}, bf16[4096,128]{1,0:T(8,128)(2,1)S(1)}, u32[]{:S(2)}, u32[]{:S(2)}) collective-permute-start(bf16[4096,128]{1,0:T(8,128)(2,1)S(1)} %get-tuple-element.43), channel_id=1, source_target_pairs={{1,0},{0,1},{3,2},{2,3},{5,4},{4,5},{7,6},{6,7},{9,8},{8,9},{11,10... | collective-permute-start | bytes 3145736 | tf_op jit(solution)/shard_map/ppermute | solution.py:41
  140.4 7.9 %collective-permute-start.18 = (bf16[1024,128]{1,0:T(8,128)(2,1)S(1)}, bf16[1024,128]{1,0:T(8,128)(2,1)S(1)}, u32[]{:S(2)}, u32[]{:S(2)}) collective-permute-start(bf16[1024,128]{1,0:T(8,128)(2,1)S(1)} %bitcast.33), channel_id=1, source_target_pairs={{8,0},{9,1},{10,2},{11,3},{12,4},{13,5},{14,6},{15,7},{0,8},{1,9},... | collective-permute-start | bytes 786440 | tf_op jit(solution)/shard_map/ppermute | solution.py:41
  141.4 10.7 %collective-permute-start.19 = (bf16[1024,128]{1,0:T(8,128)(2,1)S(1)}, bf16[1024,128]{1,0:T(8,128)(2,1)S(1)}, u32[]{:S(2)}, u32[]{:S(2)}) collective-permute-start(bf16[1024,128]{1,0:T(8,128)(2,1)S(1)} %bitcast.34), channel_id=1, source_target_pairs={{4,0},{5,1},{6,2},{7,3},{0,4},{1,5},{2,6},{3,7},{12,8},{13,9},{14,... | collective-permute-start | bytes 786440 | tf_op jit(solution)/shard_map/ppermute | solution.py:41
  143.9 12.0 %collective-permute-start.20 = (bf16[1024,128]{1,0:T(8,128)(2,1)S(1)}, bf16[1024,128]{1,0:T(8,128)(2,1)S(1)}, u32[]{:S(2)}, u32[]{:S(2)}) collective-permute-start(bf16[1024,128]{1,0:T(8,128)(2,1)S(1)} %bitcast.35), channel_id=1, source_target_pairs={{2,0},{3,1},{4,2},{5,3},{6,4},{7,5},{0,6},{1,7},{10,8},{11,9},{12,... | collective-permute-start | bytes 786440 | tf_op jit(solution)/shard_map/ppermute | solution.py:41
  145.1 11.6 %collective-permute-start.21 = (bf16[1024,128]{1,0:T(8,128)(2,1)S(1)}, bf16[1024,128]{1,0:T(8,128)(2,1)S(1)}, u32[]{:S(2)}, u32[]{:S(2)}) collective-permute-start(bf16[1024,128]{1,0:T(8,128)(2,1)S(1)} %bitcast.36), channel_id=1, source_target_pairs={{6,0},{7,1},{0,2},{1,3},{2,4},{3,5},{4,6},{5,7},{14,8},{15,9},{8,1... | collective-permute-start | bytes 786440 | tf_op jit(solution)/shard_map/ppermute | solution.py:41
  148.3 10.3 %collective-permute-start.22 = (bf16[1024,128]{1,0:T(8,128)(2,1)S(1)}, bf16[1024,128]{1,0:T(8,128)(2,1)S(1)}, u32[]{:S(2)}, u32[]{:S(2)}) collective-permute-start(bf16[1024,128]{1,0:T(8,128)(2,1)S(1)} %collective-permute-done.18), channel_id=1, source_target_pairs={{2,0},{3,1},{4,2},{5,3},{6,4},{7,5},{0,6},{1,7},{10,8},{11,9},{12,... | collective-permute-start | bytes 786440 | tf_op jit(solution)/shard_map/ppermute | solution.py:41
  149.9 10.1 %collective-permute-start.23 = (bf16[1024,128]{1,0:T(8,128)(2,1)S(1)}, bf16[1024,128]{1,0:T(8,128)(2,1)S(1)}, u32[]{:S(2)}, u32[]{:S(2)}) collective-permute-start(bf16[1024,128]{1,0:T(8,128)(2,1)S(1)} %collective-permute-done.18), channel_id=1, source_target_pairs={{6,0},{7,1},{0,2},{1,3},{2,4},{3,5},{4,6},{5,7},{14,8},{15,9},{8,1... | collective-permute-start | bytes 786440 | tf_op jit(solution)/shard_map/ppermute | solution.py:41
  152.2 7.9 %collective-permute-start.24 = (bf16[1024,128]{1,0:T(8,128)(2,1)S(1)}, bf16[1024,128]{1,0:T(8,128)(2,1)S(1)}, u32[]{:S(2)}, u32[]{:S(2)}) collective-permute-start(bf16[1024,128]{1,0:T(8,128)(2,1)S(1)} %collective-permute-done.19), channel_id=1, source_target_pairs={{8,0},{9,1},{10,2},{11,3},{12,4},{13,5},{14,6},{15,7},{0,8},{1,9},... | collective-permute-start | bytes 786440 | tf_op jit(solution)/shard_map/ppermute | solution.py:41
  (8 other events, 66.5 us)

commit v6 on v5

--- a/solution.py
+++ b/solution.py
@@ -40,8 +40,9 @@
     def fetch(block, *shift):
         return lax.ppermute(block, "row", row_peers(*shift))
 
-    across = fetch(own, 1, 0, 0)
-    opposite, above, below = fetch(own, 0, 2, 0), fetch(own, 0, 1, 0), fetch(own, 0, 3, 0)
+    opposite, across = fetch(own, 0, 2, 0), fetch(own, 1, 0, 0)
+    above, below = fetch(own, 0, 1, 0), fetch(own, 0, 3, 0)
+    opposite, across = lax.optimization_barrier((opposite, across))
     relayed = [fetch(across, 0, 1, 0), fetch(across, 0, 3, 0), fetch(opposite, 1, 0, 0)]
     direct = [own, across, opposite, above, below]
     order = direct + relayed

time: 200 us -> 203 us (1.015)
  starting transfers between devices: 42 us -> 46.1 us
    ppermute x27, starting transfers between devices: 32 us -> 36.2 us  [fetch(): return lax.ppermute(block, 'row', row_peers(*shift))]
  transfers between devices with their start and end apart: 28 -> 28, of which waited for: 22 -> 17; matrix products, arithmetic and copies ran while one was open for 3% -> 3% of each run, Pallas kernels for 1% -> 1%
where the time goes in v6:
time: 203 us; the launch traced here: 202 us
  blocking collectives  90.7 us (45%)
  starting transfers between devices  46.1 us (23%)
  waiting for transfers between devices  38.8 us (19%)
  Pallas kernels  16.7 us (8%)
  local copies, waits for them, and re-layouts  5.43 us (3%)
  other arithmetic  2.1 us (1%)
    all_to_all x6, blocking collectives, swap(): return lax.all_to_all(cells, 'sector', 0, 0, tiled=True)  90.7 us
    ppermute x27, starting transfers between devices, fetch(): return lax.ppermute(block, 'row', row_peers(*shift))  36.2 us
    ppermute x27, waiting for transfers between devices, fetch(): return lax.ppermute(block, 'row', row_peers(*shift))  33.7 us
    pallas_call x3, Pallas kernels, block_product(): pl.pallas_call(functools.partial(product_kernel, message, keep), out_shap...  10.8 us
    all_to_all x1, starting transfers between devices, swap(): return lax.all_to_all(cells, 'sector', 0, 0, tiled=True)  9.94 us
    all_to_all x1, waiting for transfers between devices, swap(): return lax.all_to_all(cells, 'sector', 0, 0, tiled=True)  5.03 us
  transfers between devices with their start and end apart: 28, of which 17 were waited for; matrix products, arithmetic and copies ran while one was open for 3% of the time, Pallas kernels for 1%

profile of v6, /device:TPU:2, one launch (start us, length us, event | category | flops | bytes accessed | tf_op | source)
XLA Modules:
  0.0 201.8 jit_solution(15685229043792157402)
XLA Ops:
  1.3 9.9 %all-to-all-start = ((s32[16,1,1]{2,1,0:T(1,128)}), s32[16,1,1]{2,1,0:T(1,128)S(1)}, u32[]{:S(2)}, u32[]{:S(2)}) async-start(s32[16,1,1]{2,1,0:T(1,128)} %broadcast_in_dim.48), calls=%async_computation | async-start | bytes 16384 | tf_op jit(solution)/shard_map/all_to_all | solution.py:311
  13.2 5.0 %all-to-all-done = s32[16,1,1]{2,1,0:T(1,128)S(1)} async-done(((s32[16,1,1]{2,1,0:T(1,128)}), s32[16,1,1]{2,1,0:T(1,128)S(1)}, u32[]{:S(2)}, u32[]{:S(2)}) %all-to-all-start) | async-done | bytes 96 | tf_op jit(solution)/shard_map/all_to_all | solution.py:311
  19.9 3.1 %collective-permute-start.2 = (bf16[1024,128]{1,0:T(8,128)(2,1)S(1)}, bf16[1024,128]{1,0:T(8,128)(2,1)S(1)}, u32[]{:S(2)}, u32[]{:S(2)}) collective-permute-start(bf16[1024,128]{1,0:T(8,128)(2,1)S(1)} %get-tuple-element.38), channel_id=1, source_target_pairs={{2,0},{3,1},{4,2},{5,3},{6,4},{7,5},{0,6},{1,7},{10,8},{11,9},{12,... | collective-permute-start | bytes 786440 | tf_op jit(solution)/shard_map/ppermute | solution.py:41
  28.3 5.3 %collective-permute-done = bf16[1024,128]{1,0:T(8,128)(2,1)S(1)} collective-permute-done((bf16[1024,128]{1,0:T(8,128)(2,1)S(1)}, bf16[1024,128]{1,0:T(8,128)(2,1)S(1)}, u32[]{:S(2)}, u32[]{:S(2)}) %collective-permute-start) | collective-permute-done | bytes 262176 | tf_op jit(solution)/shard_map/ppermute | solution.py:41
  40.0 2.6 %collective-permute-done.5 = bf16[1024,128]{1,0:T(8,128)(2,1)S(1)} collective-permute-done((bf16[1024,128]{1,0:T(8,128)(2,1)S(1)}, bf16[1024,128]{1,0:T(8,128)(2,1)S(1)}, u32[]{:S(2)}, u32[]{:S(2)}) %collective-permute-start.5) | collective-permute-done | bytes 262176 | tf_op jit(solution)/shard_map/ppermute | solution.py:41
  46.5 3.7 %shard_map.93 = f32[16,72,128]{2,1,0:T(8,128)S(1)} custom-call(s32[64]{0:T(128)S(1)} %reshape.77.columns, bf16[4,16,256,256]{3,2,1,0:T(8,128)(2,1)S(1)} %bitcast.28, bf16[16384,128]{1,0:T(8,128)(2,1)S(1)} %constant_dynamic-update-slice_fusion.gathered), custom_call_target="tpu_custom_call" | custom-call | flops 1073741824 | bytes 8388608 | tf_op jit(solution)/shard_map/pallas_call | solution.py:136
  50.3 16.1 %all_to_all.36 = f16[16,72,128]{2,1,0:T(8,128)(2,1)S(1)} all-to-all(f16[16,72,128]{2,1,0:T(8,128)(2,1)S(1)} %convert_element_type.38), channel_id=1, replica_groups=mesh['sector'=16,'row'=16] {'sector'}, dimensions={0} | all-to-all | bytes 589824 | tf_op jit(solution)/shard_map/all_to_all | solution.py:311
  67.5 14.2 %all_to_all.37 = bf16[16,64,128]{2,1,0:T(8,128)(2,1)S(1)} all-to-all(bf16[16,64,128]{2,1,0:T(8,128)(2,1)S(1)} %get-tuple-element.47), channel_id=1, replica_groups=mesh['sector'=16,'row'=16] {'sector'}, dimensions={0} | all-to-all | bytes 524288 | tf_op jit(solution)/shard_map/all_to_all | solution.py:311
  85.9 2.6 %collective-permute-start.11 = (bf16[1024,128]{1,0:T(8,128)(2,1)S(1)}, bf16[1024,128]{1,0:T(8,128)(2,1)S(1)}, u32[]{:S(2)}, u32[]{:S(2)}) collective-permute-start(bf16[1024,128]{1,0:T(8,128)(2,1)S(1)} %bitcast.40), channel_id=1, source_target_pairs={{2,0},{3,1},{4,2},{5,3},{6,4},{7,5},{0,6},{1,7},{10,8},{11,9},{12,... | collective-permute-start | bytes 786440 | tf_op jit(solution)/shard_map/ppermute | solution.py:41
  88.6 3.1 %collective-permute-done.9 = bf16[1024,128]{1,0:T(8,128)(2,1)S(1)} collective-permute-done((bf16[1024,128]{1,0:T(8,128)(2,1)S(1)}, bf16[1024,128]{1,0:T(8,128)(2,1)S(1)}, u32[]{:S(2)}, u32[]{:S(2)}) %collective-permute-start.9) | collective-permute-done | bytes 262176 | tf_op jit(solution)/shard_map/ppermute | solution.py:41
  91.8 3.5 %collective-permute-start.13 = (bf16[1024,128]{1,0:T(8,128)(2,1)S(1)}, bf16[1024,128]{1,0:T(8,128)(2,1)S(1)}, u32[]{:S(2)}, u32[]{:S(2)}) collective-permute-start(bf16[1024,128]{1,0:T(8,128)(2,1)S(1)} %collective-permute-done.10), channel_id=1, source_target_pairs={{2,0},{3,1},{4,2},{5,3},{6,4},{7,5},{0,6},{1,7},{10,8},{11,9},{12,... | collective-permute-start | bytes 786440 | tf_op jit(solution)/shard_map/ppermute | solution.py:41
  100.2 2.6 %collective-permute-done.14 = bf16[1024,128]{1,0:T(8,128)(2,1)S(1)} collective-permute-done((bf16[1024,128]{1,0:T(8,128)(2,1)S(1)}, bf16[1024,128]{1,0:T(8,128)(2,1)S(1)}, u32[]{:S(2)}, u32[]{:S(2)}) %collective-permute-start.14) | collective-permute-done | bytes 262176 | tf_op jit(solution)/shard_map/ppermute | solution.py:41
  103.6 2.3 %collective-permute-done.17 = bf16[4096,128]{1,0:T(8,128)(2,1)S(1)} collective-permute-done((bf16[4096,128]{1,0:T(8,128)(2,1)S(1)}, bf16[4096,128]{1,0:T(8,128)(2,1)S(1)}, u32[]{:S(2)}, u32[]{:S(2)}) %collective-permute-start.17) | collective-permute-done | bytes 1048608 | tf_op jit(solution)/shard_map/ppermute | solution.py:41
  106.1 3.7 %shard_map.95 = (f32[16,72,128]{2,1,0:T(8,128)S(1)}, f32[1024,128]{1,0:T(8,128)S(1)}) custom-call(s32[64]{0:T(128)S(1)} %reshape.77.columns, bf16[4,16,256,256]{3,2,1,0:T(8,128)(2,1)S(1)} %bitcast.29, bf16[16384,128]{1,0:T(8,128)(2,1)S(1)} %constant_dynamic-update-slice_fusion.15.gathered), custom_call_target="tpu_custom_call" | custom-call | flops 1073741824 | bytes 8388608 | tf_op jit(solution)/shard_map/pallas_call | solution.py:136
  109.8 16.4 %all_to_all.38 = f16[16,72,128]{2,1,0:T(8,128)(2,1)S(1)} all-to-all(f16[16,72,128]{2,1,0:T(8,128)(2,1)S(1)} %convert_element_type.40), channel_id=1, replica_groups=mesh['sector'=16,'row'=16] {'sector'}, dimensions={0} | all-to-all | bytes 589824 | tf_op jit(solution)/shard_map/all_to_all | solution.py:311
  127.4 14.2 %all_to_all.39 = bf16[16,64,128]{2,1,0:T(8,128)(2,1)S(1)} all-to-all(bf16[16,64,128]{2,1,0:T(8,128)(2,1)S(1)} %get-tuple-element.55), channel_id=1, replica_groups=mesh['sector'=16,'row'=16] {'sector'}, dimensions={0} | all-to-all | bytes 524288 | tf_op jit(solution)/shard_map/all_to_all | solution.py:311
  145.2 2.5 %collective-permute-start.20 = (bf16[1024,128]{1,0:T(8,128)(2,1)S(1)}, bf16[1024,128]{1,0:T(8,128)(2,1)S(1)}, u32[]{:S(2)}, u32[]{:S(2)}) collective-permute-start(bf16[1024,128]{1,0:T(8,128)(2,1)S(1)} %bitcast.35), channel_id=1, source_target_pairs={{2,0},{3,1},{4,2},{5,3},{6,4},{7,5},{0,6},{1,7},{10,8},{11,9},{12,... | collective-permute-start | bytes 786440 | tf_op jit(solution)/shard_map/ppermute | solution.py:41
  147.9 3.8 %collective-permute-done.18 = bf16[1024,128]{1,0:T(8,128)(2,1)S(1)} collective-permute-done((bf16[1024,128]{1,0:T(8,128)(2,1)S(1)}, bf16[1024,128]{1,0:T(8,128)(2,1)S(1)}, u32[]{:S(2)}, u32[]{:S(2)}) %collective-permute-start.18) | collective-permute-done | bytes 262176 | tf_op jit(solution)/shard_map/ppermute | solution.py:41
  151.7 3.9 %collective-permute-start.22 = (bf16[1024,128]{1,0:T(8,128)(2,1)S(1)}, bf16[1024,128]{1,0:T(8,128)(2,1)S(1)}, u32[]{:S(2)}, u32[]{:S(2)}) collective-permute-start(bf16[1024,128]{1,0:T(8,128)(2,1)S(1)} %collective-permute-done.19), channel_id=1, source_target_pairs={{2,0},{3,1},{4,2},{5,3},{6,4},{7,5},{0,6},{1,7},{10,8},{11,9},{12,... | collective-permute-start | bytes 786440 | tf_op jit(solution)/shard_map/ppermute | solution.py:41
  158.1 2.5 %collective-permute-done.22 = bf16[1024,128]{1,0:T(8,128)(2,1)S(1)} collective-permute-done((bf16[1024,128]{1,0:T(8,128)(2,1)S(1)}, bf16[1024,128]{1,0:T(8,128)(2,1)S(1)}, u32[]{:S(2)}, u32[]{:S(2)}) %collective-permute-start.22) | collective-permute-done | bytes 262176 | tf_op jit(solution)/shard_map/ppermute | solution.py:41
  160.5 2.6 %collective-permute-done.23 = bf16[1024,128]{1,0:T(8,128)(2,1)S(1)} collective-permute-done((bf16[1024,128]{1,0:T(8,128)(2,1)S(1)}, bf16[1024,128]{1,0:T(8,128)(2,1)S(1)}, u32[]{:S(2)}, u32[]{:S(2)}) %collective-permute-start.23) | collective-permute-done | bytes 262176 | tf_op jit(solution)/shard_map/ppermute | solution.py:41
  166.4 3.4 %shard_map.97 = bf16[1024,128]{1,0:T(8,128)(2,1)S(1)} custom-call(s32[64]{0:T(128)S(1)} %reshape.77.columns, bf16[4,16,256,256]{3,2,1,0:T(8,128)(2,1)S(1)} %bitcast.30, bf16[16384,128]{1,0:T(8,128)(2,1)S(1)} %constant_dynamic-update-slice_fusion.30.gathered, f32[1024,128]{1,0:T(8,128)S(1)} %get-tuple-element.62.refs_0_), custom_call_target="tpu_custom_call" | custom-call | flops 1073741824 | bytes 8388608 | tf_op jit(solution)/shard_map/pallas_call | solution.py:136
  169.9 15.1 %all_to_all.40.refs_1_ = bf16[16,64,128]{2,1,0:T(8,128)(2,1)S(1)} all-to-all(bf16[16,64,128]{2,1,0:T(8,128)(2,1)S(1)} %bitcast.31), channel_id=1, replica_groups=mesh['sector'=16,'row'=16] {'sector'}, dimensions={0} | all-to-all | bytes 524288 | tf_op jit(solution)/shard_map/all_to_all | solution.py:311
  186.1 14.8 %all_to_all.41 = bf16[16,64,128]{2,1,0:T(8,128)(2,1)S(1)} all-to-all(bf16[16,64,128]{2,1,0:T(8,128)(2,1)S(1)} %shard_map.98), channel_id=1, replica_groups=mesh['sector'=16,'row'=16] {'sector'}, dimensions={0} | all-to-all | bytes 524288 | tf_op jit(solution)/shard_map/all_to_all | solution.py:311
  (113 shorter events, 43.0 us)
Async XLA Ops:
  1.3 17.0 %all-to-all-start = ((s32[16,1,1]{2,1,0:T(1,128)}), s32[16,1,1]{2,1,0:T(1,128)S(1)}, u32[]{:S(2)}, u32[]{:S(2)}) async-start(s32[16,1,1]{2,1,0:T(1,128)} %broadcast_in_dim.48), calls=%async_computation | async-start | bytes 16384 | tf_op jit(solution)/shard_map/all_to_all | solution.py:311
  19.9 17.9 %collective-permute-start.2 = (bf16[1024,128]{1,0:T(8,128)(2,1)S(1)}, bf16[1024,128]{1,0:T(8,128)(2,1)S(1)}, u32[]{:S(2)}, u32[]{:S(2)}) collective-permute-start(bf16[1024,128]{1,0:T(8,128)(2,1)S(1)} %get-tuple-element.38), channel_id=1, source_target_pairs={{2,0},{3,1},{4,2},{5,3},{6,4},{7,5},{0,6},{1,7},{10,8},{11,9},{12,... | collective-permute-start | bytes 786440 | tf_op jit(solution)/shard_map/ppermute | solution.py:41
  23.0 10.7 %collective-permute-start = (bf16[1024,128]{1,0:T(8,128)(2,1)S(1)}, bf16[1024,128]{1,0:T(8,128)(2,1)S(1)}, u32[]{:S(2)}, u32[]{:S(2)}) collective-permute-start(bf16[1024,128]{1,0:T(8,128)(2,1)S(1)} %get-tuple-element.38), channel_id=1, source_target_pairs={{4,0},{5,1},{6,2},{7,3},{0,4},{1,5},{2,6},{3,7},{12,8},{13,9},{14,... | collective-permute-start | bytes 786440 | tf_op jit(solution)/shard_map/ppermute | solution.py:41
  23.6 10.0 %collective-permute-start.1 = (bf16[1024,128]{1,0:T(8,128)(2,1)S(1)}, bf16[1024,128]{1,0:T(8,128)(2,1)S(1)}, u32[]{:S(2)}, u32[]{:S(2)}) collective-permute-start(bf16[1024,128]{1,0:T(8,128)(2,1)S(1)} %get-tuple-element.38), channel_id=1, source_target_pairs={{8,0},{9,1},{10,2},{11,3},{12,4},{13,5},{14,6},{15,7},{0,8},{1,9},... | collective-permute-start | bytes 786440 | tf_op jit(solution)/shard_map/ppermute | solution.py:41
  26.5 13.3 %collective-permute-start.3 = (bf16[1024,128]{1,0:T(8,128)(2,1)S(1)}, bf16[1024,128]{1,0:T(8,128)(2,1)S(1)}, u32[]{:S(2)}, u32[]{:S(2)}) collective-permute-start(bf16[1024,128]{1,0:T(8,128)(2,1)S(1)} %get-tuple-element.38), channel_id=1, source_target_pairs={{6,0},{7,1},{0,2},{1,3},{2,4},{3,5},{4,6},{5,7},{14,8},{15,9},{8,1... | collective-permute-start | bytes 786440 | tf_op jit(solution)/shard_map/ppermute | solution.py:41
  33.6 6.4 %collective-permute-start.4 = (bf16[1024,128]{1,0:T(8,128)(2,1)S(1)}, bf16[1024,128]{1,0:T(8,128)(2,1)S(1)}, u32[]{:S(2)}, u32[]{:S(2)}) collective-permute-start(bf16[1024,128]{1,0:T(8,128)(2,1)S(1)} %collective-permute-done.1), channel_id=1, source_target_pairs={{2,0},{3,1},{4,2},{5,3},{6,4},{7,5},{0,6},{1,7},{10,8},{11,9},{12,... | collective-permute-start | bytes 786440 | tf_op jit(solution)/shard_map/ppermute | solution.py:41
  35.0 7.6 %collective-permute-start.5 = (bf16[1024,128]{1,0:T(8,128)(2,1)S(1)}, bf16[1024,128]{1,0:T(8,128)(2,1)S(1)}, u32[]{:S(2)}, u32[]{:S(2)}) collective-permute-start(bf16[1024,128]{1,0:T(8,128)(2,1)S(1)} %collective-permute-done.1), channel_id=1, source_target_pairs={{6,0},{7,1},{0,2},{1,3},{2,4},{3,5},{4,6},{5,7},{14,8},{15,9},{8,1... | collective-permute-start | bytes 786440 | tf_op jit(solution)/shard_map/ppermute | solution.py:41
  35.7 7.9 %collective-permute-start.6 = (bf16[1024,128]{1,0:T(8,128)(2,1)S(1)}, bf16[1024,128]{1,0:T(8,128)(2,1)S(1)}, u32[]{:S(2)}, u32[]{:S(2)}) collective-permute-start(bf16[1024,128]{1,0:T(8,128)(2,1)S(1)} %collective-permute-done), channel_id=1, source_target_pairs={{8,0},{9,1},{10,2},{11,3},{12,4},{13,5},{14,6},{15,7},{0,8},{1,9},... | collective-permute-start | bytes 786440 | tf_op jit(solution)/shard_map/ppermute | solution.py:41
  81.7 10.1 %collective-permute-start.9 = (bf16[1024,128]{1,0:T(8,128)(2,1)S(1)}, bf16[1024,128]{1,0:T(8,128)(2,1)S(1)}, u32[]{:S(2)}, u32[]{:S(2)}) collective-permute-start(bf16[1024,128]{1,0:T(8,128)(2,1)S(1)} %bitcast.38), channel_id=1, source_target_pairs={{4,0},{5,1},{6,2},{7,3},{0,4},{1,5},{2,6},{3,7},{12,8},{13,9},{14,... | collective-permute-start | bytes 786440 | tf_op jit(solution)/shard_map/ppermute | solution.py:41
  83.8 8.0 %collective-permute-start.10 = (bf16[1024,128]{1,0:T(8,128)(2,1)S(1)}, bf16[1024,128]{1,0:T(8,128)(2,1)S(1)}, u32[]{:S(2)}, u32[]{:S(2)}) collective-permute-start(bf16[1024,128]{1,0:T(8,128)(2,1)S(1)} %bitcast.39), channel_id=1, source_target_pairs={{8,0},{9,1},{10,2},{11,3},{12,4},{13,5},{14,6},{15,7},{0,8},{1,9},... | collective-permute-start | bytes 786440 | tf_op jit(solution)/shard_map/ppermute | solution.py:41
  85.9 11.6 %collective-permute-start.11 = (bf16[1024,128]{1,0:T(8,128)(2,1)S(1)}, bf16[1024,128]{1,0:T(8,128)(2,1)S(1)}, u32[]{:S(2)}, u32[]{:S(2)}) collective-permute-start(bf16[1024,128]{1,0:T(8,128)(2,1)S(1)} %bitcast.40), channel_id=1, source_target_pairs={{2,0},{3,1},{4,2},{5,3},{6,4},{7,5},{0,6},{1,7},{10,8},{11,9},{12,... | collective-permute-start | bytes 786440 | tf_op jit(solution)/shard_map/ppermute | solution.py:41
  88.5 9.6 %collective-permute-start.12 = (bf16[1024,128]{1,0:T(8,128)(2,1)S(1)}, bf16[1024,128]{1,0:T(8,128)(2,1)S(1)}, u32[]{:S(2)}, u32[]{:S(2)}) collective-permute-start(bf16[1024,128]{1,0:T(8,128)(2,1)S(1)} %bitcast.41), channel_id=1, source_target_pairs={{6,0},{7,1},{0,2},{1,3},{2,4},{3,5},{4,6},{5,7},{14,8},{15,9},{8,1... | collective-permute-start | bytes 786440 | tf_op jit(solution)/shard_map/ppermute | solution.py:41
  91.8 8.4 %collective-permute-start.13 = (bf16[1024,128]{1,0:T(8,128)(2,1)S(1)}, bf16[1024,128]{1,0:T(8,128)(2,1)S(1)}, u32[]{:S(2)}, u32[]{:S(2)}) collective-permute-start(bf16[1024,128]{1,0:T(8,128)(2,1)S(1)} %collective-permute-done.10), channel_id=1, source_target_pairs={{2,0},{3,1},{4,2},{5,3},{6,4},{7,5},{0,6},{1,7},{10,8},{11,9},{12,... | collective-permute-start | bytes 786440 | tf_op jit(solution)/shard_map/ppermute | solution.py:41
  95.2 7.6 %collective-permute-start.14 = (bf16[1024,128]{1,0:T(8,128)(2,1)S(1)}, bf16[1024,128]{1,0:T(8,128)(2,1)S(1)}, u32[]{:S(2)}, u32[]{:S(2)}) collective-permute-start(bf16[1024,128]{1,0:T(8,128)(2,1)S(1)} %collective-permute-done.10), channel_id=1, source_target_pairs={{6,0},{7,1},{0,2},{1,3},{2,4},{3,5},{4,6},{5,7},{14,8},{15,9},{8,1... | collective-permute-start | bytes 786440 | tf_op jit(solution)/shard_map/ppermute | solution.py:41
  95.2 7.9 %collective-permute-start.15 = (bf16[1024,128]{1,0:T(8,128)(2,1)S(1)}, bf16[1024,128]{1,0:T(8,128)(2,1)S(1)}, u32[]{:S(2)}, u32[]{:S(2)}) collective-permute-start(bf16[1024,128]{1,0:T(8,128)(2,1)S(1)} %collective-permute-done.9), channel_id=1, source_target_pairs={{8,0},{9,1},{10,2},{11,3},{12,4},{13,5},{14,6},{15,7},{0,8},{1,9},... | collective-permute-start | bytes 786440 | tf_op jit(solution)/shard_map/ppermute | solution.py:41
  97.6 5.9 %collective-permute-start.16 = (bf16[4096,128]{1,0:T(8,128)(2,1)S(1)}, bf16[4096,128]{1,0:T(8,128)(2,1)S(1)}, u32[]{:S(2)}, u32[]{:S(2)}) collective-permute-start(bf16[4096,128]{1,0:T(8,128)(2,1)S(1)} %get-tuple-element.53), channel_id=1, source_target_pairs={{1,0},{0,1},{3,2},{2,3},{5,4},{4,5},{7,6},{6,7},{9,8},{8,9},{11,10... | collective-permute-start | bytes 3145736 | tf_op jit(solution)/shard_map/ppermute | solution.py:41
  141.6 10.1 %collective-permute-start.18 = (bf16[1024,128]{1,0:T(8,128)(2,1)S(1)}, bf16[1024,128]{1,0:T(8,128)(2,1)S(1)}, u32[]{:S(2)}, u32[]{:S(2)}) collective-permute-start(bf16[1024,128]{1,0:T(8,128)(2,1)S(1)} %bitcast.33), channel_id=1, source_target_pairs={{4,0},{5,1},{6,2},{7,3},{0,4},{1,5},{2,6},{3,7},{12,8},{13,9},{14,... | collective-permute-start | bytes 786440 | tf_op jit(solution)/shard_map/ppermute | solution.py:41
  143.1 8.6 %collective-permute-start.19 = (bf16[1024,128]{1,0:T(8,128)(2,1)S(1)}, bf16[1024,128]{1,0:T(8,128)(2,1)S(1)}, u32[]{:S(2)}, u32[]{:S(2)}) collective-permute-start(bf16[1024,128]{1,0:T(8,128)(2,1)S(1)} %bitcast.34), channel_id=1, source_target_pairs={{8,0},{9,1},{10,2},{11,3},{12,4},{13,5},{14,6},{15,7},{0,8},{1,9},... | collective-permute-start | bytes 786440 | tf_op jit(solution)/shard_map/ppermute | solution.py:41
  145.2 12.7 %collective-permute-start.20 = (bf16[1024,128]{1,0:T(8,128)(2,1)S(1)}, bf16[1024,128]{1,0:T(8,128)(2,1)S(1)}, u32[]{:S(2)}, u32[]{:S(2)}) collective-permute-start(bf16[1024,128]{1,0:T(8,128)(2,1)S(1)} %bitcast.35), channel_id=1, source_target_pairs={{2,0},{3,1},{4,2},{5,3},{6,4},{7,5},{0,6},{1,7},{10,8},{11,9},{12,... | collective-permute-start | bytes 786440 | tf_op jit(solution)/shard_map/ppermute | solution.py:41
  147.7 10.4 %collective-permute-start.21 = (bf16[1024,128]{1,0:T(8,128)(2,1)S(1)}, bf16[1024,128]{1,0:T(8,128)(2,1)S(1)}, u32[]{:S(2)}, u32[]{:S(2)}) collective-permute-start(bf16[1024,128]{1,0:T(8,128)(2,1)S(1)} %bitcast.36), channel_id=1, source_target_pairs={{6,0},{7,1},{0,2},{1,3},{2,4},{3,5},{4,6},{5,7},{14,8},{15,9},{8,1... | collective-permute-start | bytes 786440 | tf_op jit(solution)/shard_map/ppermute | solution.py:41
  151.7 8.9 %collective-permute-start.22 = (bf16[1024,128]{1,0:T(8,128)(2,1)S(1)}, bf16[1024,128]{1,0:T(8,128)(2,1)S(1)}, u32[]{:S(2)}, u32[]{:S(2)}) collective-permute-start(bf16[1024,128]{1,0:T(8,128)(2,1)S(1)} %collective-permute-done.19), channel_id=1, source_target_pairs={{2,0},{3,1},{4,2},{5,3},{6,4},{7,5},{0,6},{1,7},{10,8},{11,9},{12,... | collective-permute-start | bytes 786440 | tf_op jit(solution)/shard_map/ppermute | solution.py:41
  155.6 7.6 %collective-permute-start.23 = (bf16[1024,128]{1,0:T(8,128)(2,1)S(1)}, bf16[1024,128]{1,0:T(8,128)(2,1)S(1)}, u32[]{:S(2)}, u32[]{:S(2)}) collective-permute-start(bf16[1024,128]{1,0:T(8,128)(2,1)S(1)} %collective-permute-done.19), channel_id=1, source_target_pairs={{6,0},{7,1},{0,2},{1,3},{2,4},{3,5},{4,6},{5,7},{14,8},{15,9},{8,1... | collective-permute-start | bytes 786440 | tf_op jit(solution)/shard_map/ppermute | solution.py:41
  155.6 7.9 %collective-permute-start.24 = (bf16[1024,128]{1,0:T(8,128)(2,1)S(1)}, bf16[1024,128]{1,0:T(8,128)(2,1)S(1)}, u32[]{:S(2)}, u32[]{:S(2)}) collective-permute-start(bf16[1024,128]{1,0:T(8,128)(2,1)S(1)} %collective-permute-done.18), channel_id=1, source_target_pairs={{8,0},{9,1},{10,2},{11,3},{12,4},{13,5},{14,6},{15,7},{0,8},{1,9},... | collective-permute-start | bytes 786440 | tf_op jit(solution)/shard_map/ppermute | solution.py:41
  157.9 5.9 %collective-permute-start.25 = (bf16[4096,128]{1,0:T(8,128)(2,1)S(1)}, bf16[4096,128]{1,0:T(8,128)(2,1)S(1)}, u32[]{:S(2)}, u32[]{:S(2)}) collective-permute-start(bf16[4096,128]{1,0:T(8,128)(2,1)S(1)} %get-tuple-element.61), channel_id=1, source_target_pairs={{1,0},{0,1},{3,2},{2,3},{5,4},{4,5},{7,6},{6,7},{9,8},{8,9},{11,10... | collective-permute-start | bytes 3145736 | tf_op jit(solution)/shard_map/ppermute | solution.py:41
  (8 other events, 67.5 us)

commit v7 on v5

--- a/solution.py
+++ b/solution.py
@@ -224,7 +224,7 @@
 def coefficient_kernel(classes, own, cosine, sine, diagonals, couplings, loads, rounded, table):
     sectors = table.shape[1]
     coupling = couplings[...]
-    diagonal = [diagonals[classes[s]] for s in range(sectors)]
+    diagonal = [diagonals[classes[s, 0]] for s in range(sectors)]
     factors, reduced = reduce_coefficients([-coupling] * sectors, diagonal, [-coupling] * sectors)
     gains = [
         apply_reduction(
@@ -312,7 +312,7 @@
     def own_slice(cells, axis):
         return lax.dynamic_slice_in_dim(cells, sector_id * slice_rows, slice_rows, axis)
 
-    all_classes = swap(jnp.broadcast_to(sector_class[:, None], (sectors, 1))).reshape(-1)
+    all_classes = swap(jnp.broadcast_to(sector_class[:, None], (sectors, 1)))
     turns = (engine_order[0] * jnp.arange(sectors, dtype=jnp.int32)) % sectors
     angle = turns.astype(jnp.float32) * (2.0 * math.pi / sectors)
     cosine, sine = jnp.cos(angle), jnp.sin(angle)

time: 200 us -> 200 us (level)
  no operation moved by 1% of the time
where the time goes in v7:
time: 200 us; the launch traced here: 199 us
  blocking collectives  92 us (46%)
  starting transfers between devices  42 us (21%)
  waiting for transfers between devices  38.9 us (19%)
  Pallas kernels  16.9 us (8%)
  local copies, waits for them, and re-layouts  5.42 us (3%)
    all_to_all x6, blocking collectives, swap(): return lax.all_to_all(cells, 'sector', 0, 0, tiled=True)  92 us
    ppermute x27, waiting for transfers between devices, fetch(): return lax.ppermute(block, 'row', row_peers(*shift))  33.9 us
    ppermute x27, starting transfers between devices, fetch(): return lax.ppermute(block, 'row', row_peers(*shift))  32.1 us
    pallas_call x3, Pallas kernels, block_product(): pl.pallas_call(functools.partial(product_kernel, message, keep), out_shap...  10.8 us
    all_to_all x1, starting transfers between devices, swap(): return lax.all_to_all(cells, 'sector', 0, 0, tiled=True)  9.94 us
    all_to_all x1, waiting for transfers between devices, swap(): return lax.all_to_all(cells, 'sector', 0, 0, tiled=True)  5.03 us
  transfers between devices with their start and end apart: 28, of which 22 were waited for; matrix products, arithmetic and copies ran while one was open for 3% of the time, Pallas kernels for 1%

profile of v7, /device:TPU:2, one launch (start us, length us, event | category | flops | bytes accessed | tf_op | source)
XLA Modules:
  0.0 198.7 jit_solution(17184828842748080419)
XLA Ops:
  1.3 9.9 %all-to-all-start = ((s32[16,1,1]{2,1,0:T(1,128)}), s32[16,1,1]{2,1,0:T(1,128)S(1)}, u32[]{:S(2)}, u32[]{:S(2)}) async-start(s32[16,1,1]{2,1,0:T(1,128)} %broadcast_in_dim.48), calls=%async_computation | async-start | bytes 16384 | tf_op jit(solution)/shard_map/all_to_all | solution.py:310
  13.2 5.0 %all-to-all-done = s32[16,1,1]{2,1,0:T(1,128)S(1)} async-done(((s32[16,1,1]{2,1,0:T(1,128)}), s32[16,1,1]{2,1,0:T(1,128)S(1)}, u32[]{:S(2)}, u32[]{:S(2)}) %all-to-all-start) | async-done | bytes 96 | tf_op jit(solution)/shard_map/all_to_all | solution.py:310
  19.6 3.1 %collective-permute-start.2 = (bf16[1024,128]{1,0:T(8,128)(2,1)S(1)}, bf16[1024,128]{1,0:T(8,128)(2,1)S(1)}, u32[]{:S(2)}, u32[]{:S(2)}) collective-permute-start(bf16[1024,128]{1,0:T(8,128)(2,1)S(1)} %get-tuple-element.32), channel_id=1, source_target_pairs={{2,0},{3,1},{4,2},{5,3},{6,4},{7,5},{0,6},{1,7},{10,8},{11,9},{12,... | collective-permute-start | bytes 786440 | tf_op jit(solution)/shard_map/ppermute | solution.py:41
  28.1 3.1 %collective-permute-done = bf16[1024,128]{1,0:T(8,128)(2,1)S(1)} collective-permute-done((bf16[1024,128]{1,0:T(8,128)(2,1)S(1)}, bf16[1024,128]{1,0:T(8,128)(2,1)S(1)}, u32[]{:S(2)}, u32[]{:S(2)}) %collective-permute-start) | collective-permute-done | bytes 262176 | tf_op jit(solution)/shard_map/ppermute | solution.py:41
  38.1 3.7 %collective-permute-done.5 = bf16[1024,128]{1,0:T(8,128)(2,1)S(1)} collective-permute-done((bf16[1024,128]{1,0:T(8,128)(2,1)S(1)}, bf16[1024,128]{1,0:T(8,128)(2,1)S(1)}, u32[]{:S(2)}, u32[]{:S(2)}) %collective-permute-start.5) | collective-permute-done | bytes 262176 | tf_op jit(solution)/shard_map/ppermute | solution.py:41
  42.3 2.3 %collective-permute-done.8 = bf16[4096,128]{1,0:T(8,128)(2,1)S(1)} collective-permute-done((bf16[4096,128]{1,0:T(8,128)(2,1)S(1)}, bf16[4096,128]{1,0:T(8,128)(2,1)S(1)}, u32[]{:S(2)}, u32[]{:S(2)}) %collective-permute-start.8) | collective-permute-done | bytes 1048608 | tf_op jit(solution)/shard_map/ppermute | solution.py:41
  44.8 3.7 %shard_map.93 = f32[16,72,128]{2,1,0:T(8,128)S(1)} custom-call(s32[64]{0:T(128)S(1)} %reshape.72.columns, bf16[4,16,256,256]{3,2,1,0:T(8,128)(2,1)S(1)} %bitcast.29, bf16[16384,128]{1,0:T(8,128)(2,1)S(1)} %constant_dynamic-update-slice_fusion.gathered), custom_call_target="tpu_custom_call" | custom-call | flops 1073741824 | bytes 8388608 | tf_op jit(solution)/shard_map/pallas_call | solution.py:135
  48.5 16.4 %all_to_all.38 = f16[16,72,128]{2,1,0:T(8,128)(2,1)S(1)} all-to-all(f16[16,72,128]{2,1,0:T(8,128)(2,1)S(1)} %convert_element_type.38), channel_id=1, replica_groups=mesh['sector'=16,'row'=16] {'sector'}, dimensions={0} | all-to-all | bytes 589824 | tf_op jit(solution)/shard_map/all_to_all | solution.py:310
  66.1 14.2 %all_to_all.39 = bf16[16,64,128]{2,1,0:T(8,128)(2,1)S(1)} all-to-all(bf16[16,64,128]{2,1,0:T(8,128)(2,1)S(1)} %get-tuple-element.39), channel_id=1, replica_groups=mesh['sector'=16,'row'=16] {'sector'}, dimensions={0} | all-to-all | bytes 524288 | tf_op jit(solution)/shard_map/all_to_all | solution.py:310
  82.3 2.2 %collective-permute-start.10 = (bf16[1024,128]{1,0:T(8,128)(2,1)S(1)}, bf16[1024,128]{1,0:T(8,128)(2,1)S(1)}, u32[]{:S(2)}, u32[]{:S(2)}) collective-permute-start(bf16[1024,128]{1,0:T(8,128)(2,1)S(1)} %bitcast.41), channel_id=1, source_target_pairs={{4,0},{5,1},{6,2},{7,3},{0,4},{1,5},{2,6},{3,7},{12,8},{13,9},{14,... | collective-permute-start | bytes 786440 | tf_op jit(solution)/shard_map/ppermute | solution.py:41
  84.5 2.4 %collective-permute-start.11 = (bf16[1024,128]{1,0:T(8,128)(2,1)S(1)}, bf16[1024,128]{1,0:T(8,128)(2,1)S(1)}, u32[]{:S(2)}, u32[]{:S(2)}) collective-permute-start(bf16[1024,128]{1,0:T(8,128)(2,1)S(1)} %bitcast.42), channel_id=1, source_target_pairs={{2,0},{3,1},{4,2},{5,3},{6,4},{7,5},{0,6},{1,7},{10,8},{11,9},{12,... | collective-permute-start | bytes 786440 | tf_op jit(solution)/shard_map/ppermute | solution.py:41
  88.1 2.2 %collective-permute-start.13 = (bf16[1024,128]{1,0:T(8,128)(2,1)S(1)}, bf16[1024,128]{1,0:T(8,128)(2,1)S(1)}, u32[]{:S(2)}, u32[]{:S(2)}) collective-permute-start(bf16[1024,128]{1,0:T(8,128)(2,1)S(1)} %collective-permute-done.9), channel_id=1, source_target_pairs={{2,0},{3,1},{4,2},{5,3},{6,4},{7,5},{0,6},{1,7},{10,8},{11,9},{12,... | collective-permute-start | bytes 786440 | tf_op jit(solution)/shard_map/ppermute | solution.py:41
  90.4 2.7 %collective-permute-done.10 = bf16[1024,128]{1,0:T(8,128)(2,1)S(1)} collective-permute-done((bf16[1024,128]{1,0:T(8,128)(2,1)S(1)}, bf16[1024,128]{1,0:T(8,128)(2,1)S(1)}, u32[]{:S(2)}, u32[]{:S(2)}) %collective-permute-start.10) | collective-permute-done | bytes 262176 | tf_op jit(solution)/shard_map/ppermute | solution.py:41
  101.9 2.3 %collective-permute-done.17 = bf16[4096,128]{1,0:T(8,128)(2,1)S(1)} collective-permute-done((bf16[4096,128]{1,0:T(8,128)(2,1)S(1)}, bf16[4096,128]{1,0:T(8,128)(2,1)S(1)}, u32[]{:S(2)}, u32[]{:S(2)}) %collective-permute-start.17) | collective-permute-done | bytes 1048608 | tf_op jit(solution)/shard_map/ppermute | solution.py:41
  104.4 3.7 %shard_map.95 = (f32[16,72,128]{2,1,0:T(8,128)S(1)}, f32[1024,128]{1,0:T(8,128)S(1)}) custom-call(s32[64]{0:T(128)S(1)} %reshape.72.columns, bf16[4,16,256,256]{3,2,1,0:T(8,128)(2,1)S(1)} %bitcast.30, bf16[16384,128]{1,0:T(8,128)(2,1)S(1)} %constant_dynamic-update-slice_fusion.15.gathered), custom_call_target="tpu_custom_call" | custom-call | flops 1073741824 | bytes 8388608 | tf_op jit(solution)/shard_map/pallas_call | solution.py:135
  108.1 16.4 %all_to_all.40 = f16[16,72,128]{2,1,0:T(8,128)(2,1)S(1)} all-to-all(f16[16,72,128]{2,1,0:T(8,128)(2,1)S(1)} %convert_element_type.40), channel_id=1, replica_groups=mesh['sector'=16,'row'=16] {'sector'}, dimensions={0} | all-to-all | bytes 589824 | tf_op jit(solution)/shard_map/all_to_all | solution.py:310
  125.7 14.5 %all_to_all.41 = bf16[16,64,128]{2,1,0:T(8,128)(2,1)S(1)} all-to-all(bf16[16,64,128]{2,1,0:T(8,128)(2,1)S(1)} %get-tuple-element.45), channel_id=1, replica_groups=mesh['sector'=16,'row'=16] {'sector'}, dimensions={0} | all-to-all | bytes 524288 | tf_op jit(solution)/shard_map/all_to_all | solution.py:310
  141.2 2.5 %collective-permute-start.19 = (bf16[1024,128]{1,0:T(8,128)(2,1)S(1)}, bf16[1024,128]{1,0:T(8,128)(2,1)S(1)}, u32[]{:S(2)}, u32[]{:S(2)}) collective-permute-start(bf16[1024,128]{1,0:T(8,128)(2,1)S(1)} %bitcast.36), channel_id=1, source_target_pairs={{4,0},{5,1},{6,2},{7,3},{0,4},{1,5},{2,6},{3,7},{12,8},{13,9},{14,... | collective-permute-start | bytes 786440 | tf_op jit(solution)/shard_map/ppermute | solution.py:41
  145.7 2.3 %collective-permute-done.18 = bf16[1024,128]{1,0:T(8,128)(2,1)S(1)} collective-permute-done((bf16[1024,128]{1,0:T(8,128)(2,1)S(1)}, bf16[1024,128]{1,0:T(8,128)(2,1)S(1)}, u32[]{:S(2)}, u32[]{:S(2)}) %collective-permute-start.18) | collective-permute-done | bytes 262176 | tf_op jit(solution)/shard_map/ppermute | solution.py:41
  151.9 2.5 %collective-permute-start.24 = (bf16[1024,128]{1,0:T(8,128)(2,1)S(1)}, bf16[1024,128]{1,0:T(8,128)(2,1)S(1)}, u32[]{:S(2)}, u32[]{:S(2)}) collective-permute-start(bf16[1024,128]{1,0:T(8,128)(2,1)S(1)} %collective-permute-done.19), channel_id=1, source_target_pairs={{8,0},{9,1},{10,2},{11,3},{12,4},{13,5},{14,6},{15,7},{0,8},{1,9},... | collective-permute-start | bytes 786440 | tf_op jit(solution)/shard_map/ppermute | solution.py:41
  160.3 2.3 %collective-permute-done.26 = bf16[4096,128]{1,0:T(8,128)(2,1)S(1)} collective-permute-done((bf16[4096,128]{1,0:T(8,128)(2,1)S(1)}, bf16[4096,128]{1,0:T(8,128)(2,1)S(1)}, u32[]{:S(2)}, u32[]{:S(2)}) %collective-permute-start.26) | collective-permute-done | bytes 1048608 | tf_op jit(solution)/shard_map/ppermute | solution.py:41
  162.8 3.4 %shard_map.97 = bf16[1024,128]{1,0:T(8,128)(2,1)S(1)} custom-call(s32[64]{0:T(128)S(1)} %reshape.72.columns, bf16[4,16,256,256]{3,2,1,0:T(8,128)(2,1)S(1)} %bitcast.31, bf16[16384,128]{1,0:T(8,128)(2,1)S(1)} %constant_dynamic-update-slice_fusion.30.gathered, f32[1024,128]{1,0:T(8,128)S(1)} %get-tuple-element.50.refs_0_), custom_call_target="tpu_custom_call" | custom-call | flops 1073741824 | bytes 8388608 | tf_op jit(solution)/shard_map/pallas_call | solution.py:135
  166.2 16.1 %all_to_all.42.refs_1_ = bf16[16,64,128]{2,1,0:T(8,128)(2,1)S(1)} all-to-all(bf16[16,64,128]{2,1,0:T(8,128)(2,1)S(1)} %bitcast.32), channel_id=1, replica_groups=mesh['sector'=16,'row'=16] {'sector'}, dimensions={0} | all-to-all | bytes 524288 | tf_op jit(solution)/shard_map/all_to_all | solution.py:310
  183.5 14.4 %all_to_all.43 = bf16[16,64,128]{2,1,0:T(8,128)(2,1)S(1)} all-to-all(bf16[16,64,128]{2,1,0:T(8,128)(2,1)S(1)} %shard_map.98), channel_id=1, replica_groups=mesh['sector'=16,'row'=16] {'sector'}, dimensions={0} | all-to-all | bytes 524288 | tf_op jit(solution)/shard_map/all_to_all | solution.py:310
  (112 shorter events, 45.4 us)
Async XLA Ops:
  1.3 17.0 %all-to-all-start = ((s32[16,1,1]{2,1,0:T(1,128)}), s32[16,1,1]{2,1,0:T(1,128)S(1)}, u32[]{:S(2)}, u32[]{:S(2)}) async-start(s32[16,1,1]{2,1,0:T(1,128)} %broadcast_in_dim.48), calls=%async_computation | async-start | bytes 16384 | tf_op jit(solution)/shard_map/all_to_all | solution.py:310
  19.6 16.0 %collective-permute-start.2 = (bf16[1024,128]{1,0:T(8,128)(2,1)S(1)}, bf16[1024,128]{1,0:T(8,128)(2,1)S(1)}, u32[]{:S(2)}, u32[]{:S(2)}) collective-permute-start(bf16[1024,128]{1,0:T(8,128)(2,1)S(1)} %get-tuple-element.32), channel_id=1, source_target_pairs={{2,0},{3,1},{4,2},{5,3},{6,4},{7,5},{0,6},{1,7},{10,8},{11,9},{12,... | collective-permute-start | bytes 786440 | tf_op jit(solution)/shard_map/ppermute | solution.py:41
  22.7 10.7 %collective-permute-start.1 = (bf16[1024,128]{1,0:T(8,128)(2,1)S(1)}, bf16[1024,128]{1,0:T(8,128)(2,1)S(1)}, u32[]{:S(2)}, u32[]{:S(2)}) collective-permute-start(bf16[1024,128]{1,0:T(8,128)(2,1)S(1)} %get-tuple-element.32), channel_id=1, source_target_pairs={{4,0},{5,1},{6,2},{7,3},{0,4},{1,5},{2,6},{3,7},{12,8},{13,9},{14,... | collective-permute-start | bytes 786440 | tf_op jit(solution)/shard_map/ppermute | solution.py:41
  23.3 7.9 %collective-permute-start = (bf16[1024,128]{1,0:T(8,128)(2,1)S(1)}, bf16[1024,128]{1,0:T(8,128)(2,1)S(1)}, u32[]{:S(2)}, u32[]{:S(2)}) collective-permute-start(bf16[1024,128]{1,0:T(8,128)(2,1)S(1)} %get-tuple-element.32), channel_id=1, source_target_pairs={{8,0},{9,1},{10,2},{11,3},{12,4},{13,5},{14,6},{15,7},{0,8},{1,9},... | collective-permute-start | bytes 786440 | tf_op jit(solution)/shard_map/ppermute | solution.py:41
  26.2 11.7 %collective-permute-start.3 = (bf16[1024,128]{1,0:T(8,128)(2,1)S(1)}, bf16[1024,128]{1,0:T(8,128)(2,1)S(1)}, u32[]{:S(2)}, u32[]{:S(2)}) collective-permute-start(bf16[1024,128]{1,0:T(8,128)(2,1)S(1)} %get-tuple-element.32), channel_id=1, source_target_pairs={{6,0},{7,1},{0,2},{1,3},{2,4},{3,5},{4,6},{5,7},{14,8},{15,9},{8,1... | collective-permute-start | bytes 786440 | tf_op jit(solution)/shard_map/ppermute | solution.py:41
  31.2 6.9 %collective-permute-start.4 = (bf16[1024,128]{1,0:T(8,128)(2,1)S(1)}, bf16[1024,128]{1,0:T(8,128)(2,1)S(1)}, u32[]{:S(2)}, u32[]{:S(2)}) collective-permute-start(bf16[1024,128]{1,0:T(8,128)(2,1)S(1)} %collective-permute-done), channel_id=1, source_target_pairs={{2,0},{3,1},{4,2},{5,3},{6,4},{7,5},{0,6},{1,7},{10,8},{11,9},{12,... | collective-permute-start | bytes 786440 | tf_op jit(solution)/shard_map/ppermute | solution.py:41
  32.3 9.5 %collective-permute-start.5 = (bf16[1024,128]{1,0:T(8,128)(2,1)S(1)}, bf16[1024,128]{1,0:T(8,128)(2,1)S(1)}, u32[]{:S(2)}, u32[]{:S(2)}) collective-permute-start(bf16[1024,128]{1,0:T(8,128)(2,1)S(1)} %collective-permute-done), channel_id=1, source_target_pairs={{6,0},{7,1},{0,2},{1,3},{2,4},{3,5},{4,6},{5,7},{14,8},{15,9},{8,1... | collective-permute-start | bytes 786440 | tf_op jit(solution)/shard_map/ppermute | solution.py:41
  33.4 8.4 %collective-permute-start.6 = (bf16[1024,128]{1,0:T(8,128)(2,1)S(1)}, bf16[1024,128]{1,0:T(8,128)(2,1)S(1)}, u32[]{:S(2)}, u32[]{:S(2)}) collective-permute-start(bf16[1024,128]{1,0:T(8,128)(2,1)S(1)} %collective-permute-done.1), channel_id=1, source_target_pairs={{8,0},{9,1},{10,2},{11,3},{12,4},{13,5},{14,6},{15,7},{0,8},{1,9},... | collective-permute-start | bytes 786440 | tf_op jit(solution)/shard_map/ppermute | solution.py:41
  37.3 4.9 %collective-permute-start.7 = (bf16[4096,128]{1,0:T(8,128)(2,1)S(1)}, bf16[4096,128]{1,0:T(8,128)(2,1)S(1)}, u32[]{:S(2)}, u32[]{:S(2)}) collective-permute-start(bf16[4096,128]{1,0:T(8,128)(2,1)S(1)} %pad_maximum_fusion), channel_id=1, source_target_pairs={{1,0},{0,1},{3,2},{2,3},{5,4},{4,5},{7,6},{6,7},{9,8},{8,9},{11,10... | collective-permute-start | bytes 3145736 | tf_op jit(solution)/shard_map/ppermute | solution.py:41
  80.3 7.9 %collective-permute-start.9 = (bf16[1024,128]{1,0:T(8,128)(2,1)S(1)}, bf16[1024,128]{1,0:T(8,128)(2,1)S(1)}, u32[]{:S(2)}, u32[]{:S(2)}) collective-permute-start(bf16[1024,128]{1,0:T(8,128)(2,1)S(1)} %bitcast.40), channel_id=1, source_target_pairs={{8,0},{9,1},{10,2},{11,3},{12,4},{13,5},{14,6},{15,7},{0,8},{1,9},... | collective-permute-start | bytes 786440 | tf_op jit(solution)/shard_map/ppermute | solution.py:41
  82.3 10.8 %collective-permute-start.10 = (bf16[1024,128]{1,0:T(8,128)(2,1)S(1)}, bf16[1024,128]{1,0:T(8,128)(2,1)S(1)}, u32[]{:S(2)}, u32[]{:S(2)}) collective-permute-start(bf16[1024,128]{1,0:T(8,128)(2,1)S(1)} %bitcast.41), channel_id=1, source_target_pairs={{4,0},{5,1},{6,2},{7,3},{0,4},{1,5},{2,6},{3,7},{12,8},{13,9},{14,... | collective-permute-start | bytes 786440 | tf_op jit(solution)/shard_map/ppermute | solution.py:41
  84.5 12.2 %collective-permute-start.11 = (bf16[1024,128]{1,0:T(8,128)(2,1)S(1)}, bf16[1024,128]{1,0:T(8,128)(2,1)S(1)}, u32[]{:S(2)}, u32[]{:S(2)}) collective-permute-start(bf16[1024,128]{1,0:T(8,128)(2,1)S(1)} %bitcast.42), channel_id=1, source_target_pairs={{2,0},{3,1},{4,2},{5,3},{6,4},{7,5},{0,6},{1,7},{10,8},{11,9},{12,... | collective-permute-start | bytes 786440 | tf_op jit(solution)/shard_map/ppermute | solution.py:41
  86.9 11.1 %collective-permute-start.12 = (bf16[1024,128]{1,0:T(8,128)(2,1)S(1)}, bf16[1024,128]{1,0:T(8,128)(2,1)S(1)}, u32[]{:S(2)}, u32[]{:S(2)}) collective-permute-start(bf16[1024,128]{1,0:T(8,128)(2,1)S(1)} %bitcast.43), channel_id=1, source_target_pairs={{6,0},{7,1},{0,2},{1,3},{2,4},{3,5},{4,6},{5,7},{14,8},{15,9},{8,1... | collective-permute-start | bytes 786440 | tf_op jit(solution)/shard_map/ppermute | solution.py:41
  88.1 11.5 %collective-permute-start.13 = (bf16[1024,128]{1,0:T(8,128)(2,1)S(1)}, bf16[1024,128]{1,0:T(8,128)(2,1)S(1)}, u32[]{:S(2)}, u32[]{:S(2)}) collective-permute-start(bf16[1024,128]{1,0:T(8,128)(2,1)S(1)} %collective-permute-done.9), channel_id=1, source_target_pairs={{2,0},{3,1},{4,2},{5,3},{6,4},{7,5},{0,6},{1,7},{10,8},{11,9},{12,... | collective-permute-start | bytes 786440 | tf_op jit(solution)/shard_map/ppermute | solution.py:41
  90.4 11.0 %collective-permute-start.14 = (bf16[1024,128]{1,0:T(8,128)(2,1)S(1)}, bf16[1024,128]{1,0:T(8,128)(2,1)S(1)}, u32[]{:S(2)}, u32[]{:S(2)}) collective-permute-start(bf16[1024,128]{1,0:T(8,128)(2,1)S(1)} %collective-permute-done.9), channel_id=1, source_target_pairs={{6,0},{7,1},{0,2},{1,3},{2,4},{3,5},{4,6},{5,7},{14,8},{15,9},{8,1... | collective-permute-start | bytes 786440 | tf_op jit(solution)/shard_map/ppermute | solution.py:41
  93.1 8.3 %collective-permute-start.15 = (bf16[1024,128]{1,0:T(8,128)(2,1)S(1)}, bf16[1024,128]{1,0:T(8,128)(2,1)S(1)}, u32[]{:S(2)}, u32[]{:S(2)}) collective-permute-start(bf16[1024,128]{1,0:T(8,128)(2,1)S(1)} %collective-permute-done.10), channel_id=1, source_target_pairs={{8,0},{9,1},{10,2},{11,3},{12,4},{13,5},{14,6},{15,7},{0,8},{1,9},... | collective-permute-start | bytes 786440 | tf_op jit(solution)/shard_map/ppermute | solution.py:41
  96.9 4.9 %collective-permute-start.16 = (bf16[4096,128]{1,0:T(8,128)(2,1)S(1)}, bf16[4096,128]{1,0:T(8,128)(2,1)S(1)}, u32[]{:S(2)}, u32[]{:S(2)}) collective-permute-start(bf16[4096,128]{1,0:T(8,128)(2,1)S(1)} %get-tuple-element.43), channel_id=1, source_target_pairs={{1,0},{0,1},{3,2},{2,3},{5,4},{4,5},{7,6},{6,7},{9,8},{8,9},{11,10... | collective-permute-start | bytes 3145736 | tf_op jit(solution)/shard_map/ppermute | solution.py:41
  140.2 7.9 %collective-permute-start.18 = (bf16[1024,128]{1,0:T(8,128)(2,1)S(1)}, bf16[1024,128]{1,0:T(8,128)(2,1)S(1)}, u32[]{:S(2)}, u32[]{:S(2)}) collective-permute-start(bf16[1024,128]{1,0:T(8,128)(2,1)S(1)} %bitcast.35), channel_id=1, source_target_pairs={{8,0},{9,1},{10,2},{11,3},{12,4},{13,5},{14,6},{15,7},{0,8},{1,9},... | collective-permute-start | bytes 786440 | tf_op jit(solution)/shard_map/ppermute | solution.py:41
  141.2 10.7 %collective-permute-start.19 = (bf16[1024,128]{1,0:T(8,128)(2,1)S(1)}, bf16[1024,128]{1,0:T(8,128)(2,1)S(1)}, u32[]{:S(2)}, u32[]{:S(2)}) collective-permute-start(bf16[1024,128]{1,0:T(8,128)(2,1)S(1)} %bitcast.36), channel_id=1, source_target_pairs={{4,0},{5,1},{6,2},{7,3},{0,4},{1,5},{2,6},{3,7},{12,8},{13,9},{14,... | collective-permute-start | bytes 786440 | tf_op jit(solution)/shard_map/ppermute | solution.py:41
  143.6 12.0 %collective-permute-start.20 = (bf16[1024,128]{1,0:T(8,128)(2,1)S(1)}, bf16[1024,128]{1,0:T(8,128)(2,1)S(1)}, u32[]{:S(2)}, u32[]{:S(2)}) collective-permute-start(bf16[1024,128]{1,0:T(8,128)(2,1)S(1)} %bitcast.37), channel_id=1, source_target_pairs={{2,0},{3,1},{4,2},{5,3},{6,4},{7,5},{0,6},{1,7},{10,8},{11,9},{12,... | collective-permute-start | bytes 786440 | tf_op jit(solution)/shard_map/ppermute | solution.py:41
  144.8 11.6 %collective-permute-start.21 = (bf16[1024,128]{1,0:T(8,128)(2,1)S(1)}, bf16[1024,128]{1,0:T(8,128)(2,1)S(1)}, u32[]{:S(2)}, u32[]{:S(2)}) collective-permute-start(bf16[1024,128]{1,0:T(8,128)(2,1)S(1)} %bitcast.38), channel_id=1, source_target_pairs={{6,0},{7,1},{0,2},{1,3},{2,4},{3,5},{4,6},{5,7},{14,8},{15,9},{8,1... | collective-permute-start | bytes 786440 | tf_op jit(solution)/shard_map/ppermute | solution.py:41
  148.1 10.3 %collective-permute-start.22 = (bf16[1024,128]{1,0:T(8,128)(2,1)S(1)}, bf16[1024,128]{1,0:T(8,128)(2,1)S(1)}, u32[]{:S(2)}, u32[]{:S(2)}) collective-permute-start(bf16[1024,128]{1,0:T(8,128)(2,1)S(1)} %collective-permute-done.18), channel_id=1, source_target_pairs={{2,0},{3,1},{4,2},{5,3},{6,4},{7,5},{0,6},{1,7},{10,8},{11,9},{12,... | collective-permute-start | bytes 786440 | tf_op jit(solution)/shard_map/ppermute | solution.py:41
  149.6 10.1 %collective-permute-start.23 = (bf16[1024,128]{1,0:T(8,128)(2,1)S(1)}, bf16[1024,128]{1,0:T(8,128)(2,1)S(1)}, u32[]{:S(2)}, u32[]{:S(2)}) collective-permute-start(bf16[1024,128]{1,0:T(8,128)(2,1)S(1)} %collective-permute-done.18), channel_id=1, source_target_pairs={{6,0},{7,1},{0,2},{1,3},{2,4},{3,5},{4,6},{5,7},{14,8},{15,9},{8,1... | collective-permute-start | bytes 786440 | tf_op jit(solution)/shard_map/ppermute | solution.py:41
  151.9 7.9 %collective-permute-start.24 = (bf16[1024,128]{1,0:T(8,128)(2,1)S(1)}, bf16[1024,128]{1,0:T(8,128)(2,1)S(1)}, u32[]{:S(2)}, u32[]{:S(2)}) collective-permute-start(bf16[1024,128]{1,0:T(8,128)(2,1)S(1)} %collective-permute-done.19), channel_id=1, source_target_pairs={{8,0},{9,1},{10,2},{11,3},{12,4},{13,5},{14,6},{15,7},{0,8},{1,9},... | collective-permute-start | bytes 786440 | tf_op jit(solution)/shard_map/ppermute | solution.py:41
  (8 other events, 66.3 us)
